TPU v7x, 32 devices: a whole 2x2x4 slice. The times are simulated.
32 devices in a mesh: groups: 2 (over x), row: 8 (over z, y), col: 2 (over core).
Axes of the slice: x: 2, y: 2, z: 4, core: 2. Of those that a mesh axis runs over, the one named last changes fastest.
Arguments:
- canvas: bfloat16 [512, 64, 512], P(('groups', 'row'), 'col'), parts along dimension 0, may hold values from -50 to 50
- keep_mask: int32 [512, 64], P(('groups', 'row'), 'col'), parts along dimension 0, may hold values from 0 to 1, as said below
- w_qkv: bfloat16 [512, 1536], replicated, may hold values from -0.25 to 0.25
- w_spread: bfloat16 [5, 5, 1536], replicated, may hold values from -1.25 to 1.25
- w_group: bfloat16 [48, 32, 32], replicated, may hold values from -1 to 1
- w_proj: bfloat16 [1024, 512], replicated, may hold values from -0.1875 to 0.1875
- gain_attn: float32 [512], replicated, may hold values from 0.1 to 1.9
- w_expand: bfloat16 [512, 4096], replicated, may hold values from -0.25 to 0.25
- w_spatial: bfloat16 [3, 3, 4096], replicated, may hold values from -2 to 2
- w_reduce: bfloat16 [2048, 512], replicated, may hold values from -0.125 to 0.125
- gain_ff: float32 [512], replicated, may hold values from 0.1 to 1.9
Outputs:
- decoded: bfloat16 [512, 64, 512], P(('groups', 'row'), 'col'), parts along dimension 0
There are 2 independent parts, one for each index of `groups`. A program takes and returns all parts, laid end to end along the dimension named above; an argument that names none is the same for every part. Nothing has to cross between parts.
Inputs may be any that keep to these rules, and one draw needn't show every extreme that they name: `keep_mask`: one bit per cell.
All inputs are finite; a program needn't handle non-finite values.
Results may differ from a plain program's by a relative error of at most 0.008.
Values may be sent and summed in bfloat16 or wider, within the bound.
No kernel may reach another device: no remote copies, remote signals or barrier semaphores. Data moves between devices by JAX's collectives and lax.ppermute only.
A program may use at most 128 MiB of HBM per device.

v0:
```python
import jax
import jax.numpy as jnp
from jax import lax
from jax.sharding import PartitionSpec as P


def with_halo(cells, sides, width):
    for axis, dim in sides:
        count = lax.axis_size(axis)
        ends = count - 1
        head = lax.slice_in_dim(cells, 0, width, axis=dim)
        tail = lax.slice_in_dim(cells, cells.shape[dim] - width, cells.shape[dim], axis=dim)
        cells = jnp.concatenate(
            [
                lax.ppermute(tail, axis, [(i, (i + 1) % count) for i in range(ends)]),
                cells,
                lax.ppermute(head, axis, [((i + 1) % count, i) for i in range(ends)]),
            ],
            axis=dim,
        )
    return cells


def depthwise(padded, weight, tile_rows, tile_cols, kernel_span):
    summed = jnp.zeros((tile_rows, tile_cols, padded.shape[2]), jnp.float32)
    for shift_row in range(kernel_span):
        for shift_col in range(kernel_span):
            window = padded[shift_row : shift_row + tile_rows, shift_col : shift_col + tile_cols]
            summed = summed + window.astype(jnp.float32) * weight[shift_row, shift_col].astype(
                jnp.float32
            )
    return summed


def rms_scale(branch, gain):
    return branch * lax.rsqrt(jnp.mean(branch * branch, axis=-1, keepdims=True) + 1e-05) * gain


def pointwise(features, weight):
    shape_in = features.shape
    result = jnp.dot(features.reshape(-1, shape_in[2]), weight, preferred_element_type=jnp.float32)
    return result.reshape(shape_in[0], shape_in[1], weight.shape[1])


def body(
    canvas,
    keep_mask,
    w_qkv,
    w_spread,
    w_group,
    w_proj,
    gain_attn,
    w_expand,
    w_spatial,
    w_reduce,
    gain_ff,
):
    tile_rows, tile_cols, channels = canvas.shape
    cell_count = tile_rows * tile_cols
    heads = w_group.shape[0] // 3
    head_size = w_group.shape[1]
    hidden_units = w_reduce.shape[0]
    projected = pointwise(canvas, w_qkv).astype(jnp.bfloat16)
    padded = with_halo(projected, (("row", 0), ("col", 1)), 2)
    spread = depthwise(padded, w_spread, tile_rows, tile_cols, 5).astype(jnp.bfloat16)
    grouped = spread.reshape(cell_count, 3 * heads, head_size)
    aggregated = jnp.einsum(
        "cgi,gio->cgo", grouped, w_group, preferred_element_type=jnp.float32
    ).astype(jnp.bfloat16)
    both = jnp.concatenate(
        [
            projected.reshape(cell_count, 3, heads, head_size),
            aggregated.reshape(cell_count, 3, heads, head_size),
        ],
        axis=2,
    )
    queries, keys_raw, value_rows = (both[:, 0], both[:, 1], both[:, 2])
    keep = keep_mask.reshape(cell_count).astype(jnp.bfloat16)
    key_feats = jax.nn.relu(keys_raw) * keep[:, None, None]
    local_kv = jnp.einsum("chi,chj->hij", key_feats, value_rows, preferred_element_type=jnp.float32)
    local_ksum = jnp.sum(key_feats.astype(jnp.float32), axis=0)
    kv_stats, key_sums = lax.psum((local_kv, local_ksum), ("row", "col"))
    query_feats = jax.nn.relu(queries).astype(jnp.float32)
    numerator = jnp.einsum("chi,hij->chj", query_feats, kv_stats, precision=lax.Precision.HIGHEST)
    denominator = (
        jnp.einsum("chi,hi->ch", query_feats, key_sums, precision=lax.Precision.HIGHEST) + 1.0
    )
    attended = (
        (numerator / denominator[:, :, None]).astype(jnp.bfloat16).reshape(cell_count, 2 * channels)
    )
    branch = jnp.dot(attended, w_proj, preferred_element_type=jnp.float32)
    flat = canvas.reshape(cell_count, channels)
    midway = (flat.astype(jnp.float32) + rms_scale(branch, gain_attn)).astype(jnp.bfloat16)
    midway_tile = midway.reshape(tile_rows, tile_cols, channels)
    expanded = jax.nn.silu(pointwise(midway_tile, w_expand)).astype(jnp.bfloat16)
    padded_hidden = with_halo(expanded, (("row", 0), ("col", 1)), 1)
    conv = depthwise(padded_hidden, w_spatial, tile_rows, tile_cols, 3)
    gated = (conv[..., :hidden_units] * jax.nn.silu(conv[..., hidden_units:])).astype(jnp.bfloat16)
    reduced = jnp.dot(
        gated.reshape(cell_count, hidden_units), w_reduce, preferred_element_type=jnp.float32
    )
    decoded = (midway.astype(jnp.float32) + rms_scale(reduced, gain_ff)).astype(jnp.bfloat16)
    return decoded.reshape(tile_rows, tile_cols, channels)


def solution(mesh):
    return jax.shard_map(
        body,
        mesh=mesh,
        in_specs=(
            P(("groups", "row"), "col", None),
            P(("groups", "row"), "col"),
            P(),
            P(),
            P(),
            P(),
            P(),
            P(),
            P(),
            P(),
            P(),
        ),
        out_specs=P(("groups", "row"), "col", None),
        check_vma=False,
    )
```

profile of v0, /device:TPU:0, one launch (start us, length us, event | category | flops | bytes accessed | tf_op | source)
XLA Modules:
  0.0 372.6 jit_solution(5897505733610228699)
XLA Ops:
  6.5 3.7 convolution_convert_fusion
  10.2 1.7 copy-done.2
  11.9 4.9 %collective-permute-start = (bf16[2,32,1536]{2,1,0:T(8,128)(2,1)S(1)}, bf16[2,32,1536]{2,1,0:T(8,128)(2,1)S(1)}, u32[]{:S(2)}, u32[]{:S(2)}) collective-permute-start(bf16[2,32,1536]{2,1,0:T(8,128)(2,1)S(1)} %get-tuple-element.42), channel_id=1, source_target_pairs={{0,2},{2,4},{4,6},{6,8},{8,10},{10,12},{12,14},{1,3},{3,5},{5,7},{... | collective-permute-start | bytes 589832 | tf_op jit(solution)/shard_map/ppermute | solution.py:15
  18.3 14.6 %reshape.58 = bf16[1024,3,16,32]{3,2,1,0:T(8,128)(2,1)} reshape(bf16[32,32,1536]{2,1,0:T(8,128)(2,1)} %copy-done.2) | data formatting | bytes 6291456 | tf_op jit(solution)/shard_map/reshape | solution.py:72
  33.7 13.4 %copy.26 = bf16[1024,3,16,32]{0,3,2,1:T(8,128)(2,1)} copy(bf16[1024,3,16,32]{3,2,1,0:T(8,128)(2,1)} %reshape.58) | data formatting | bytes 6291456 | tf_op jit(solution)/shard_map/reshape | solution.py:72
  47.1 1.9 pad_maximum_fusion.12
  53.9 2.7 maximum_maximum_fusion.1
  56.6 24.0 %add_convert_fusion = bf16[32,32,1536]{2,1,0:T(8,128)(2,1)} fusion(bf16[32,32,1536]{2,1,0:T(8,128)(2,1)S(1)} %copy-done.3, bf16[2,32,1536]{2,1,0:T(8,128)(2,1)S(1)} %collective-permute-done.1, bf16[2,32,1536]{2,1,0:T(8,128)(2,1)S(1)} %collective-permute-done, bf16[36,34,1536]{2,1,0:T(8,128)(2,1)S(1)} %get-tuple-element.39, ...), kind=kLoop, calls=%fused_computation.14 | loop fusion | flops 124256256 | bytes 69752832 | tf_op jit(solution)/shard_map/convert_element_type | solution.py:65
  80.6 14.6 %reshape.59 = bf16[1024,48,32]{2,1,0:T(8,128)(2,1)} reshape(bf16[32,32,1536]{2,1,0:T(8,128)(2,1)} %add_convert_fusion) | data formatting | bytes 6291456 | tf_op jit(solution)/shard_map/reshape | solution.py:66
  95.1 13.5 %fusion.6 = bf16[48,1024,32]{1,2,0:T(8,128)(2,1)} fusion(bf16[48,32,32]{1,2,0:T(8,128)(2,1)S(1)} %copy.25, bf16[1024,48,32]{2,1,0:T(8,128)(2,1)} %reshape.59), kind=kOutput, calls=%fused_computation.29 | convolution fusion | flops 102236160 | bytes 6389760 | tf_op jit(solution)/shard_map/cgi,gio->cgo/dot_general | solution.py:67
  108.6 3.0 fusion.18
  113.8 63.0 %psum.15 = f32[32,32]{1,0:T(8,128)S(1)} all-reduce(f32[32,32]{1,0:T(8,128)S(1)} %get-tuple-element.30), channel_id=1, replica_groups=mesh['groups'=2,'row'=8,'col'=2] {'row','col'}, use_global_device_ids=true, to_apply=%region_2.3 | all-reduce | flops 1024 | bytes 8192 | tf_op jit(solution)/shard_map/psum | solution.py:82
  176.8 2.5 fusion.26
  179.4 85.6 %all-reduce.2.cloned.1.call-done = f32[32,32,32]{2,1,0:T(8,128)} async-done(((f32[32,32,32]{2,1,0:T(8,128)}), f32[32,32,32]{2,1,0:T(8,128)}) %all-reduce.2.cloned.1.call-update) | async-done | bytes 131088 | tf_op jit(solution)/shard_map/psum | solution.py:82
  265.0 3.7 fusion.3
  271.2 4.5 %fusion.27 = f32[1024,4096]{1,0:T(8,128)S(1)} fusion(bf16[1024,512]{1,0:T(8,128)(2,1)S(1)} %fusion.19, bf16[512,4096]{1,0:T(8,128)(2,1)S(1)} %copy-done.13), kind=kOutput, calls=%fused_computation.94 | convolution fusion | flops 4294967296 | bytes 22020096 | tf_op jit(solution)/shard_map/dot_general | solution.py:41
  275.8 4.5 %multiply_convert_fusion = bf16[32,32,4096]{2,1,0:T(8,128)(2,1)S(1)} fusion(f32[32,32,4096]{2,1,0:T(8,128)S(1)} %bitcast.61), kind=kLoop, calls=%fused_computation.1 | loop fusion | flops 20971520 | bytes 25165824 | tf_op jit(solution)/shard_map/convert_element_type | solution.py:95
  280.4 2.6 collective-permute-start.4
  284.3 10.4 %collective-permute-done.4 = bf16[1,32,4096]{2,1,0:T(8,128)(2,1)S(1)} collective-permute-done((bf16[1,32,4096]{2,1,0:T(8,128)(2,1)S(1)}, bf16[1,32,4096]{2,1,0:T(8,128)(2,1)S(1)}, u32[]{:S(2)}, u32[]{:S(2)}) %collective-permute-start.4) | collective-permute-done | bytes 262176 | tf_op jit(solution)/shard_map/ppermute | solution.py:15
  298.0 3.1 collective-permute-start.6
  302.9 14.7 %maximum_maximum_fusion = (bf16[34,33,4096]{2,1,0:T(8,128)(2,1)}, bf16[34,33,4096]{2,1,0:T(8,128)(2,1)}) fusion(bf16[1,32,4096]{2,1,0:T(8,128)(2,1)S(1)} %collective-permute-done.5, bf16[32,32,4096]{2,1,0:T(8,128)(2,1)S(1)} %multiply_convert_fusion, bf16[1,32,4096]{2,1,0:T(8,128)(2,1)S(1)} %collective-permute-done.4, bf16[34,1,4096]{2,1,0:T(2,128)(2,1)S(1)} %copy.29, ...), kind=kLoop, calls=%fused_computation.4 | loop fusion | flops 73531392 | bytes 27852800 | tf_op jit(solution)/shard_map/concatenate | solution.py:13
  317.6 36.8 %multiply_add_fusion = f32[32,32,4096]{2,1,0:T(8,128)} fusion(bf16[32,32,4096]{2,1,0:T(8,128)(2,1)} %copy-done.1, bf16[34,33,4096]{2,1,0:T(8,128)(2,1)} %get-tuple-element.33, bf16[1,32,4096]{2,1,0:T(8,128)(2,1)S(1)} %collective-permute-done.5, bf16[34,33,4096]{2,1,0:T(8,128)(2,1)} %get-tuple-element.32, bf16[1,32,4096]{2,1,0:T(8,128)(2,1)S(1)} %collective-permute-done.4, ...), kind=kLoop, calls=%fused_computation | loop fusion | flops 117440512 | bytes 76169216 | tf_op jit(solution)/shard_map/add | solution.py:29
  354.4 7.1 %fusion.2 = bf16[32,32,2048]{2,1,0:T(8,128)(2,1)S(1)} fusion(f32[32,32,4096]{2,1,0:T(8,128)} %multiply_add_fusion), kind=kLoop, calls=%fused_computation.7 | loop fusion | flops 12582912 | bytes 20971520 | tf_op jit(solution)/shard_map/convert_element_type | solution.py:98
  361.5 2.4 multiply_reduce_fusion
  (64 shorter events, 19.5 us)
Async XLA Ops:
  6.5 355.0 %copy-start = (bf16[2048,512]{1,0:T(8,128)(2,1)S(1)}, bf16[2048,512]{1,0:T(8,128)(2,1)}, u32[]{:S(2)}) copy-start(bf16[2048,512]{1,0:T(8,128)(2,1)} %param.20) | copy-start | bytes 6291460
  6.5 258.4 %all-reduce.2.cloned.1.call-start = ((), (), s32[]{:S(2)}) async-start(), calls=%async_computation | async-start | bytes 1048576 | tf_op jit(solution)/shard_map/psum | solution.py:82
  10.2 1.7 copy-start.2
  11.9 35.2 %collective-permute-start = (bf16[2,32,1536]{2,1,0:T(8,128)(2,1)S(1)}, bf16[2,32,1536]{2,1,0:T(8,128)(2,1)S(1)}, u32[]{:S(2)}, u32[]{:S(2)}) collective-permute-start(bf16[2,32,1536]{2,1,0:T(8,128)(2,1)S(1)} %get-tuple-element.42), channel_id=1, source_target_pairs={{0,2},{2,4},{4,6},{6,8},{8,10},{10,12},{12,14},{1,3},{3,5},{5,7},{... | collective-permute-start | bytes 589832 | tf_op jit(solution)/shard_map/ppermute | solution.py:15
  16.8 16.0 %copy-start.10 = (s32[32,32]{1,0:T(8,128)S(1)}, s32[32,32]{1,0:T(8,128)}, u32[]{:S(2)}) copy-start(s32[32,32]{1,0:T(8,128)} %param.12) | copy-start | bytes 12292
  16.8 16.1 %copy-start.7 = (bf16[48,32,32]{0,2,1:T(8,128)(2,1)S(1)}, bf16[48,32,32]{0,2,1:T(8,128)(2,1)}, u32[]{:S(2)}) copy-start(bf16[48,32,32]{0,2,1:T(8,128)(2,1)} %param.15) | copy-start | bytes 294916
  16.8 30.3 %collective-permute-start.1 = (bf16[2,32,1536]{2,1,0:T(8,128)(2,1)S(1)}, bf16[2,32,1536]{2,1,0:T(8,128)(2,1)S(1)}, u32[]{:S(2)}, u32[]{:S(2)}) collective-permute-start(bf16[2,32,1536]{2,1,0:T(8,128)(2,1)S(1)} %get-tuple-element.43), channel_id=1, source_target_pairs={{2,0},{4,2},{6,4},{8,6},{10,8},{12,10},{14,12},{3,1},{5,3},{7,5},{... | collective-permute-start | bytes 589832 | tf_op jit(solution)/shard_map/ppermute | solution.py:17
  33.7 18.1 %copy-start.9 = (bf16[5,5,1536]{2,1,0:T(8,128)(2,1)S(1)}, bf16[5,5,1536]{2,1,0:T(8,128)(2,1)}, u32[]{:S(2)}) copy-start(bf16[5,5,1536]{2,1,0:T(8,128)(2,1)} %param.14) | copy-start | bytes 230404
  47.1 6.7 %copy-start.3 = (bf16[32,32,1536]{2,1,0:T(8,128)(2,1)S(1)}, bf16[32,32,1536]{2,1,0:T(8,128)(2,1)}, u32[]{:S(2)}) copy-start(bf16[32,32,1536]{2,1,0:T(8,128)(2,1)} %copy-done.2) | copy-start | bytes 9437188
  49.0 3.2 collective-permute-start.2
  50.5 3.4 collective-permute-start.3
  95.1 13.5 %copy-start.4 = (bf16[1024,3,16,32]{0,3,2,1:T(8,128)(2,1)S(1)}, bf16[1024,3,16,32]{0,3,2,1:T(8,128)(2,1)}, u32[]{:S(2)}) copy-start(bf16[1024,3,16,32]{0,3,2,1:T(8,128)(2,1)} %copy.26) | copy-start | bytes 9437188
  108.6 3.0 copy-start.5
  179.4 89.3 %copy-start.14 = (bf16[1024,512]{1,0:T(8,128)(2,1)S(1)}, bf16[1024,512]{1,0:T(8,128)(2,1)}, u32[]{:S(2)}) copy-start(bf16[1024,512]{1,0:T(8,128)(2,1)} %param.16) | copy-start | bytes 3145732
  268.7 1.4 copy-start.6
  268.7 1.4 copy-start.11
  268.7 2.5 copy-start.13
  280.3 22.6 %copy-start.1 = (bf16[32,32,4096]{2,1,0:T(8,128)(2,1)}, bf16[32,32,4096]{2,1,0:T(8,128)(2,1)S(1)}, u32[]{:S(2)}) copy-start(bf16[32,32,4096]{2,1,0:T(8,128)(2,1)S(1)} %multiply_convert_fusion) | copy-start | bytes 25165828
  280.3 20.8 %copy-start.8 = (bf16[3,3,4096]{2,1,0:T(4,128)(2,1)S(1)}, bf16[3,3,4096]{2,1,0:T(4,128)(2,1)}, u32[]{:S(2)}) copy-start(bf16[3,3,4096]{2,1,0:T(4,128)(2,1)} %param.19) | copy-start | bytes 221188
  280.4 14.3 %collective-permute-start.4 = (bf16[1,32,4096]{2,1,0:T(8,128)(2,1)S(1)}, bf16[1,32,4096]{2,1,0:T(8,128)(2,1)S(1)}, u32[]{:S(2)}, u32[]{:S(2)}) collective-permute-start(bf16[1,32,4096]{2,1,0:T(8,128)(2,1)S(1)} %get-tuple-element.36), channel_id=1, source_target_pairs={{0,2},{2,4},{4,6},{6,8},{8,10},{10,12},{12,14},{1,3},{3,5},{5,7},{... | collective-permute-start | bytes 786440 | tf_op jit(solution)/shard_map/ppermute | solution.py:15
  283.0 11.7 %collective-permute-start.5 = (bf16[1,32,4096]{2,1,0:T(8,128)(2,1)S(1)}, bf16[1,32,4096]{2,1,0:T(8,128)(2,1)S(1)}, u32[]{:S(2)}, u32[]{:S(2)}) collective-permute-start(bf16[1,32,4096]{2,1,0:T(8,128)(2,1)S(1)} %get-tuple-element.37), channel_id=1, source_target_pairs={{2,0},{4,2},{6,4},{8,6},{10,8},{12,10},{14,12},{3,1},{5,3},{7,5},{... | collective-permute-start | bytes 786440 | tf_op jit(solution)/shard_map/ppermute | solution.py:17
  296.7 4.5 %collective-permute-start.7 = (bf16[34,1,4096]{2,0,1:T(8,128)(2,1)S(1)}, bf16[34,1,4096]{2,0,1:T(8,128)(2,1)S(1)}, u32[]{:S(2)}, u32[]{:S(2)}) collective-permute-start(bf16[34,1,4096]{2,0,1:T(8,128)(2,1)S(1)} %copy.30), channel_id=1, source_target_pairs={{1,0},{3,2},{5,4},{7,6},{9,8},{11,10},{13,12},{15,14},{17,16},{19,... | collective-permute-start | bytes 835592 | tf_op jit(solution)/shard_map/ppermute | solution.py:17
  298.0 4.3 %collective-permute-start.6 = (bf16[34,1,4096]{2,0,1:T(8,128)(2,1)S(1)}, bf16[34,1,4096]{2,0,1:T(8,128)(2,1)S(1)}, u32[]{:S(2)}, u32[]{:S(2)}) collective-permute-start(bf16[34,1,4096]{2,0,1:T(8,128)(2,1)S(1)} %copy.28), channel_id=1, source_target_pairs={{0,1},{2,3},{4,5},{6,7},{8,9},{10,11},{12,13},{14,15},{16,17},{18,... | collective-permute-start | bytes 835592 | tf_op jit(solution)/shard_map/ppermute | solution.py:15
  361.5 2.4 copy-start.12
Sparse Core Ops, SparseCore 0:
  176.9 87.9 all-reduce.1
where the time goes:
time: 378 us; the launch traced here: 373 us
  other arithmetic  99 us (26%)
  waiting for transfers between devices  98.1 us (26%)
  blocking collectives  63 us (17%)
  local copies, waits for them, and re-layouts  47.6 us (13%)
  matrix products  33.2 us (9%)
  starting transfers between devices  17.4 us (5%)
  between operations  14.2 us (4%)
    psum x1, waiting for transfers between devices, body(): kv_stats, key_sums = lax.psum((local_kv, local_ksum), ('row', 'col'))  85.6 us
    psum x1, blocking collectives, body(): kv_stats, key_sums = lax.psum((local_kv, local_ksum), ('row', 'col'))  63 us
    add x1, other arithmetic, depthwise(): summed + window.astype(jnp.float32) * weight[shift_row, shift_col].astype...  36.8 us
    reshape x2, local copies, waits for them, and re-layouts, body(): projected.reshape(cell_count, 3, heads, head_size)  28 us
    convert_element_type x1, other arithmetic, body(): depthwise(padded, w_spread, tile_rows, tile_cols, 5).astype(jnp.bfloat16)  24 us
    concatenate x2, other arithmetic, with_halo(): jnp.concatenate([lax.ppermute(tail, axis, [(i, (i + 1) % count) for i in...  17.4 us
    reshape x1, local copies, waits for them, and re-layouts, body(): grouped = spread.reshape(cell_count, 3 * heads, head_size)  14.6 us
    dot_general x1, matrix products, body(): jnp.einsum('cgi,gio->cgo', grouped, w_group, preferred_element_type=jnp.f...  13.5 us
  transfers between devices with their start and end apart: 9, of which 4 were waited for; matrix products, arithmetic and copies ran while one was open for 9% of the time, Pallas kernels for 0%

commit v1 on v0

v1 whole, which is shorter than its diff:
```python
import functools

import jax
import jax.numpy as jnp
from jax import lax
from jax.experimental import pallas as pl
from jax.experimental.pallas import tpu as pltpu
from jax.sharding import PartitionSpec as P

LANES = 128
BLOCK = 256
PAD = 8
VMEM_BYTES = 60 * 1024 * 1024
BF16 = jnp.bfloat16
F32 = jnp.float32


def depthwise_rows(load, taps, span, out_rows, emit):
    sums = {}
    for row_in in range(out_rows + span - 1):
        views = [load(row_in, b) for b in range(span)]
        for a in range(span):
            row_out = row_in - a
            if not 0 <= row_out < out_rows:
                continue
            part = views[0] * taps[a * span]
            for b in range(1, span):
                part = part + views[b] * taps[a * span + b]
            sums[row_out] = part if a == 0 else sums[row_out] + part
            if a == span - 1:
                emit(row_out, sums.pop(row_out))


def tap_list(weight_ref, lanes, rows):
    count = weight_ref.shape[0]
    return [
        jnp.broadcast_to(weight_ref[t : t + 1, lanes], (rows, LANES)).astype(BF16)
        for t in range(count)
    ]


def head_mask(size, head):
    return (
        lax.broadcasted_iota(jnp.int32, (size, size), 0) // head
        == lax.broadcasted_iota(jnp.int32, (size, size), 1) // head
    )


def spread_blocks(rows, head):
    size = rows.shape[0]
    pick = (
        lax.broadcasted_iota(jnp.int32, (head, size), 1) % head
        == lax.broadcasted_iota(jnp.int32, (head, size), 0)
    ).astype(BF16)
    wide = jnp.dot(rows, pick, preferred_element_type=F32)
    return jnp.where(head_mask(size, head), wide, 0.0).astype(BF16)


def project(dims, main_ref, rows_ref, cols_ref, w_ref, place, on_main):
    tile_rows, tile_cols, reach, tall = dims
    stride = tile_cols + PAD
    w = w_ref[...]
    group = 4
    for first in range(0, tile_rows, group):
        p = jnp.dot(
            main_ref[first * tile_cols : (first + group) * tile_cols],
            w,
            preferred_element_type=F32,
        )
        for k in range(group):
            place(first + k, p[k * tile_cols : (k + 1) * tile_cols])
        on_main(first * tile_cols, p)
    p = jnp.dot(rows_ref[...], w, preferred_element_type=F32)
    for k in range(reach):
        place(k - reach, p[k * tile_cols : (k + 1) * tile_cols])
        low = (reach + k) * tile_cols
        place(tile_rows + k, p[low : low + tile_cols])
    p = jnp.dot(cols_ref[...], w, preferred_element_type=F32)
    for side in range(2):
        for k in range(reach):
            col = k - reach if side == 0 else tile_cols + k
            low = (side * reach + k) * tall
            place((PAD + col, tall, stride), p[low : low + tall])


def placer(buf, reach, stride):
    def place(where, values):
        for ch in range(values.shape[1] // LANES):
            part = values[:, ch * LANES : (ch + 1) * LANES]
            if isinstance(where, tuple):
                start, count, step = where
                buf[ch, pl.ds(start, count, stride=step), :] = part
            else:
                start = PAD + (where + reach) * stride
                buf[ch, pl.ds(start, part.shape[0]), :] = part

    return place


def key_value_kernel(
    dims,
    head,
    main_ref,
    rows_ref,
    cols_ref,
    keep_ref,
    wk_ref,
    wv_ref,
    sk_ref,
    sv_ref,
    gk_ref,
    gv_ref,
    stats_ref,
    buf_k,
    buf_v,
    mat_k,
    mat_v,
    agg_k,
    agg_v,
):
    tile_rows, tile_cols, reach, tall = dims
    stride = tile_cols + PAD

    def keep_keys(start, p):
        rows = p.shape[0]
        keep = keep_ref[start : start + rows]
        for ch in range(BLOCK // LANES):
            lanes = slice(ch * LANES, (ch + 1) * LANES)
            mat_k[start : start + rows, lanes] = (
                jnp.maximum(p[:, lanes].astype(BF16), 0) * keep
            )

    def keep_values(start, p):
        mat_v[start : start + p.shape[0]] = p.astype(BF16)

    project(dims, main_ref, rows_ref, cols_ref, wk_ref, placer(buf_k, reach, stride), keep_keys)
    project(dims, main_ref, rows_ref, cols_ref, wv_ref, placer(buf_v, reach, stride), keep_values)

    def summarise(scale, keys, values):
        kv = lax.dot_general(
            keys[...], values[...], (((0,), (0,)), ((), ())), preferred_element_type=F32
        )
        lane_head = lax.broadcasted_iota(jnp.int32, (head, BLOCK), 1) // head
        packed = jnp.zeros((head, BLOCK), F32)
        for h in range(BLOCK // head):
            packed = packed + jnp.where(lane_head == h, kv[h * head : (h + 1) * head], 0.0)
        stats_ref[scale, 0:head, :] = packed
        total = jnp.sum(keys[...].astype(F32), axis=0, keepdims=True)
        stats_ref[scale, head : head + 8, :] = jnp.broadcast_to(total, (8, BLOCK))

    summarise(0, mat_k, mat_v)

    for buf, sp_ref, out in ((buf_k, sk_ref, mat_k), (buf_v, sv_ref, mat_v)):
        for ch in range(BLOCK // LANES):
            lanes = slice(ch * LANES, (ch + 1) * LANES)
            taps = tap_list(sp_ref, lanes, tile_cols)

            def load(row_in, b, buf=buf, ch=ch):
                start = PAD + (row_in + 1) * stride + b - 2
                return buf[ch, pl.ds(start, tile_cols), :].astype(BF16)

            def emit(row, value, out=out, lanes=lanes):
                out[row * tile_cols : (row + 1) * tile_cols, lanes] = value

            depthwise_rows(load, taps, 5, tile_rows, emit)

    for spread, g_ref, out, is_key in (
        (mat_k, gk_ref, agg_k, True),
        (mat_v, gv_ref, agg_v, False),
    ):
        blocks = spread_blocks(g_ref[...], head)
        cells = spread.shape[0]
        step = 256
        for start in range(0, cells, step):
            agg = jnp.dot(
                spread[start : start + step], blocks, preferred_element_type=F32
            ).astype(BF16)
            if is_key:
                keep = keep_ref[start : start + step]
                agg = jnp.maximum(agg, 0)
                for ch in range(BLOCK // LANES):
                    lanes = slice(ch * LANES, (ch + 1) * LANES)
                    out[start : start + step, lanes] = agg[:, lanes] * keep
            else:
                out[start : start + step] = agg
    summarise(1, agg_k, agg_v)


def query_kernel(
    dims, head, main_ref, rows_ref, cols_ref, wq_ref, sq_ref, gq_ref, q_ref, buf, spread
):
    tile_rows, tile_cols, reach, tall = dims
    stride = tile_cols + PAD
    cells = tile_rows * tile_cols
    project(
        dims,
        main_ref,
        rows_ref,
        cols_ref,
        wq_ref,
        placer(buf, reach, stride),
        lambda start, p: None,
    )

    def slot(row):
        if row < 0:
            return cells
        if row >= tile_rows:
            return cells + tile_cols
        return row * tile_cols

    side0 = cells + 2 * tile_cols
    for ch in range(BLOCK // LANES):
        lanes = slice(ch * LANES, (ch + 1) * LANES)
        for row in range(-1, tile_rows + 1):
            start = PAD + (row + reach) * stride
            value = buf[ch, pl.ds(start, tile_cols), :].astype(BF16)
            q_ref[0, 0, slot(row) : slot(row) + tile_cols, lanes] = jnp.maximum(value, 0)
        for side, col in enumerate((-1, tile_cols)):
            value = buf[ch, pl.ds(PAD + 2 * stride + col, tall, stride=stride), :].astype(BF16)
            low = side0 + side * tall
            q_ref[0, 0, low : low + tall, lanes] = jnp.maximum(value, 0)

        taps = tap_list(sq_ref, lanes, tile_cols)

        def load(row_in, b, ch=ch):
            start = PAD + row_in * stride + b - 2
            return buf[ch, pl.ds(start, tile_cols), :].astype(BF16)

        def emit(row, value, lanes=lanes):
            low = slot(row - 1)
            spread[low : low + tile_cols, lanes] = value

        depthwise_rows(load, taps, 5, tile_rows + 2, emit)
        taps = tap_list(sq_ref, lanes, tall)
        for side, col in enumerate((-1, tile_cols)):
            total = None
            for a in range(5):
                part = None
                for b in range(5):
                    start = PAD + a * stride + col + b - 2
                    view = buf[ch, pl.ds(start, tall, stride=stride), :].astype(BF16)
                    term = view * taps[a * 5 + b]
                    part = term if part is None else part + term
                total = part if total is None else total + part
            low = side0 + side * tall
            spread[low : low + tall, lanes] = total

    blocks = spread_blocks(gq_ref[...], head)
    count = spread.shape[0]
    for start in range(0, count, 256):
        stop = min(count, start + 256)
        agg = jnp.dot(spread[start:stop], blocks, preferred_element_type=F32)
        q_ref[1, 0, start:stop] = jnp.maximum(agg.astype(BF16), 0)


def rms_add(residual, branch, gain):
    scale = lax.rsqrt(jnp.mean(branch * branch, axis=-1, keepdims=True) + 1e-05)
    return residual.astype(F32) + branch * scale * gain


def feed_kernel(
    dims,
    head,
    flags_ref,
    main_ref,
    edge_ref,
    q_ref,
    stats_ref,
    wp_ref,
    gain_a_ref,
    wev_ref,
    weg_ref,
    spv_ref,
    spg_ref,
    wr_ref,
    gain_f_ref,
    out_ref,
    mid,
    att,
    buf_v,
    buf_g,
    gated,
):
    tile_rows, tile_cols, reach, tall = dims
    stride = tile_cols + PAD
    cells = tile_rows * tile_cols
    step_index = pl.program_id(0)
    scales, heads_blocks = q_ref.shape[0], q_ref.shape[1]

    @pl.when(step_index == 0)
    def _():
        same = head_mask(BLOCK, head)
        eye = lax.broadcasted_iota(jnp.int32, (BLOCK, BLOCK), 0) == lax.broadcasted_iota(
            jnp.int32, (BLOCK, BLOCK), 1
        )
        count = mid.shape[0]
        bounds = [(s, s + 256) for s in range(0, cells, 256)] + [(cells, count)]
        for scale in range(scales):
            for blk in range(heads_blocks):
                lanes = slice(blk * BLOCK, (blk + 1) * BLOCK)
                packed = stats_ref[scale, 0:head, lanes]
                kv = jnp.where(same, jnp.concatenate([packed] * (BLOCK // head), axis=0), 0.0)
                sums = stats_ref[scale, head : head + 1, lanes]
                diag = jnp.where(eye, jnp.broadcast_to(sums, (BLOCK, BLOCK)), 0.0)
                ks = jnp.dot(
                    diag.astype(BF16), same.astype(BF16), preferred_element_type=F32
                ).astype(BF16)
                kv = kv.astype(BF16)
                low = (scale * heads_blocks + blk) * BLOCK
                for start, stop in bounds:
                    q = q_ref[scale, blk, start:stop]
                    num = jnp.dot(q, kv, preferred_element_type=F32)
                    den = jnp.dot(q, ks, preferred_element_type=F32)
                    att[start:stop, low : low + BLOCK] = (num / (den + 1.0)).astype(BF16)
        gain = gain_a_ref[...]
        for start, stop in bounds:
            branch = jnp.dot(att[start:stop], wp_ref[...], preferred_element_type=F32)
            if start < cells:
                mid[start:stop] = rms_add(main_ref[start:stop], branch, gain).astype(BF16)
            else:
                value = rms_add(edge_ref[...], branch, gain)
                index = lax.broadcasted_iota(jnp.int32, (stop - start, 1), 0)
                side = index - 2 * tile_cols
                place = lax.rem(side + tall, tall)
                in_rows = index < 2 * tile_cols
                is_top = (index < tile_cols) | (~in_rows & (place == 0))
                is_bottom = (in_rows & (index >= tile_cols)) | (
                    ~in_rows & (place == tile_rows + 1)
                )
                is_left = ~in_rows & (side < tall)
                is_right = ~in_rows & (side >= tall)
                dead = (
                    (is_top & (flags_ref[0] == 0))
                    | (is_bottom & (flags_ref[1] == 0))
                    | (is_left & (flags_ref[2] == 0))
                    | (is_right & (flags_ref[3] == 0))
                )
                mid[start:stop] = jnp.where(dead, 0.0, value).astype(BF16)

    def silu(x):
        half = 0.5 * x
        return half * jnp.tanh(half) + half

    for w_ref, buf in ((wev_ref, buf_v), (weg_ref, buf_g)):
        w = w_ref[...]
        place = placer(buf, 1, stride)
        group = 4
        for first in range(0, tile_rows, group):
            p = silu(
                jnp.dot(
                    mid[first * tile_cols : (first + group) * tile_cols],
                    w,
                    preferred_element_type=F32,
                )
            )
            for k in range(group):
                place(first + k, p[k * tile_cols : (k + 1) * tile_cols])
        p = silu(jnp.dot(mid[cells:], w, preferred_element_type=F32))
        place(-1, p[:tile_cols])
        place(tile_rows, p[tile_cols : 2 * tile_cols])
        for side, col in enumerate((-1, tile_cols)):
            low = 2 * tile_cols + side * tall
            place((PAD + col, tall, stride), p[low : low + tall])

    base = step_index * BLOCK
    for ch in range(BLOCK // LANES):
        lanes = slice(ch * LANES, (ch + 1) * LANES)
        halves = []
        for buf, sp_ref in ((buf_v, spv_ref), (buf_g, spg_ref)):
            rows = []

            def load(row_in, b, buf=buf):
                start = PAD + row_in * stride + b - 1
                return buf[ch, pl.ds(start, tile_cols), :].astype(BF16)

            halves.append((load, tap_list(sp_ref, lanes, tile_cols)))

        pending = {}

        def finish(row, gate):
            value = pending.pop(row).astype(F32)
            result = value * silu(gate.astype(F32))
            col0 = pl.multiple_of(base + ch * LANES, LANES)
            gated[row * tile_cols : (row + 1) * tile_cols, pl.ds(col0, LANES)] = result.astype(
                BF16
            )

        depthwise_pair(halves, 3, tile_rows, pending, finish)

    @pl.when(step_index == pl.num_programs(0) - 1)
    def _():
        gain = gain_f_ref[...]
        for start in range(0, cells, 256):
            reduced = jnp.dot(
                gated[start : start + 256], wr_ref[...], preferred_element_type=F32
            )
            out_ref[start : start + 256] = rms_add(
                mid[start : start + 256], reduced, gain
            ).astype(BF16)


def depthwise_pair(halves, span, out_rows, pending, finish):
    sums = ({}, {})
    for row_in in range(out_rows + span - 1):
        for side, (load, taps) in enumerate(halves):
            views = [load(row_in, b) for b in range(span)]
            for a in range(span):
                row_out = row_in - a
                if not 0 <= row_out < out_rows:
                    continue
                part = views[0] * taps[a * span]
                for b in range(1, span):
                    part = part + views[b] * taps[a * span + b]
                sums[side][row_out] = part if a == 0 else sums[side][row_out] + part
                if a == span - 1:
                    if side == 0:
                        pending[row_out] = sums[0].pop(row_out)
                    else:
                        finish(row_out, sums[1].pop(row_out))


def neighbours(axis):
    count = lax.axis_size(axis)
    forward = [(i, i + 1) for i in range(count - 1)]
    return forward, [(b, a) for a, b in forward]


def total_over(x, axes):
    for axis in axes:
        count = lax.axis_size(axis)
        if count & (count - 1):
            x = lax.psum(x, axis)
            continue
        step = 1
        while step < count:
            x = x + lax.ppermute(x, axis, [(i, i ^ step) for i in range(count)])
            step *= 2
    return x


def body(
    canvas,
    keep_mask,
    w_qkv,
    w_spread,
    w_group,
    w_proj,
    gain_attn,
    w_expand,
    w_spatial,
    w_reduce,
    gain_ff,
):
    tile_rows, tile_cols, channels = canvas.shape
    cells = tile_rows * tile_cols
    head = w_group.shape[1]
    hidden = w_reduce.shape[0]
    blocks = channels // BLOCK
    reach = 3
    tall = tile_rows + PAD
    stride = tile_cols + PAD
    dims = (tile_rows, tile_cols, reach, tall)
    flat_rows = -(-(PAD + (tall + 4) * stride) // 8) * 8
    flat_rows_ff = PAD + tall * stride

    down, up = neighbours("row")
    above = lax.ppermute(canvas[tile_rows - reach :], "row", down)
    below = lax.ppermute(canvas[:reach], "row", up)

    def strip(low):
        return jnp.concatenate(
            [
                above[:, low : low + reach],
                canvas[:, low : low + reach],
                below[:, low : low + reach],
                jnp.zeros((tall - tile_rows - 2 * reach, reach, channels), canvas.dtype),
            ],
            axis=0,
        ).transpose(1, 0, 2)

    col_index = lax.axis_index("col")
    col_count = lax.axis_size("col")
    row_index = lax.axis_index("row")
    row_count = lax.axis_size("row")
    first, last = strip(0), strip(tile_cols - reach)
    if col_count == 2:
        got = lax.ppermute(jnp.where(col_index == 0, last, first), "col", [(0, 1), (1, 0)])
        left = jnp.where(col_index == 1, got, 0)
        right = jnp.where(col_index == 0, got, 0)
    else:
        right_way, left_way = neighbours("col")
        left = lax.ppermute(last, "col", right_way)
        right = lax.ppermute(first, "col", left_way)

    main = canvas.reshape(cells, channels)
    rows_in = jnp.concatenate([above, below], axis=0).reshape(2 * reach * tile_cols, channels)
    cols_in = jnp.concatenate([left, right], axis=0).reshape(2 * reach * tall, channels)
    filler = jnp.zeros((reach - 1, channels), canvas.dtype)
    edge = jnp.concatenate(
        [
            above[reach - 1],
            below[0],
            left[reach - 1, reach - 1 :],
            filler,
            right[0, reach - 1 :],
            filler,
        ],
        axis=0,
    )
    keep = jnp.broadcast_to(keep_mask.reshape(cells, 1).astype(BF16), (cells, LANES))
    flags = jnp.stack(
        [
            (row_index > 0),
            (row_index < row_count - 1),
            (col_index > 0),
            (col_index < col_count - 1),
        ]
    ).astype(jnp.int32)
    spread_w = w_spread.reshape(25, 3 * channels).astype(F32)
    group_w = w_group.reshape(3 * channels, head)
    spatial_w = w_spatial.reshape(9, 2 * hidden).astype(F32)

    def whole(shape):
        return pl.BlockSpec(shape, lambda *_: (0,) * len(shape))

    params = pltpu.CompilerParams(
        dimension_semantics=("arbitrary",), vmem_limit_bytes=VMEM_BYTES
    )

    stats = pl.pallas_call(
        functools.partial(key_value_kernel, dims, head),
        grid=(blocks,),
        in_specs=[
            whole(main.shape),
            whole(rows_in.shape),
            whole(cols_in.shape),
            whole(keep.shape),
            pl.BlockSpec((channels, BLOCK), lambda j: (0, blocks + j)),
            pl.BlockSpec((channels, BLOCK), lambda j: (0, 2 * blocks + j)),
            pl.BlockSpec((25, BLOCK), lambda j: (0, blocks + j)),
            pl.BlockSpec((25, BLOCK), lambda j: (0, 2 * blocks + j)),
            pl.BlockSpec((BLOCK, head), lambda j: (blocks + j, 0)),
            pl.BlockSpec((BLOCK, head), lambda j: (2 * blocks + j, 0)),
        ],
        out_specs=pl.BlockSpec((2, head + 8, BLOCK), lambda j: (0, 0, j)),
        out_shape=jax.ShapeDtypeStruct((2, head + 8, channels), F32),
        scratch_shapes=[
            pltpu.VMEM((BLOCK // LANES, flat_rows, LANES), F32),
            pltpu.VMEM((BLOCK // LANES, flat_rows, LANES), F32),
            pltpu.VMEM((cells, BLOCK), BF16),
            pltpu.VMEM((cells, BLOCK), BF16),
            pltpu.VMEM((cells, BLOCK), BF16),
            pltpu.VMEM((cells, BLOCK), BF16),
        ],
        compiler_params=params,
        cost_estimate=pl.CostEstimate(
            flops=2 * cells * channels * 2 * channels,
            bytes_accessed=4 * cells * channels,
            transcendentals=0,
        ),
        name="key_value",
    )(main, rows_in, cols_in, keep, w_qkv, w_qkv, spread_w, spread_w, group_w, group_w)
    stats = total_over(stats, ("col", "row"))

    count = cells + 2 * tile_cols + 2 * tall
    queries = pl.pallas_call(
        functools.partial(query_kernel, dims, head),
        grid=(blocks,),
        in_specs=[
            whole(main.shape),
            whole(rows_in.shape),
            whole(cols_in.shape),
            pl.BlockSpec((channels, BLOCK), lambda j: (0, j)),
            pl.BlockSpec((25, BLOCK), lambda j: (0, j)),
            pl.BlockSpec((BLOCK, head), lambda j: (j, 0)),
        ],
        out_specs=pl.BlockSpec((2, 1, count, BLOCK), lambda j: (0, j, 0, 0)),
        out_shape=jax.ShapeDtypeStruct((2, blocks, count, BLOCK), BF16),
        scratch_shapes=[
            pltpu.VMEM((BLOCK // LANES, flat_rows, LANES), F32),
            pltpu.VMEM((count, BLOCK), BF16),
        ],
        compiler_params=params,
        cost_estimate=pl.CostEstimate(
            flops=2 * cells * channels * channels,
            bytes_accessed=6 * cells * channels,
            transcendentals=0,
        ),
        name="query",
    )(main, rows_in, cols_in, w_qkv, spread_w, group_w)

    steps = hidden // BLOCK
    decoded = pl.pallas_call(
        functools.partial(feed_kernel, dims, head),
        grid=(steps,),
        in_specs=[
            pl.BlockSpec(memory_space=pltpu.SMEM),
            whole(main.shape),
            whole(edge.shape),
            whole(queries.shape),
            whole(stats.shape),
            whole(w_proj.shape),
            whole((1, channels)),
            pl.BlockSpec((channels, BLOCK), lambda j: (0, j)),
            pl.BlockSpec((channels, BLOCK), lambda j: (0, steps + j)),
            pl.BlockSpec((9, BLOCK), lambda j: (0, j)),
            pl.BlockSpec((9, BLOCK), lambda j: (0, steps + j)),
            whole(w_reduce.shape),
            whole((1, channels)),
        ],
        out_specs=whole(main.shape),
        out_shape=jax.ShapeDtypeStruct(main.shape, BF16),
        scratch_shapes=[
            pltpu.VMEM((count, channels), BF16),
            pltpu.VMEM((count, 2 * channels), BF16),
            pltpu.VMEM((BLOCK // LANES, flat_rows_ff, LANES), F32),
            pltpu.VMEM((BLOCK // LANES, flat_rows_ff, LANES), F32),
            pltpu.VMEM((cells, hidden), BF16),
        ],
        compiler_params=params,
        name="feed",
    )(
        flags,
        main,
        edge,
        queries,
        stats,
        w_proj,
        gain_attn.reshape(1, channels),
        w_expand,
        w_expand,
        spatial_w,
        spatial_w,
        w_reduce,
        gain_ff.reshape(1, channels),
    )
    return decoded.reshape(tile_rows, tile_cols, channels)


def solution(mesh):
    tile = P(("groups", "row"), "col", None)
    return jax.shard_map(
        body,
        mesh=mesh,
        in_specs=(tile, P(("groups", "row"), "col")) + (P(),) * 9,
        out_specs=tile,
        check_vma=False,
    )
```

time: 378 us -> 86.8 us (0.23); the launches traced: 373 us -> 86.4 us
  other arithmetic: 99 us -> 4.08 us
  waiting for transfers between devices: 98.1 us -> 13 us
  blocking collectives: 63 us -> 0 us
  Pallas kernels: 0 us -> 43.5 us
  local copies, waits for them, and re-layouts: 47.6 us -> 12.3 us
  matrix products: 33.2 us -> 0 us
  between operations: 14.2 us -> 0.16 us
  starting transfers between devices: 17.4 us -> 13.5 us
    psum x1 -> x0, waiting for transfers between devices: 85.6 us -> none  [body(): kv_stats, key_sums = lax.psum((local_kv, local_ksum), ('row', 'col'))]
    psum x1 -> x0, blocking collectives: 63 us -> none  [body(): kv_stats, key_sums = lax.psum((local_kv, local_ksum), ('row', 'col'))]
    pallas_call x0 -> x3, Pallas kernels: none -> 43.5 us  [the longest x1 26.2 us: body(): pl.pallas_call(functools.partial(feed_kernel, dims, head), grid=(steps,),...]
    reshape x3 -> x0, local copies, waits for them, and re-layouts: 42.6 us -> none  [the longest x2 28 us: body(): projected.reshape(cell_count, 3, heads, head_size)]
    convert_element_type x6 -> x2, other arithmetic: 37.4 us -> 1.38 us  [the longest x1 0.72 us: body(): keep_mask.reshape(cells, 1).astype(BF16)]
    add x2 -> x4, other arithmetic: 36.8 us -> 1.68 us  [total_over(): x = x + lax.ppermute(x, axis, [(i, i ^ step) for i in range(count)])]
    dot_general x8 -> x0, matrix products: 33.2 us -> none  [the longest x1 13.5 us: body(): jnp.einsum('cgi,gio->cgo', grouped, w_group, preferred_element_type=jnp.f...]
    concatenate x2, other arithmetic: 17.4 us -> 0.88 us  [the longest x1 0.75 us: body(): jnp.concatenate([left, right], axis=0).reshape(2 * reach * tall, channels)]
  transfers between devices with their start and end apart: 9 -> 7, of which waited for: 4 -> 4; matrix products, arithmetic and copies ran while one was open for 9% -> 14% of each run, Pallas kernels for 0% -> 8%
where the time goes in v1:
time: 86.8 us; the launch traced here: 86.4 us
  Pallas kernels  43.5 us (50%)
  starting transfers between devices  13.5 us (16%)
  waiting for transfers between devices  13 us (15%)
  local copies, waits for them, and re-layouts  12.3 us (14%)
  other arithmetic  4.08 us (5%)
    pallas_call x1, Pallas kernels, body(): pl.pallas_call(functools.partial(feed_kernel, dims, head), grid=(steps,),...  26.2 us
    pallas_call x1, Pallas kernels, body(): pl.pallas_call(functools.partial(key_value_kernel, dims, head), grid=(blo...  10.1 us
    ppermute x4, waiting for transfers between devices, total_over(): x = x + lax.ppermute(x, axis, [(i, i ^ step) for i in range(count)])  8.71 us
    pallas_call x1, Pallas kernels, body(): pl.pallas_call(functools.partial(query_kernel, dims, head), grid=(blocks,...  7.22 us
    ppermute x4, starting transfers between devices, total_over(): x = x + lax.ppermute(x, axis, [(i, i ^ step) for i in range(count)])  7.19 us
    concatenate x1, local copies, waits for them, and re-layouts, body(): jnp.concatenate([above[reach - 1], below[0], left[reach - 1, reach - 1:],...  5.07 us
    ppermute x1, starting transfers between devices, body(): above = lax.ppermute(canvas[tile_rows - reach:], 'row', down)  4.91 us
    ppermute x1, waiting for transfers between devices, body(): below = lax.ppermute(canvas[:reach], 'row', up)  4.21 us
  transfers between devices with their start and end apart: 7, of which 4 were waited for; matrix products, arithmetic and copies ran while one was open for 14% of the time, Pallas kernels for 8%

profile of v1, /device:TPU:0, one launch (start us, length us, event | category | flops | bytes accessed | tf_op | source)
XLA Modules:
  0.0 86.4 jit_solution(17073037752355096599)
XLA Ops:
  0.0 1.0 %fusion.2 = (bf16[3,32,512]{2,1,0:T(8,128)(2,1)S(1)}, bf16[3,32,512]{2,1,0:T(8,128)(2,1)S(1)}) fusion(bf16[32,32,512]{2,1,0:T(8,128)(2,1)} %param.11), kind=kLoop, calls=%fused_computation.12 | loop fusion | bytes 393216 | tf_op jit(solution)/shard_map/slice | solution.py:469
  1.1 4.9 %collective-permute-start = (bf16[3,32,512]{2,0,1:T(4,128)(2,1)S(1)}, bf16[3,32,512]{2,0,1:T(4,128)(2,1)S(1)}, u32[]{:S(2)}, u32[]{:S(2)}) collective-permute-start(bf16[3,32,512]{2,0,1:T(4,128)(2,1)S(1)} %copy.25), channel_id=1, source_target_pairs={{0,2},{2,4},{4,6},{6,8},{8,10},{10,12},{12,14},{1,3},{3,5},{5,7},{... | collective-permute-start | bytes 294920 | tf_op jit(solution)/shard_map/ppermute | solution.py:468
  6.1 1.3 %collective-permute-start.1 = (bf16[3,32,512]{2,0,1:T(4,128)(2,1)S(1)}, bf16[3,32,512]{2,0,1:T(4,128)(2,1)S(1)}, u32[]{:S(2)}, u32[]{:S(2)}) collective-permute-start(bf16[3,32,512]{2,0,1:T(4,128)(2,1)S(1)} %copy.26), channel_id=1, source_target_pairs={{2,0},{4,2},{6,4},{8,6},{10,8},{12,10},{14,12},{3,1},{5,3},{7,5},{... | collective-permute-start | bytes 294920 | tf_op jit(solution)/shard_map/ppermute | solution.py:469
  7.4 1.1 %fusion.1 = (bf16[32,3,512]{2,1,0:T(4,128)(2,1)S(1)}, bf16[32,3,512]{2,1,0:T(4,128)(2,1)S(1)}) fusion(bf16[32,32,512]{2,1,0:T(8,128)(2,1)} %param.11), kind=kLoop, calls=%fused_computation.11 | loop fusion | bytes 393216 | tf_op jit(solution)/shard_map/slice | solution.py:475
  8.8 4.2 %collective-permute-done.1 = bf16[3,32,512]{2,0,1:T(4,128)(2,1)S(1)} collective-permute-done((bf16[3,32,512]{2,0,1:T(4,128)(2,1)S(1)}, bf16[3,32,512]{2,0,1:T(4,128)(2,1)S(1)}, u32[]{:S(2)}, u32[]{:S(2)}) %collective-permute-start.1) | collective-permute-done | bytes 98336 | tf_op jit(solution)/shard_map/ppermute | solution.py:469
  13.2 0.7 convert_element_type.30
  14.0 0.7 reshape.43.sq_ref.sk_ref.sv_ref
  14.7 1.3 %copy.22 = bf16[48,32,32]{2,1,0:T(8,128)(2,1)} copy(bf16[48,32,32]{0,2,1:T(8,128)(2,1)S(1)} %copy-done) | data formatting | bytes 196608 | tf_op args[4]
  16.2 0.8 copy.21
  17.0 0.7 pad_maximum_fusion.1
  17.7 0.9 %broadcast_in_dim.15.keep_ref = bf16[1024,128]{1,0:T(8,128)(2,1)} broadcast(bf16[1024]{0:T(1024)(128)(2,1)S(1)} %convert_element_type.31), dimensions={0} | broadcast | bytes 264192 | tf_op jit(solution)/shard_map/broadcast_in_dim | solution.py:511
  18.6 10.1 %key_value.1 = f32[2,40,512]{2,1,0:T(8,128)} custom-call(bf16[1024,512]{1,0:T(8,128)(2,1)} %bitcast.23, bf16[192,512]{1,0:T(8,128)(2,1)} %bitcast.31, bf16[240,512]{1,0:T(8,128)(2,1)} %bitcast.29, bf16[1024,128]{1,0:T(8,128)(2,1)} %broadcast_in_dim.15.keep_ref, bf16[512,1536]{1,0:T(8,128)(2,1)} %wv_ref.1, bf16[512,1536]{1,0:T(8,128)(2,1)} %wv_ref.1, ...), custom_call_target="tpu_custom_call" | custom-call | flops 1073741824 | bytes 2097152 | tf_op jit(solution)/shard_map/key_value/pallas_call | solution.py:531
  29.2 1.2 %collective-permute-done.3 = f32[2,40,512]{2,1,0:T(8,128)S(1)} collective-permute-done((f32[2,40,512]{2,1,0:T(8,128)}, f32[2,40,512]{2,1,0:T(8,128)S(1)}, u32[]{:S(2)}, u32[]{:S(2)}) %collective-permute-start.3) | collective-permute-done | bytes 163872 | tf_op jit(solution)/shard_map/ppermute | solution.py:437
  30.4 0.9 %add.12 = f32[2,40,512]{2,1,0:T(8,128)S(1)} add(f32[2,40,512]{2,1,0:T(8,128)} %key_value.1, f32[2,40,512]{2,1,0:T(8,128)S(1)} %collective-permute-done.3) | non-fusion elementwise | flops 40960 | bytes 491520 | tf_op jit(solution)/shard_map/add | solution.py:437
  31.4 2.5 %collective-permute-start.4 = (f32[2,40,512]{2,1,0:T(8,128)S(1)}, f32[2,40,512]{2,1,0:T(8,128)S(1)}, u32[]{:S(2)}, u32[]{:S(2)}) collective-permute-start(f32[2,40,512]{2,1,0:T(8,128)S(1)} %add.12), channel_id=1, source_target_pairs={{0,2},{2,0},{4,6},{6,4},{8,10},{10,8},{12,14},{14,12},{1,3},{3,1},... | collective-permute-start | bytes 491528 | tf_op jit(solution)/shard_map/ppermute | solution.py:437
  33.9 4.7 %collective-permute-done.4 = f32[2,40,512]{2,1,0:T(8,128)S(1)} collective-permute-done((f32[2,40,512]{2,1,0:T(8,128)S(1)}, f32[2,40,512]{2,1,0:T(8,128)S(1)}, u32[]{:S(2)}, u32[]{:S(2)}) %collective-permute-start.4) | collective-permute-done | bytes 163872 | tf_op jit(solution)/shard_map/ppermute | solution.py:437
  38.6 1.6 %collective-permute-start.5 = (f32[2,40,512]{2,1,0:T(8,128)S(1)}, f32[2,40,512]{2,1,0:T(8,128)S(1)}, u32[]{:S(2)}, u32[]{:S(2)}) collective-permute-start(f32[2,40,512]{2,1,0:T(8,128)S(1)} %add.13), channel_id=1, source_target_pairs={{0,4},{2,6},{4,0},{6,2},{8,12},{10,14},{12,8},{14,10},{1,5},{3,7},... | collective-permute-start | bytes 491528 | tf_op jit(solution)/shard_map/ppermute | solution.py:437
  40.3 0.8 reshape.44.spv_ref.spg_ref
  41.8 2.7 %collective-permute-done.5 = f32[2,40,512]{2,1,0:T(8,128)S(1)} collective-permute-done((f32[2,40,512]{2,1,0:T(8,128)S(1)}, f32[2,40,512]{2,1,0:T(8,128)S(1)}, u32[]{:S(2)}, u32[]{:S(2)}) %collective-permute-start.5) | collective-permute-done | bytes 163872 | tf_op jit(solution)/shard_map/ppermute | solution.py:437
  44.6 2.6 %collective-permute-start.6 = (f32[2,40,512]{2,1,0:T(8,128)S(1)}, f32[2,40,512]{2,1,0:T(8,128)S(1)}, u32[]{:S(2)}, u32[]{:S(2)}) collective-permute-start(f32[2,40,512]{2,1,0:T(8,128)S(1)} %add.14), channel_id=1, source_target_pairs={{0,8},{2,10},{4,12},{6,14},{8,0},{10,2},{12,4},{14,6},{1,9},{3,11}... | collective-permute-start | bytes 491528 | tf_op jit(solution)/shard_map/ppermute | solution.py:437
  47.2 5.1 %concatenate.17.edge_ref = bf16[144,512]{1,0:T(8,128)(2,1)} concatenate(bf16[32,512]{1,0:T(8,128)(2,1)S(1)} %bitcast.33, bf16[32,512]{1,0:T(8,128)(2,1)S(1)} %bitcast.34, bf16[38,512]{1,0:T(8,128)(2,1)S(1)} %get-tuple-element.16, bf16[2,512]{1,0:T(2,128)(2,1)S(1)} %broadcast_in_dim.14, bf16[38,512]{1,0:T(8,128)(2,1)S(1)} %get-tuple-element.15, bf16[2,512]{1,0:T(2,128)(2,1)S(1)} %broadcast_in_dim.14), dimensions={0} | concatenate | bytes 294912 | tf_op jit(solution)/shard_map/concatenate | solution.py:500
  52.3 7.2 %query.1.q_ref = bf16[2,2,1168,256]{3,2,1,0:T(8,128)(2,1)} custom-call(bf16[1024,512]{1,0:T(8,128)(2,1)} %bitcast.24, bf16[192,512]{1,0:T(8,128)(2,1)} %bitcast.32, bf16[240,512]{1,0:T(8,128)(2,1)} %bitcast.30, bf16[512,1536]{1,0:T(8,128)(2,1)} %wv_ref.1, f32[25,1536]{1,0:T(8,128)} %reshape.43.sq_ref.sk_ref.sv_ref, bf16[1536,32]{1,0:T(8,128)(2,1)} %bitcast.28), custom_call_target="tpu_custom_call" | custom-call | flops 536870912 | bytes 3145728 | tf_op jit(solution)/shard_map/query/pallas_call | solution.py:567
  59.5 0.7 add.15.stats_ref
  60.2 26.2 %feed.1 = bf16[1024,512]{1,0:T(8,128)(2,1)} custom-call(s32[4]{0:T(128)} %add_convert_fusion.flags_ref, bf16[1024,512]{1,0:T(8,128)(2,1)} %bitcast.25, bf16[144,512]{1,0:T(8,128)(2,1)} %concatenate.17.edge_ref, bf16[2,2,1168,256]{3,2,1,0:T(8,128)(2,1)} %query.1.q_ref, f32[2,40,512]{2,1,0:T(8,128)} %add.15.stats_ref, bf16[1024,512]{1,0:T(8,128)(2,1)} %wp_ref.1, ...), custom_call_target="tpu_custom_call" | custom-call | tf_op jit(solution)/shard_map/feed/pallas_call | solution.py:594
  (32 shorter events, 2.2 us)
Async XLA Ops:
  0.0 14.0 %copy-start.1 = (bf16[5,5,1536]{2,1,0:T(8,128)(2,1)S(1)}, bf16[5,5,1536]{2,1,0:T(8,128)(2,1)}, u32[]{:S(2)}) copy-start(bf16[5,5,1536]{2,1,0:T(8,128)(2,1)} %param.14) | copy-start | bytes 230404
  0.0 14.7 %copy-start = (bf16[48,32,32]{0,2,1:T(8,128)(2,1)S(1)}, bf16[48,32,32]{0,2,1:T(8,128)(2,1)}, u32[]{:S(2)}) copy-start(bf16[48,32,32]{0,2,1:T(8,128)(2,1)} %param.15) | copy-start | bytes 294916
  1.1 7.6 %collective-permute-start = (bf16[3,32,512]{2,0,1:T(4,128)(2,1)S(1)}, bf16[3,32,512]{2,0,1:T(4,128)(2,1)S(1)}, u32[]{:S(2)}, u32[]{:S(2)}) collective-permute-start(bf16[3,32,512]{2,0,1:T(4,128)(2,1)S(1)} %copy.25), channel_id=1, source_target_pairs={{0,2},{2,4},{4,6},{6,8},{8,10},{10,12},{12,14},{1,3},{3,5},{5,7},{... | collective-permute-start | bytes 294920 | tf_op jit(solution)/shard_map/ppermute | solution.py:468
  6.1 6.9 %collective-permute-start.1 = (bf16[3,32,512]{2,0,1:T(4,128)(2,1)S(1)}, bf16[3,32,512]{2,0,1:T(4,128)(2,1)S(1)}, u32[]{:S(2)}, u32[]{:S(2)}) collective-permute-start(bf16[3,32,512]{2,0,1:T(4,128)(2,1)S(1)} %copy.26), channel_id=1, source_target_pairs={{2,0},{4,2},{6,4},{8,6},{10,8},{12,10},{14,12},{3,1},{5,3},{7,5},{... | collective-permute-start | bytes 294920 | tf_op jit(solution)/shard_map/ppermute | solution.py:469
  13.1 3.8 %collective-permute-start.2 = (bf16[3,40,512]{2,1,0:T(8,128)(2,1)S(1)}, bf16[3,40,512]{2,1,0:T(8,128)(2,1)S(1)}, u32[]{:S(2)}, u32[]{:S(2)}) collective-permute-start(bf16[3,40,512]{2,1,0:T(8,128)(2,1)S(1)} %fusion), channel_id=1, source_target_pairs={{0,1},{1,0},{2,3},{3,2},{4,5},{5,4},{6,7},{7,6},{8,9},{9,8},{10,11... | collective-permute-start | bytes 368648 | tf_op jit(solution)/shard_map/ppermute | solution.py:488
  18.6 21.6 %copy-start.2 = (bf16[3,3,4096]{2,1,0:T(4,128)(2,1)S(1)}, bf16[3,3,4096]{2,1,0:T(4,128)(2,1)}, u32[]{:S(2)}) copy-start(bf16[3,3,4096]{2,1,0:T(4,128)(2,1)} %param.19) | copy-start | bytes 221188
  28.7 1.7 %collective-permute-start.3 = (f32[2,40,512]{2,1,0:T(8,128)}, f32[2,40,512]{2,1,0:T(8,128)S(1)}, u32[]{:S(2)}, u32[]{:S(2)}) collective-permute-start(f32[2,40,512]{2,1,0:T(8,128)} %key_value.1), channel_id=1, source_target_pairs={{0,1},{1,0},{2,3},{3,2},{4,5},{5,4},{6,7},{7,6},{8,9},{9,8},{10,11... | collective-permute-start | bytes 491528 | tf_op jit(solution)/shard_map/ppermute | solution.py:437
  31.4 7.2 %collective-permute-start.4 = (f32[2,40,512]{2,1,0:T(8,128)S(1)}, f32[2,40,512]{2,1,0:T(8,128)S(1)}, u32[]{:S(2)}, u32[]{:S(2)}) collective-permute-start(f32[2,40,512]{2,1,0:T(8,128)S(1)} %add.12), channel_id=1, source_target_pairs={{0,2},{2,0},{4,6},{6,4},{8,10},{10,8},{12,14},{14,12},{1,3},{3,1},... | collective-permute-start | bytes 491528 | tf_op jit(solution)/shard_map/ppermute | solution.py:437
  38.6 6.0 %collective-permute-start.5 = (f32[2,40,512]{2,1,0:T(8,128)S(1)}, f32[2,40,512]{2,1,0:T(8,128)S(1)}, u32[]{:S(2)}, u32[]{:S(2)}) collective-permute-start(f32[2,40,512]{2,1,0:T(8,128)S(1)} %add.13), channel_id=1, source_target_pairs={{0,4},{2,6},{4,0},{6,2},{8,12},{10,14},{12,8},{14,10},{1,5},{3,7},... | collective-permute-start | bytes 491528 | tf_op jit(solution)/shard_map/ppermute | solution.py:437
  44.6 14.9 %collective-permute-start.6 = (f32[2,40,512]{2,1,0:T(8,128)S(1)}, f32[2,40,512]{2,1,0:T(8,128)S(1)}, u32[]{:S(2)}, u32[]{:S(2)}) collective-permute-start(f32[2,40,512]{2,1,0:T(8,128)S(1)} %add.14), channel_id=1, source_target_pairs={{0,8},{2,10},{4,12},{6,14},{8,0},{10,2},{12,4},{14,6},{1,9},{3,11}... | collective-permute-start | bytes 491528 | tf_op jit(solution)/shard_map/ppermute | solution.py:437

commit v2 on v0

v2 whole, which is shorter than its diff:
```python
import functools

import jax
import jax.numpy as jnp
from jax import lax
from jax.experimental import pallas as pl
from jax.experimental.pallas import tpu as pltpu
from jax.sharding import PartitionSpec as P

LANES = 128
BLOCK = 256
PAD = 8
REACH = 3
VMEM_BYTES = 60 * 1024 * 1024
BF16 = jnp.bfloat16
F32 = jnp.float32


def lane_chunks(width=BLOCK):
    return [slice(low, low + LANES) for low in range(0, width, LANES)]


def depthwise_rows(streams, span, out_rows, emit):
    sums = [{} for _ in streams]
    for row_in in range(out_rows + span - 1):
        for side, (load, taps) in enumerate(streams):
            views = [load(row_in, b) for b in range(span)]
            for a in range(span):
                row_out = row_in - a
                if not 0 <= row_out < out_rows:
                    continue
                part = views[0] * taps[a * span]
                for b in range(1, span):
                    part = part + views[b] * taps[a * span + b]
                sums[side][row_out] = part if a == 0 else sums[side][row_out] + part
        done = row_in - span + 1
        if done >= 0:
            emit(done, *[s.pop(done) for s in sums])


def tap_list(weight_ref, lanes, rows):
    span = weight_ref.shape[0]
    return [
        jnp.broadcast_to(weight_ref[a, b : b + 1, lanes].astype(F32), (rows, LANES)).astype(BF16)
        for a in range(span)
        for b in range(span)
    ]


def head_mask(size, head):
    return (
        lax.broadcasted_iota(jnp.int32, (size, size), 0) // head
        == lax.broadcasted_iota(jnp.int32, (size, size), 1) // head
    )


def spread_blocks(group_ref):
    count, head, _ = group_ref.shape
    size = count * head
    rows = group_ref[...].reshape(size, head)
    pick = (
        lax.broadcasted_iota(jnp.int32, (head, size), 1) % head
        == lax.broadcasted_iota(jnp.int32, (head, size), 0)
    ).astype(BF16)
    wide = jnp.dot(rows, pick, preferred_element_type=F32)
    return jnp.where(head_mask(size, head), wide, 0.0).astype(BF16)


def fill_keep(keep_ref, out):
    rows, cols = keep_ref.shape
    cell = lax.broadcasted_iota(jnp.int32, (rows * cols, rows), 0)
    own_row = cell // cols == lax.broadcasted_iota(jnp.int32, (rows * cols, rows), 1)
    lines = jnp.dot(
        own_row.astype(BF16), keep_ref[...].astype(F32).astype(BF16), preferred_element_type=F32
    )
    cell = lax.broadcasted_iota(jnp.int32, (rows * cols, cols), 0)
    own_col = cell % cols == lax.broadcasted_iota(jnp.int32, (rows * cols, cols), 1)
    picked = jnp.where(own_col, lines, 0.0).astype(BF16)
    out[...] = jnp.dot(picked, jnp.ones((cols, LANES), BF16), preferred_element_type=F32).astype(
        BF16
    )


def summarise(keys, values, head):
    kv = lax.dot_general(
        keys[...], values[...], (((0,), (0,)), ((), ())), preferred_element_type=F32
    )
    lane_head = lax.broadcasted_iota(jnp.int32, (head, BLOCK), 1) // head
    packed = jnp.zeros((head, BLOCK), F32)
    for h in range(BLOCK // head):
        packed = packed + jnp.where(lane_head == h, kv[h * head : (h + 1) * head], 0.0)
    total = jnp.sum(keys[...].astype(F32), axis=0, keepdims=True)
    return packed, jnp.broadcast_to(total, (8, BLOCK))


def early_kernel(head, main_ref, keep_ref, wk_ref, wv_ref, proj_ref, stats_ref, keep, mat_k):
    @pl.when(pl.program_id(0) == 0)
    def _():
        fill_keep(keep_ref, keep)

    cells = main_ref.shape[0]
    step = 256
    for index, w_ref in enumerate((wk_ref, wv_ref)):
        w = w_ref[...]
        for start in range(0, cells, step):
            p = jnp.dot(main_ref[start : start + step], w, preferred_element_type=F32).astype(BF16)
            proj_ref[0, index, start : start + step] = p
            if index == 0:
                for lanes in lane_chunks():
                    mat_k[start : start + step, lanes] = (
                        jnp.maximum(p[:, lanes], 0) * keep[start : start + step]
                    )
    packed, total = summarise(mat_k, proj_ref.at[0, 1], head)
    stats_ref[0, 0:head] = packed
    stats_ref[0, head : head + 8] = total


def query_project_kernel(main_ref, w_ref, proj_ref):
    cells = main_ref.shape[0]
    step = 256
    w = w_ref[...]
    for start in range(0, cells, step):
        proj_ref[0, start : start + step] = jnp.dot(
            main_ref[start : start + step], w, preferred_element_type=F32
        ).astype(BF16)


def fill_projected(tile, flags, main, halos, w_ref, buf):
    rows, cols = tile
    stride = cols + PAD
    above_ref, below_ref, left_ref, right_ref = halos
    w = w_ref[...]

    def put(row, col, values):
        for ch, lanes in enumerate(lane_chunks()):
            start = PAD + (row + REACH) * stride + col
            buf[ch, pl.ds(start, values.shape[0]), :] = values[:, lanes]

    for row in range(rows):
        put(row, 0, main(slice(row * cols, (row + 1) * cols)).astype(F32))
    for halo_ref, row0 in ((above_ref, -REACH), (below_ref, rows)):
        p = jnp.dot(halo_ref[...], w, preferred_element_type=F32)
        for k in range(REACH):
            low = k * stride
            put(row0 + k, 0, p[low : low + cols])
            tail = p[low + cols : low + stride]
            put(row0 + k, -REACH, jnp.where(flags[0], tail, 0.0)[0:REACH])
            put(row0 + k, cols, jnp.where(flags[1], tail, 0.0)[REACH : 2 * REACH])
    for halo_ref, col0, flag in ((left_ref, -REACH, flags[0]), (right_ref, cols, flags[1])):
        p = jnp.where(flag, jnp.dot(halo_ref[...], w, preferred_element_type=F32), 0.0)
        for k in range(REACH):
            for ch, lanes in enumerate(lane_chunks()):
                start = PAD + REACH * stride + col0 + k
                buf[ch, pl.ds(start, rows, stride=stride), :] = p[k * rows : (k + 1) * rows, lanes]


def key_value_kernel(
    tile,
    head,
    flags_ref,
    proj_ref,
    above_ref,
    below_ref,
    left_ref,
    right_ref,
    keep_ref,
    early_ref,
    wk_ref,
    wv_ref,
    sk_ref,
    sv_ref,
    gk_ref,
    gv_ref,
    stats_ref,
    buf_k,
    buf_v,
    keep,
    mat_k,
    mat_v,
    agg_k,
    agg_v,
):
    rows, cols = tile
    stride = cols + PAD

    @pl.when(pl.program_id(0) == 0)
    def _():
        fill_keep(keep_ref, keep)

    flags = (flags_ref[2] != 0, flags_ref[3] != 0)
    halos = (above_ref, below_ref, left_ref, right_ref)
    parts = (
        (0, wk_ref, sk_ref, gk_ref, buf_k, mat_k, agg_k),
        (1, wv_ref, sv_ref, gv_ref, buf_v, mat_v, agg_v),
    )
    for index, w_ref, s_ref, g_ref, buf, mat, agg_out in parts:
        fill_projected(tile, flags, lambda at, i=index: proj_ref[0, i, at], halos, w_ref, buf)
    for index, w_ref, s_ref, g_ref, buf, mat, agg_out in parts:
        for ch, lanes in enumerate(lane_chunks()):
            taps = tap_list(s_ref, lanes, cols)

            def load(row_in, b, buf=buf, ch=ch):
                start = PAD + (row_in + 1) * stride + b - 2
                return buf[ch, pl.ds(start, cols), :].astype(BF16)

            def emit(row, value, out=mat, lanes=lanes):
                out[row * cols : (row + 1) * cols, lanes] = value

            depthwise_rows([(load, taps)], 5, rows, emit)
        blocks = spread_blocks(g_ref)
        step = 256
        for start in range(0, mat.shape[0], step):
            agg = jnp.dot(mat[start : start + step], blocks, preferred_element_type=F32)
            agg = agg.astype(BF16)
            if index == 0:
                for lanes in lane_chunks():
                    agg_out[start : start + step, lanes] = (
                        jnp.maximum(agg[:, lanes], 0) * keep[start : start + step]
                    )
            else:
                agg_out[start : start + step] = agg
    packed, total = summarise(agg_k, agg_v, head)
    stats_ref[0, 0:head] = early_ref[0, 0:head].astype(BF16)
    stats_ref[0, head : 2 * head] = packed.astype(BF16)
    stats_ref[0, 2 * head :] = jnp.concatenate(
        [early_ref[0, head : head + 8], total], axis=0
    ).astype(BF16)


def query_kernel(
    tile,
    flags_ref,
    proj_ref,
    above_ref,
    below_ref,
    left_ref,
    right_ref,
    w_ref,
    s_ref,
    g_ref,
    edge_ref,
    q_ref,
    buf,
    spread,
):
    rows, cols = tile
    stride = cols + PAD
    cells = rows * cols
    tall = rows + PAD
    flags = (flags_ref[2] != 0, flags_ref[3] != 0)
    halos = (above_ref, below_ref, left_ref, right_ref)
    fill_projected(tile, flags, lambda at: proj_ref[0, at], halos, w_ref, buf)
    side0 = cells + 2 * cols

    def slot(row):
        if row < 0:
            return cells
        if row >= rows:
            return cells + cols
        return row * cols

    for ch, lanes in enumerate(lane_chunks()):
        for row in (-1, rows):
            start = PAD + (row + REACH) * stride
            value = buf[ch, pl.ds(start, cols), :].astype(BF16)
            low = slot(row) - cells
            edge_ref[0, low : low + cols, lanes] = jnp.maximum(value, 0)
        for side, col in enumerate((-1, cols)):
            start = PAD + (REACH - 1) * stride + col
            value = buf[ch, pl.ds(start, tall, stride=stride), :].astype(BF16)
            low = 2 * cols + side * tall
            edge_ref[0, low : low + tall, lanes] = jnp.maximum(value, 0)

        taps = tap_list(s_ref, lanes, cols)

        def load(row_in, b, ch=ch):
            start = PAD + row_in * stride + b - 2
            return buf[ch, pl.ds(start, cols), :].astype(BF16)

        def emit(row, value, lanes=lanes):
            low = slot(row - 1)
            spread[low : low + cols, lanes] = value

        depthwise_rows([(load, taps)], 5, rows + 2, emit)
        taps = tap_list(s_ref, lanes, tall)
        for side, col in enumerate((-1, cols)):
            total = None
            for a in range(5):
                part = None
                for b in range(5):
                    start = PAD + a * stride + col + b - 2
                    view = buf[ch, pl.ds(start, tall, stride=stride), :].astype(BF16)
                    term = view * taps[a * 5 + b]
                    part = term if part is None else part + term
                total = part if total is None else total + part
            low = side0 + side * tall
            spread[low : low + tall, lanes] = total

    blocks = spread_blocks(g_ref)
    count = spread.shape[0]
    for start in range(0, count, 256):
        stop = min(count, start + 256)
        agg = jnp.dot(spread[start:stop], blocks, preferred_element_type=F32)
        q_ref[0, start:stop] = jnp.maximum(agg.astype(BF16), 0)


def rms_add(residual, branch, gain):
    scale = lax.rsqrt(jnp.mean(branch * branch, axis=-1, keepdims=True) + 1e-05)
    return residual.astype(F32) + branch * scale * gain


def silu(x):
    half = 0.5 * x
    return half * jnp.tanh(half) + half


def feed_kernel(
    tile,
    head,
    flags_ref,
    main_ref,
    above_ref,
    below_ref,
    left_ref,
    right_ref,
    proj_ref,
    q_edge_ref,
    q_far_ref,
    mine_ref,
    other_ref,
    wp_ref,
    gain_a_ref,
    wev_ref,
    weg_ref,
    spv_ref,
    spg_ref,
    wr_ref,
    gain_f_ref,
    out_ref,
    mid,
    att,
    edge,
    buf_v,
    buf_g,
    gated,
):
    rows, cols = tile
    stride = cols + PAD
    cells = rows * cols
    tall = rows + PAD
    step_index = pl.program_id(0)
    blocks = proj_ref.shape[0]
    channels = main_ref.shape[1]

    @pl.when(step_index == 0)
    def _():
        same = head_mask(BLOCK, head)
        eye = lax.broadcasted_iota(jnp.int32, (BLOCK, BLOCK), 0) == lax.broadcasted_iota(
            jnp.int32, (BLOCK, BLOCK), 1
        )
        count = mid.shape[0]
        bounds = [(s, s + 256) for s in range(0, cells, 256)] + [(cells, count)]
        for blk in range(blocks):
            mine = flags_ref[4] == blk
            for scale in range(2):
                low = scale * head
                packed = jnp.where(
                    mine,
                    mine_ref[low : low + head].astype(F32),
                    other_ref[low : low + head].astype(F32),
                )
                kv = jnp.where(same, jnp.concatenate([packed] * (BLOCK // head), axis=0), 0.0)
                both = jnp.where(
                    mine,
                    mine_ref[2 * head : 2 * head + 16].astype(F32),
                    other_ref[2 * head : 2 * head + 16].astype(F32),
                )
                sums = both[8 * scale : 8 * scale + 1]
                diag = jnp.where(eye, jnp.broadcast_to(sums, (BLOCK, BLOCK)), 0.0)
                ks = jnp.dot(
                    diag.astype(BF16), same.astype(BF16), preferred_element_type=F32
                ).astype(BF16)
                kv = kv.astype(BF16)
                low = scale * channels + blk * BLOCK
                for start, stop in bounds:
                    if scale:
                        q = q_far_ref[blk, start:stop]
                    elif start < cells:
                        q = jnp.maximum(proj_ref[blk, start:stop], 0)
                    else:
                        q = q_edge_ref[blk]
                    num = jnp.dot(q, kv, preferred_element_type=F32)
                    den = jnp.dot(q, ks, preferred_element_type=F32)
                    att[start:stop, low : low + BLOCK] = (num / (den + 1.0)).astype(BF16)

        edge[0:cols] = above_ref[(REACH - 1) * stride : (REACH - 1) * stride + cols].astype(F32)
        edge[cols : 2 * cols] = below_ref[0:cols].astype(F32)
        top_tail = above_ref[(REACH - 1) * stride + cols : REACH * stride].astype(F32)
        low_tail = below_ref[cols:stride].astype(F32)
        for side, (ref, near) in enumerate(((left_ref, REACH - 1), (right_ref, 0))):
            base = 2 * cols + side * tall
            pick = side * REACH + near
            edge[base : base + 1] = top_tail[pick : pick + 1]
            edge[base + 1 : base + 1 + rows] = ref[near * rows : (near + 1) * rows].astype(F32)
            edge[base + 1 + rows : base + 2 + rows] = low_tail[pick : pick + 1]
            edge[base + 2 + rows : base + tall] = jnp.zeros((tall - rows - 2, channels), F32)

        gain = gain_a_ref[...]
        for start, stop in bounds:
            branch = jnp.dot(att[start:stop], wp_ref[...], preferred_element_type=F32)
            if start < cells:
                mid[start:stop] = rms_add(main_ref[start:stop], branch, gain).astype(BF16)
            else:
                value = rms_add(edge[...], branch, gain)
                index = lax.broadcasted_iota(jnp.int32, (stop - start, 1), 0)
                side = index - 2 * cols
                place = lax.rem(side + tall, tall)
                in_rows = index < 2 * cols
                is_top = (index < cols) | (~in_rows & (place == 0))
                is_bottom = (in_rows & (index >= cols)) | (~in_rows & (place == rows + 1))
                is_left = ~in_rows & (side < tall)
                is_right = ~in_rows & (side >= tall)
                dead = (
                    (is_top & (flags_ref[0] == 0))
                    | (is_bottom & (flags_ref[1] == 0))
                    | (is_left & (flags_ref[2] == 0))
                    | (is_right & (flags_ref[3] == 0))
                )
                mid[start:stop] = jnp.where(dead, 0.0, value).astype(BF16)

    for w_ref, buf in ((wev_ref, buf_v), (weg_ref, buf_g)):
        w = w_ref[...]

        def put(row, values, buf=buf):
            start = PAD + (row + 1) * stride
            for ch, lanes in enumerate(lane_chunks()):
                buf[ch, pl.ds(start, cols), :] = values[:, lanes]

        group = 4
        for first in range(0, rows, group):
            p = silu(
                jnp.dot(
                    mid[first * cols : (first + group) * cols], w, preferred_element_type=F32
                )
            )
            for k in range(group):
                put(first + k, p[k * cols : (k + 1) * cols])
        p = silu(jnp.dot(mid[cells:], w, preferred_element_type=F32))
        put(-1, p[:cols])
        put(rows, p[cols : 2 * cols])
        for side, col in enumerate((-1, cols)):
            low = 2 * cols + side * tall
            for ch, lanes in enumerate(lane_chunks()):
                buf[ch, pl.ds(PAD + col, tall, stride=stride), :] = p[low : low + tall, lanes]

    base = step_index * BLOCK
    for ch, lanes in enumerate(lane_chunks()):
        streams = []
        for buf, sp_ref in ((buf_v, spv_ref), (buf_g, spg_ref)):

            def load(row_in, b, buf=buf, ch=ch):
                start = PAD + row_in * stride + b - 1
                return buf[ch, pl.ds(start, cols), :].astype(BF16)

            streams.append((load, tap_list(sp_ref, lanes, cols)))
        col0 = pl.multiple_of(base + ch * LANES, LANES)

        def emit(row, value, gate, col0=col0):
            gated[row * cols : (row + 1) * cols, pl.ds(col0, LANES)] = (
                value.astype(F32) * silu(gate.astype(F32))
            ).astype(BF16)

        depthwise_rows(streams, 3, rows, emit)

    @pl.when(step_index == pl.num_programs(0) - 1)
    def _():
        gain = gain_f_ref[...]
        for start in range(0, cells, 256):
            reduced = jnp.dot(
                gated[start : start + 256], wr_ref[...], preferred_element_type=F32
            )
            out_ref[start : start + 256] = rms_add(
                mid[start : start + 256], reduced, gain
            ).astype(BF16)


def neighbours(axis):
    count = lax.axis_size(axis)
    forward = [(i, i + 1) for i in range(count - 1)]
    return forward, [(b, a) for a, b in forward]


def total_over(x, axis):
    count = lax.axis_size(axis)
    if count & (count - 1):
        return lax.psum(x.astype(F32), axis).astype(BF16)
    step = 1
    while step < count:
        rest = count // step
        radix = 4 if rest % 4 == 0 and rest != 8 else 2
        total = x.astype(F32)
        for k in range(1, radix):
            pairs = [(i, i ^ (k * step)) for i in range(count)]
            total = total + lax.ppermute(x, axis, pairs).astype(F32)
        x = total.astype(BF16)
        step *= radix
    return x


def body(
    canvas,
    keep_mask,
    w_qkv,
    w_spread,
    w_group,
    w_proj,
    gain_attn,
    w_expand,
    w_spatial,
    w_reduce,
    gain_ff,
):
    rows, cols, channels = canvas.shape
    cells = rows * cols
    head = w_group.shape[1]
    hidden = w_reduce.shape[0]
    blocks = channels // BLOCK
    per = BLOCK // head
    tall = rows + PAD
    stride = cols + PAD
    tile = (rows, cols)
    flat_rows = PAD + (tall + 4) * stride
    flat_rows_ff = PAD + tall * stride

    col_index = lax.axis_index("col")
    col_count = lax.axis_size("col")
    row_index = lax.axis_index("row")
    row_count = lax.axis_size("row")
    swap = [(0, 1), (1, 0)]
    paired = col_count == 2 and blocks == 2

    def strip(low):
        return canvas[:, low : low + REACH].transpose(1, 0, 2)

    if col_count == 2:
        low = jnp.where(col_index == 0, cols - REACH, 0)
        mine = lax.dynamic_slice_in_dim(canvas, low, REACH, axis=1).transpose(1, 0, 2)
        left = right = lax.ppermute(mine, "col", swap)
    else:
        right_way, left_way = neighbours("col")
        left = lax.ppermute(strip(cols - REACH), "col", right_way)
        right = lax.ppermute(strip(0), "col", left_way)

    def wide(low):
        return jnp.concatenate(
            [
                canvas[low : low + REACH],
                left[:, low : low + REACH].transpose(1, 0, 2),
                right[:, low : low + REACH].transpose(1, 0, 2),
                jnp.zeros((REACH, PAD - 2 * REACH, channels), canvas.dtype),
            ],
            axis=1,
        )

    down, up = neighbours("row")
    above = lax.ppermute(wide(rows - REACH), "row", down).reshape(REACH * stride, channels)
    below = lax.ppermute(wide(0), "row", up).reshape(REACH * stride, channels)
    left = left.reshape(REACH * rows, channels)
    right = right.reshape(REACH * rows, channels)
    main = canvas.reshape(cells, channels)
    flags = jnp.stack(
        [
            (row_index > 0).astype(jnp.int32),
            (row_index < row_count - 1).astype(jnp.int32),
            (col_index > 0).astype(jnp.int32),
            (col_index < col_count - 1).astype(jnp.int32),
            col_index.astype(jnp.int32) if paired else jnp.int32(0),
        ]
    )

    def whole(shape):
        return pl.BlockSpec(shape, lambda *_: (0,) * len(shape))

    smem = pl.BlockSpec(memory_space=pltpu.SMEM)
    params = pltpu.CompilerParams(
        dimension_semantics=("arbitrary",), vmem_limit_bytes=VMEM_BYTES
    )

    def cost(macs, moved):
        return pl.CostEstimate(flops=2 * macs, bytes_accessed=moved, transcendentals=0)

    proj_kv, early = pl.pallas_call(
        functools.partial(early_kernel, head),
        grid=(blocks,),
        in_specs=[
            whole(main.shape),
            whole(keep_mask.shape),
            pl.BlockSpec((channels, BLOCK), lambda j: (0, blocks + j)),
            pl.BlockSpec((channels, BLOCK), lambda j: (0, 2 * blocks + j)),
        ],
        out_specs=[
            pl.BlockSpec((1, 2, cells, BLOCK), lambda j: (j, 0, 0, 0)),
            pl.BlockSpec((1, head + 8, BLOCK), lambda j: (j, 0, 0)),
        ],
        out_shape=[
            jax.ShapeDtypeStruct((blocks, 2, cells, BLOCK), BF16),
            jax.ShapeDtypeStruct((blocks, head + 8, BLOCK), F32),
        ],
        scratch_shapes=[pltpu.VMEM((cells, LANES), BF16), pltpu.VMEM((cells, BLOCK), BF16)],
        compiler_params=params,
        cost_estimate=cost(2 * cells * channels * channels, 6 * cells * channels),
        name="early",
    )(main, keep_mask, w_qkv, w_qkv)

    proj_q = pl.pallas_call(
        query_project_kernel,
        grid=(blocks,),
        in_specs=[
            whole(main.shape),
            pl.BlockSpec((channels, BLOCK), lambda j: (0, j)),
        ],
        out_specs=pl.BlockSpec((1, cells, BLOCK), lambda j: (j, 0, 0)),
        out_shape=jax.ShapeDtypeStruct((blocks, cells, BLOCK), BF16),
        compiler_params=params,
        cost_estimate=cost(cells * channels * channels, 4 * cells * channels),
        name="query_project",
    )(main, w_qkv)

    halos = (above, below, left, right)
    halo_specs = [whole(h.shape) for h in halos]
    stats = pl.pallas_call(
        functools.partial(key_value_kernel, tile, head),
        grid=(blocks,),
        in_specs=[
            smem,
            pl.BlockSpec((1, 2, cells, BLOCK), lambda j: (j, 0, 0, 0)),
            *halo_specs,
            whole(keep_mask.shape),
            pl.BlockSpec((1, head + 8, BLOCK), lambda j: (j, 0, 0)),
            pl.BlockSpec((channels, BLOCK), lambda j: (0, blocks + j)),
            pl.BlockSpec((channels, BLOCK), lambda j: (0, 2 * blocks + j)),
            pl.BlockSpec((5, 5, BLOCK), lambda j: (0, 0, blocks + j)),
            pl.BlockSpec((5, 5, BLOCK), lambda j: (0, 0, 2 * blocks + j)),
            pl.BlockSpec((per, head, head), lambda j: (blocks + j, 0, 0)),
            pl.BlockSpec((per, head, head), lambda j: (2 * blocks + j, 0, 0)),
        ],
        out_specs=pl.BlockSpec((1, 2 * head + 16, BLOCK), lambda j: (j, 0, 0)),
        out_shape=jax.ShapeDtypeStruct((blocks, 2 * head + 16, BLOCK), BF16),
        scratch_shapes=[
            pltpu.VMEM((BLOCK // LANES, flat_rows, LANES), F32),
            pltpu.VMEM((BLOCK // LANES, flat_rows, LANES), F32),
            pltpu.VMEM((cells, LANES), BF16),
            pltpu.VMEM((cells, BLOCK), BF16),
            pltpu.VMEM((cells, BLOCK), BF16),
            pltpu.VMEM((cells, BLOCK), BF16),
            pltpu.VMEM((cells, BLOCK), BF16),
        ],
        compiler_params=params,
        cost_estimate=cost(8 * cells * channels * channels, 8 * cells * channels),
        name="key_value",
    )(
        flags,
        proj_kv,
        *halos,
        keep_mask,
        early,
        w_qkv,
        w_qkv,
        w_spread,
        w_spread,
        w_group,
        w_group,
    )
    if paired:
        sent = lax.dynamic_index_in_dim(stats, 1 - col_index, keepdims=False)
        kept = lax.dynamic_index_in_dim(stats, col_index, keepdims=False)
        got = lax.ppermute(sent, "col", swap)
        mine = total_over((kept.astype(F32) + got.astype(F32)).astype(BF16), "row")
        other = lax.ppermute(mine, "col", swap)
    else:
        stats = total_over(total_over(stats, "col"), "row")
        mine, other = stats[0], stats[blocks - 1]

    count = cells + 2 * cols + 2 * tall
    q_edge, q_far = pl.pallas_call(
        functools.partial(query_kernel, tile),
        grid=(blocks,),
        in_specs=[
            smem,
            pl.BlockSpec((1, cells, BLOCK), lambda j: (j, 0, 0)),
            *halo_specs,
            pl.BlockSpec((channels, BLOCK), lambda j: (0, j)),
            pl.BlockSpec((5, 5, BLOCK), lambda j: (0, 0, j)),
            pl.BlockSpec((per, head, head), lambda j: (j, 0, 0)),
        ],
        out_specs=[
            pl.BlockSpec((1, count - cells, BLOCK), lambda j: (j, 0, 0)),
            pl.BlockSpec((1, count, BLOCK), lambda j: (j, 0, 0)),
        ],
        out_shape=[
            jax.ShapeDtypeStruct((blocks, count - cells, BLOCK), BF16),
            jax.ShapeDtypeStruct((blocks, count, BLOCK), BF16),
        ],
        scratch_shapes=[
            pltpu.VMEM((BLOCK // LANES, flat_rows, LANES), F32),
            pltpu.VMEM((count, BLOCK), BF16),
        ],
        compiler_params=params,
        cost_estimate=cost(5 * cells * channels * channels, 6 * cells * channels),
        name="query",
    )(flags, proj_q, *halos, w_qkv, w_spread, w_group)

    steps = hidden // BLOCK
    decoded = pl.pallas_call(
        functools.partial(feed_kernel, tile, head),
        grid=(steps,),
        in_specs=[
            smem,
            whole(main.shape),
            *halo_specs,
            whole(proj_q.shape),
            whole(q_edge.shape),
            whole(q_far.shape),
            whole(mine.shape),
            whole(other.shape),
            whole(w_proj.shape),
            whole((1, channels)),
            pl.BlockSpec((channels, BLOCK), lambda j: (0, j)),
            pl.BlockSpec((channels, BLOCK), lambda j: (0, steps + j)),
            pl.BlockSpec((3, 3, BLOCK), lambda j: (0, 0, j)),
            pl.BlockSpec((3, 3, BLOCK), lambda j: (0, 0, steps + j)),
            whole(w_reduce.shape),
            whole((1, channels)),
        ],
        out_specs=whole(main.shape),
        out_shape=jax.ShapeDtypeStruct(main.shape, BF16),
        scratch_shapes=[
            pltpu.VMEM((count, channels), BF16),
            pltpu.VMEM((count, 2 * channels), BF16),
            pltpu.VMEM((count - cells, channels), F32),
            pltpu.VMEM((BLOCK // LANES, flat_rows_ff, LANES), F32),
            pltpu.VMEM((BLOCK // LANES, flat_rows_ff, LANES), F32),
            pltpu.VMEM((cells, hidden), BF16),
        ],
        compiler_params=params,
        name="feed",
    )(
        flags,
        main,
        *halos,
        proj_q,
        q_edge,
        q_far,
        mine,
        other,
        w_proj,
        gain_attn.reshape(1, channels),
        w_expand,
        w_expand,
        w_spatial,
        w_spatial,
        w_reduce,
        gain_ff.reshape(1, channels),
    )
    return decoded.reshape(rows, cols, channels)


def solution(mesh):
    tile = P(("groups", "row"), "col", None)
    return jax.shard_map(
        body,
        mesh=mesh,
        in_specs=(tile, P(("groups", "row"), "col")) + (P(),) * 9,
        out_specs=tile,
        check_vma=False,
    )
```

time: 378 us -> 80.4 us (0.21); the launches traced: 373 us -> 79.9 us
  other arithmetic: 99 us -> 0.94 us
  waiting for transfers between devices: 98.1 us -> 5.38 us
  blocking collectives: 63 us -> 0 us
  Pallas kernels: 0 us -> 51.2 us
  local copies, waits for them, and re-layouts: 47.6 us -> 7.63 us
  matrix products: 33.2 us -> 0 us
  between operations: 14.2 us -> 0.13 us
    psum x1 -> x0, waiting for transfers between devices: 85.6 us -> none  [body(): kv_stats, key_sums = lax.psum((local_kv, local_ksum), ('row', 'col'))]
    psum x1 -> x0, blocking collectives: 63 us -> none  [body(): kv_stats, key_sums = lax.psum((local_kv, local_ksum), ('row', 'col'))]
    pallas_call x0 -> x5, Pallas kernels: none -> 51.2 us  [the longest x1 26.6 us: body(): pl.pallas_call(functools.partial(feed_kernel, tile, head), grid=(steps,),...]
    reshape x3 -> x0, local copies, waits for them, and re-layouts: 42.6 us -> none  [the longest x2 28 us: body(): projected.reshape(cell_count, 3, heads, head_size)]
    add x2 -> x0, other arithmetic: 36.8 us -> none  [the longest x1 36.8 us: depthwise(): summed + window.astype(jnp.float32) * weight[shift_row, shift_col].astype...]
    convert_element_type x6 -> x3, other arithmetic: 37.4 us -> 0.83 us  [the longest x1 0.79 us: body(): mine = total_over((kept.astype(F32) + got.astype(F32)).astype(BF16), 'row')]
    dot_general x8 -> x0, matrix products: 33.2 us -> none  [the longest x1 13.5 us: body(): jnp.einsum('cgi,gio->cgo', grouped, w_group, preferred_element_type=jnp.f...]
    concatenate x2 -> x1, other arithmetic: 17.4 us -> 0.11 us  [wide(): jnp.concatenate([canvas[low:low + REACH], left[:, low:low + REACH].transp...]
  transfers between devices with their start and end apart: 9 -> 9, of which waited for: 4 -> 3; matrix products, arithmetic and copies ran while one was open for 9% -> 6% of each run, Pallas kernels for 0% -> 18%
where the time goes in v2:
time: 80.4 us; the launch traced here: 79.9 us
  Pallas kernels  51.2 us (64%)
  starting transfers between devices  14.7 us (18%)
  local copies, waits for them, and re-layouts  7.63 us (9%)
  waiting for transfers between devices  5.38 us (7%)
  other arithmetic  0.94 us (1%)
    pallas_call x1, Pallas kernels, body(): pl.pallas_call(functools.partial(feed_kernel, tile, head), grid=(steps,),...  26.6 us
    pallas_call x1, Pallas kernels, body(): pl.pallas_call(functools.partial(key_value_kernel, tile, head), grid=(blo...  10.1 us
    ppermute x4, starting transfers between devices, total_over(): total = total + lax.ppermute(x, axis, pairs).astype(F32)  7.43 us
    pallas_call x1, Pallas kernels, body(): pl.pallas_call(functools.partial(query_kernel, tile), grid=(blocks,), in_...  6.66 us
    ppermute x1, starting transfers between devices, body(): lax.ppermute(wide(rows - REACH), 'row', down)  5.34 us
    pallas_call x1, Pallas kernels, body(): pl.pallas_call(functools.partial(early_kernel, head), grid=(blocks,), in_...  4.89 us
    ppermute x4, waiting for transfers between devices, total_over(): total = total + lax.ppermute(x, axis, pairs).astype(F32)  4.15 us
    unnamed x9, local copies, waits for them, and re-layouts  3.56 us
  transfers between devices with their start and end apart: 9, of which 3 were waited for; matrix products, arithmetic and copies ran while one was open for 6% of the time, Pallas kernels for 18%

profile of v2, /device:TPU:0, one launch (start us, length us, event | category | flops | bytes accessed | tf_op | source)
XLA Modules:
  0.0 79.9 jit_solution(17982418241576846197)
XLA Ops:
  0.0 1.0 %dynamic-slice_bitcast_fusion = bf16[3,32,512]{2,0,1:T(4,128)(2,1)S(1)} fusion(bf16[32,32,512]{2,1,0:T(8,128)(2,1)} %param.11, s32[]{:T(128)S(6)} %select_n.12), kind=kLoop, calls=%fused_computation | loop fusion | bytes 196612 | tf_op jit(solution)/shard_map/transpose | solution.py:547
  1.0 0.6 collective-permute-start
  1.6 1.0 %fusion.1 = (bf16[3,32,512]{2,1,0:T(8,128)(2,1)S(1)}, bf16[3,32,512]{2,1,0:T(8,128)(2,1)S(1)}) fusion(bf16[32,32,512]{2,1,0:T(8,128)(2,1)} %param.11), kind=kLoop, calls=%fused_computation.10 | loop fusion | bytes 393216 | tf_op jit(solution)/shard_map/slice | solution.py:557
  2.8 1.3 %collective-permute-start.2 = (bf16[3,40,512]{2,1,0:T(8,128)(2,1)S(1)}, bf16[3,40,512]{2,1,0:T(8,128)(2,1)S(1)}, u32[]{:S(2)}, u32[]{:S(2)}) collective-permute-start(bf16[3,40,512]{2,1,0:T(8,128)(2,1)S(1)} %get-tuple-element.17), channel_id=1, source_target_pairs={{2,0},{4,2},{6,4},{8,6},{10,8},{12,10},{14,12},{3,1},{5,3},{7,5},{... | collective-permute-start | bytes 368648 | tf_op jit(solution)/shard_map/ppermute | solution.py:567
  4.1 5.3 %collective-permute-start.1 = (bf16[3,40,512]{2,1,0:T(8,128)(2,1)S(1)}, bf16[3,40,512]{2,1,0:T(8,128)(2,1)S(1)}, u32[]{:S(2)}, u32[]{:S(2)}) collective-permute-start(bf16[3,40,512]{2,1,0:T(8,128)(2,1)S(1)} %get-tuple-element.18), channel_id=1, source_target_pairs={{0,2},{2,4},{4,6},{6,8},{8,10},{10,12},{12,14},{1,3},{3,5},{5,7},{... | collective-permute-start | bytes 368648 | tf_op jit(solution)/shard_map/ppermute | solution.py:566
  9.4 2.3 %copy.13.g_ref.gk_ref.gv_ref = bf16[48,32,32]{2,1,0:T(8,128)(2,1)} copy(bf16[48,32,32]{0,2,1:T(8,128)(2,1)} %param.15) | data formatting | bytes 196608 | tf_op args[4]
  11.7 0.6 stack.39.flags_ref
  12.3 4.9 %early.1 = (bf16[2,2,1024,256]{3,2,1,0:T(8,128)(2,1)}, f32[2,40,256]{2,1,0:T(8,128)}) custom-call(bf16[1024,512]{1,0:T(8,128)(2,1)} %bitcast.23, s32[32,32]{1,0:T(8,128)} %keep_ref.3, bf16[512,1536]{1,0:T(8,128)(2,1)} %wv_ref.3, bf16[512,1536]{1,0:T(8,128)(2,1)} %wv_ref.3), custom_call_target="tpu_custom_call" | custom-call | flops 1073741824 | bytes 3145728 | tf_op jit(solution)/shard_map/early/pallas_call | solution.py:592
  17.1 0.7 copy.12
  17.8 0.6 copy-done.1
  18.5 10.1 %key_value.1 = bf16[2,80,256]{2,1,0:T(8,128)(2,1)} custom-call(s32[5]{0:T(128)} %stack.39.flags_ref, bf16[2,2,1024,256]{3,2,1,0:T(8,128)(2,1)} %get-tuple-element.11.proj_ref, bf16[120,512]{1,0:T(8,128)(2,1)} %bitcast.35, bf16[120,512]{1,0:T(8,128)(2,1)} %bitcast.32, bf16[96,512]{1,0:T(8,128)(2,1)} %bitcast.26, bf16[96,512]{1,0:T(8,128)(2,1)} %bitcast.27, ...), custom_call_target="tpu_custom_call" | custom-call | flops 4294967296 | bytes 4194304 | tf_op jit(solution)/shard_map/key_value/pallas_call | solution.py:631
  28.6 0.8 dynamic-slice_bitcast_fusion.1
  29.3 1.2 %collective-permute-done.3 = bf16[80,256]{1,0:T(8,128)(2,1)S(1)} collective-permute-done((bf16[80,256]{1,0:T(8,128)(2,1)S(1)}, bf16[80,256]{1,0:T(8,128)(2,1)S(1)}, u32[]{:S(2)}, u32[]{:S(2)}) %collective-permute-start.3) | collective-permute-done | bytes 40992 | tf_op jit(solution)/shard_map/ppermute | solution.py:677
  30.6 0.8 fusion
  31.4 3.0 %collective-permute-start.4 = (bf16[80,256]{1,0:T(8,128)(2,1)S(1)}, bf16[80,256]{1,0:T(8,128)(2,1)S(1)}, u32[]{:S(2)}, u32[]{:S(2)}) collective-permute-start(bf16[80,256]{1,0:T(8,128)(2,1)S(1)} %fusion), channel_id=1, source_target_pairs={{0,2},{2,0},{4,6},{6,4},{8,10},{10,8},{12,14},{14,12},{1,3},{3,1},... | collective-permute-start | bytes 122888 | tf_op jit(solution)/shard_map/ppermute | solution.py:504
  34.3 2.0 %collective-permute-done.4 = bf16[80,256]{1,0:T(8,128)(2,1)S(1)} collective-permute-done((bf16[80,256]{1,0:T(8,128)(2,1)S(1)}, bf16[80,256]{1,0:T(8,128)(2,1)S(1)}, u32[]{:S(2)}, u32[]{:S(2)}) %collective-permute-start.4) | collective-permute-done | bytes 40992 | tf_op jit(solution)/shard_map/ppermute | solution.py:504
  36.3 1.6 %collective-permute-start.5 = (bf16[80,256]{1,0:T(8,128)(2,1)S(1)}, bf16[80,256]{1,0:T(8,128)(2,1)S(1)}, u32[]{:S(2)}, u32[]{:S(2)}) collective-permute-start(bf16[80,256]{1,0:T(8,128)(2,1)S(1)} %add_convert_fusion.1), channel_id=1, source_target_pairs={{0,4},{2,6},{4,0},{6,2},{8,12},{10,14},{12,8},{14,10},{1,5},{3,7},... | collective-permute-start | bytes 122888 | tf_op jit(solution)/shard_map/ppermute | solution.py:504
  38.0 2.2 %collective-permute-start.6 = (bf16[80,256]{1,0:T(8,128)(2,1)S(1)}, bf16[80,256]{1,0:T(8,128)(2,1)S(1)}, u32[]{:S(2)}, u32[]{:S(2)}) collective-permute-start(bf16[80,256]{1,0:T(8,128)(2,1)S(1)} %add_convert_fusion.1), channel_id=1, source_target_pairs={{0,8},{2,10},{4,12},{6,14},{8,0},{10,2},{12,4},{14,6},{1,9},{3,11}... | collective-permute-start | bytes 122888 | tf_op jit(solution)/shard_map/ppermute | solution.py:504
  40.2 0.6 collective-permute-start.7
  40.8 3.0 %query_project.1.proj_ref = bf16[2,1024,256]{2,1,0:T(8,128)(2,1)} custom-call(bf16[1024,512]{1,0:T(8,128)(2,1)} %bitcast.24, bf16[512,1536]{1,0:T(8,128)(2,1)} %wv_ref.3), custom_call_target="tpu_custom_call" | custom-call | flops 536870912 | bytes 2097152 | tf_op jit(solution)/shard_map/query_project/pallas_call | solution.py:615
  43.8 2.2 %collective-permute-done.7 = bf16[80,256]{1,0:T(8,128)(2,1)S(1)} collective-permute-done((bf16[80,256]{1,0:T(8,128)(2,1)S(1)}, bf16[80,256]{1,0:T(8,128)(2,1)S(1)}, u32[]{:S(2)}, u32[]{:S(2)}) %collective-permute-start.7) | collective-permute-done | bytes 40992 | tf_op jit(solution)/shard_map/ppermute | solution.py:504
  46.1 6.7 %query.1 = (bf16[2,144,256]{2,1,0:T(8,128)(2,1)}, bf16[2,1168,256]{2,1,0:T(8,128)(2,1)}) custom-call(s32[5]{0:T(128)} %stack.39.flags_ref, bf16[2,1024,256]{2,1,0:T(8,128)(2,1)} %query_project.1.proj_ref, bf16[120,512]{1,0:T(8,128)(2,1)} %bitcast.36, bf16[120,512]{1,0:T(8,128)(2,1)} %bitcast.33, bf16[96,512]{1,0:T(8,128)(2,1)} %bitcast.28, ...), custom_call_target="tpu_custom_call" | custom-call | flops 2684354560 | bytes 3145728 | tf_op jit(solution)/shard_map/query/pallas_call | solution.py:685
  52.8 0.6 copy-done.3
  53.4 26.6 %feed.1 = bf16[1024,512]{1,0:T(8,128)(2,1)} custom-call(s32[5]{0:T(128)} %stack.39.flags_ref, bf16[1024,512]{1,0:T(8,128)(2,1)} %bitcast.25, bf16[120,512]{1,0:T(8,128)(2,1)} %bitcast.37, bf16[120,512]{1,0:T(8,128)(2,1)} %bitcast.34, bf16[96,512]{1,0:T(8,128)(2,1)} %bitcast.30, bf16[96,512]{1,0:T(8,128)(2,1)} %bitcast.31, ...), custom_call_target="tpu_custom_call" | custom-call | tf_op jit(solution)/shard_map/feed/pallas_call | solution.py:714
  (20 shorter events, 0.4 us)
Async XLA Ops:
  1.0 1.6 %collective-permute-start = (bf16[3,32,512]{2,0,1:T(4,128)(2,1)S(1)}, bf16[3,32,512]{2,0,1:T(4,128)(2,1)S(1)}, u32[]{:S(2)}, u32[]{:S(2)}) collective-permute-start(bf16[3,32,512]{2,0,1:T(4,128)(2,1)S(1)} %dynamic-slice_bitcast_fusion), channel_id=1, source_target_pairs={{0,1},{1,0},{2,3},{3,2},{4,5},{5,4},{6,7},{7,6},{8,9},{9,8},{10,11... | collective-permute-start | bytes 294920 | tf_op jit(solution)/shard_map/ppermute | solution.py:548
  2.8 15.0 %collective-permute-start.2 = (bf16[3,40,512]{2,1,0:T(8,128)(2,1)S(1)}, bf16[3,40,512]{2,1,0:T(8,128)(2,1)S(1)}, u32[]{:S(2)}, u32[]{:S(2)}) collective-permute-start(bf16[3,40,512]{2,1,0:T(8,128)(2,1)S(1)} %get-tuple-element.17), channel_id=1, source_target_pairs={{2,0},{4,2},{6,4},{8,6},{10,8},{12,10},{14,12},{3,1},{5,3},{7,5},{... | collective-permute-start | bytes 368648 | tf_op jit(solution)/shard_map/ppermute | solution.py:567
  4.1 13.8 %collective-permute-start.1 = (bf16[3,40,512]{2,1,0:T(8,128)(2,1)S(1)}, bf16[3,40,512]{2,1,0:T(8,128)(2,1)S(1)}, u32[]{:S(2)}, u32[]{:S(2)}) collective-permute-start(bf16[3,40,512]{2,1,0:T(8,128)(2,1)S(1)} %get-tuple-element.18), channel_id=1, source_target_pairs={{0,2},{2,4},{4,6},{6,8},{8,10},{10,12},{12,14},{1,3},{3,5},{5,7},{... | collective-permute-start | bytes 368648 | tf_op jit(solution)/shard_map/ppermute | solution.py:566
  17.8 0.7 copy-start.1
  17.8 0.7 copy-start.2
  29.3 1.2 %collective-permute-start.3 = (bf16[80,256]{1,0:T(8,128)(2,1)S(1)}, bf16[80,256]{1,0:T(8,128)(2,1)S(1)}, u32[]{:S(2)}, u32[]{:S(2)}) collective-permute-start(bf16[80,256]{1,0:T(8,128)(2,1)S(1)} %dynamic-slice_bitcast_fusion.1), channel_id=1, source_target_pairs={{0,1},{1,0},{2,3},{3,2},{4,5},{5,4},{6,7},{7,6},{8,9},{9,8},{10,11... | collective-permute-start | bytes 122888 | tf_op jit(solution)/shard_map/ppermute | solution.py:677
  31.4 5.0 %collective-permute-start.4 = (bf16[80,256]{1,0:T(8,128)(2,1)S(1)}, bf16[80,256]{1,0:T(8,128)(2,1)S(1)}, u32[]{:S(2)}, u32[]{:S(2)}) collective-permute-start(bf16[80,256]{1,0:T(8,128)(2,1)S(1)} %fusion), channel_id=1, source_target_pairs={{0,2},{2,0},{4,6},{6,4},{8,10},{10,8},{12,14},{14,12},{1,3},{3,1},... | collective-permute-start | bytes 122888 | tf_op jit(solution)/shard_map/ppermute | solution.py:504
  36.3 7.5 %collective-permute-start.5 = (bf16[80,256]{1,0:T(8,128)(2,1)S(1)}, bf16[80,256]{1,0:T(8,128)(2,1)S(1)}, u32[]{:S(2)}, u32[]{:S(2)}) collective-permute-start(bf16[80,256]{1,0:T(8,128)(2,1)S(1)} %add_convert_fusion.1), channel_id=1, source_target_pairs={{0,4},{2,6},{4,0},{6,2},{8,12},{10,14},{12,8},{14,10},{1,5},{3,7},... | collective-permute-start | bytes 122888 | tf_op jit(solution)/shard_map/ppermute | solution.py:504
  38.0 5.8 %collective-permute-start.6 = (bf16[80,256]{1,0:T(8,128)(2,1)S(1)}, bf16[80,256]{1,0:T(8,128)(2,1)S(1)}, u32[]{:S(2)}, u32[]{:S(2)}) collective-permute-start(bf16[80,256]{1,0:T(8,128)(2,1)S(1)} %add_convert_fusion.1), channel_id=1, source_target_pairs={{0,8},{2,10},{4,12},{6,14},{8,0},{10,2},{12,4},{14,6},{1,9},{3,11}... | collective-permute-start | bytes 122888 | tf_op jit(solution)/shard_map/ppermute | solution.py:504
  40.2 5.8 %collective-permute-start.7 = (bf16[80,256]{1,0:T(8,128)(2,1)S(1)}, bf16[80,256]{1,0:T(8,128)(2,1)S(1)}, u32[]{:S(2)}, u32[]{:S(2)}) collective-permute-start(bf16[80,256]{1,0:T(8,128)(2,1)S(1)} %add_convert_fusion.1), channel_id=1, source_target_pairs={{0,12},{2,14},{4,8},{6,10},{8,4},{10,6},{12,0},{14,2},{1,13},{3,15... | collective-permute-start | bytes 122888 | tf_op jit(solution)/shard_map/ppermute | solution.py:504
  46.0 6.8 %copy-start = (bf16[80,256]{1,0:T(8,128)(2,1)}, bf16[80,256]{1,0:T(8,128)(2,1)S(1)}, u32[]{:S(2)}) copy-start(bf16[80,256]{1,0:T(8,128)(2,1)S(1)} %add_convert_fusion.mine_ref) | copy-start | bytes 122884
  46.0 6.8 %collective-permute-start.8 = (bf16[80,256]{1,0:T(8,128)(2,1)S(1)}, bf16[80,256]{1,0:T(8,128)(2,1)S(1)}, u32[]{:S(2)}, u32[]{:S(2)}) collective-permute-start(bf16[80,256]{1,0:T(8,128)(2,1)S(1)} %add_convert_fusion.mine_ref), channel_id=1, source_target_pairs={{0,1},{1,0},{2,3},{3,2},{4,5},{5,4},{6,7},{7,6},{8,9},{9,8},{10,11... | collective-permute-start | bytes 122888 | tf_op jit(solution)/shard_map/ppermute | solution.py:679
  52.8 0.6 copy-start.3

commit v3 on v2

--- a/solution.py
+++ b/solution.py
@@ -171,7 +171,8 @@
     sv_ref,
     gk_ref,
     gv_ref,
-    stats_ref,
+    mine_ref,
+    sent_ref,
     buf_k,
     buf_v,
     keep,
@@ -220,11 +221,22 @@
             else:
                 agg_out[start : start + step] = agg
     packed, total = summarise(agg_k, agg_v, head)
-    stats_ref[0, 0:head] = early_ref[0, 0:head].astype(BF16)
-    stats_ref[0, head : 2 * head] = packed.astype(BF16)
-    stats_ref[0, 2 * head :] = jnp.concatenate(
-        [early_ref[0, head : head + 8], total], axis=0
-    ).astype(BF16)
+    own = pl.program_id(0) == flags_ref[4]
+
+    def store(out_ref):
+        out_ref[0:head] = early_ref[0, 0:head].astype(BF16)
+        out_ref[head : 2 * head] = packed.astype(BF16)
+        out_ref[2 * head :] = jnp.concatenate(
+            [early_ref[0, head : head + 8], total], axis=0
+        ).astype(BF16)
+
+    @pl.when(own)
+    def _():
+        store(mine_ref)
+
+    @pl.when(jnp.logical_not(own))
+    def _():
+        store(sent_ref)
 
 
 def query_kernel(
@@ -264,12 +276,12 @@
             start = PAD + (row + REACH) * stride
             value = buf[ch, pl.ds(start, cols), :].astype(BF16)
             low = slot(row) - cells
-            edge_ref[0, low : low + cols, lanes] = jnp.maximum(value, 0)
+            edge_ref[low : low + cols, lanes] = jnp.maximum(value, 0)
         for side, col in enumerate((-1, cols)):
             start = PAD + (REACH - 1) * stride + col
             value = buf[ch, pl.ds(start, tall, stride=stride), :].astype(BF16)
             low = 2 * cols + side * tall
-            edge_ref[0, low : low + tall, lanes] = jnp.maximum(value, 0)
+            edge_ref[low : low + tall, lanes] = jnp.maximum(value, 0)
 
         taps = tap_list(s_ref, lanes, cols)
 
@@ -301,7 +313,7 @@
     for start in range(0, count, 256):
         stop = min(count, start + 256)
         agg = jnp.dot(spread[start:stop], blocks, preferred_element_type=F32)
-        q_ref[0, start:stop] = jnp.maximum(agg.astype(BF16), 0)
+        q_ref[start:stop] = jnp.maximum(agg.astype(BF16), 0)
 
 
 def rms_add(residual, branch, gain):
@@ -318,170 +330,228 @@
     tile,
     head,
     flags_ref,
-    main_ref,
+    main_any,
     above_ref,
     below_ref,
     left_ref,
     right_ref,
-    proj_ref,
-    q_edge_ref,
-    q_far_ref,
+    proj_any,
+    q_edge_a_ref,
+    q_edge_b_ref,
+    q_far_a_any,
+    q_far_b_any,
     mine_ref,
     other_ref,
+    wp_any,
+    gain_a_ref,
+    we_any,
+    sp_ref,
+    wr_any,
+    gain_f_ref,
+    out_any,
+    main_ref,
+    proj_ref,
+    q_far_ref,
     wp_ref,
-    gain_a_ref,
-    wev_ref,
-    weg_ref,
-    spv_ref,
-    spg_ref,
+    we_ref,
     wr_ref,
-    gain_f_ref,
-    out_ref,
     mid,
+    half,
     att,
     edge,
-    buf_v,
-    buf_g,
+    buf_av,
+    buf_ag,
+    buf_bv,
+    buf_bg,
     gated,
+    result,
+    sems,
 ):
     rows, cols = tile
     stride = cols + PAD
     cells = rows * cols
     tall = rows + PAD
-    step_index = pl.program_id(0)
     blocks = proj_ref.shape[0]
     channels = main_ref.shape[1]
-
-    @pl.when(step_index == 0)
-    def _():
-        same = head_mask(BLOCK, head)
-        eye = lax.broadcasted_iota(jnp.int32, (BLOCK, BLOCK), 0) == lax.broadcasted_iota(
-            jnp.int32, (BLOCK, BLOCK), 1
+    hidden = wr_ref.shape[0]
+    steps = hidden // BLOCK
+    count = mid.shape[0]
+    big = cells // 2
+    bounds = [(0, big), (big, cells), (cells, count)]
+
+    loads = [
+        pltpu.make_async_copy(src, dst, sems.at[i])
+        for i, (src, dst) in enumerate(
+            (
+                (proj_any, proj_ref),
+                (q_far_a_any, q_far_ref.at[0]),
+                (q_far_b_any, q_far_ref.at[1]),
+                (wp_any, wp_ref),
+                (main_any, main_ref),
+                (we_any, we_ref),
+                (wr_any, wr_ref),
+            )
         )
-        count = mid.shape[0]
-        bounds = [(s, s + 256) for s in range(0, cells, 256)] + [(cells, count)]
+    ]
+    for load in loads:
+        load.start()
+    q_edges = (q_edge_a_ref, q_edge_b_ref)
+
+    edge[0:cols] = above_ref[(REACH - 1) * stride : (REACH - 1) * stride + cols].astype(F32)
+    edge[cols : 2 * cols] = below_ref[0:cols].astype(F32)
+    top_tail = above_ref[(REACH - 1) * stride + cols : REACH * stride].astype(F32)
+    low_tail = below_ref[cols:stride].astype(F32)
+    for side, (ref, near) in enumerate(((left_ref, REACH - 1), (right_ref, 0))):
+        base = 2 * cols + side * tall
+        pick = side * REACH + near
+        edge[base : base + 1] = top_tail[pick : pick + 1]
+        edge[base + 1 : base + 1 + rows] = ref[near * rows : (near + 1) * rows].astype(F32)
+        edge[base + 1 + rows : base + 2 + rows] = low_tail[pick : pick + 1]
+        edge[base + 2 + rows : base + tall] = jnp.zeros((tall - rows - 2, channels), F32)
+
+    same = head_mask(BLOCK, head)
+    eye = lax.broadcasted_iota(jnp.int32, (BLOCK, BLOCK), 0) == lax.broadcasted_iota(
+        jnp.int32, (BLOCK, BLOCK), 1
+    )
+    loads[0].wait()
+    for scale in range(2):
+        if scale:
+            loads[1].wait()
+            loads[2].wait()
         for blk in range(blocks):
             mine = flags_ref[4] == blk
-            for scale in range(2):
-                low = scale * head
-                packed = jnp.where(
-                    mine,
-                    mine_ref[low : low + head].astype(F32),
-                    other_ref[low : low + head].astype(F32),
+            low = scale * head
+            packed = jnp.where(
+                mine,
+                mine_ref[low : low + head].astype(F32),
+                other_ref[low : low + head].astype(F32),
+            )
+            kv = jnp.where(same, jnp.concatenate([packed] * (BLOCK // head), axis=0), 0.0)
+            both = jnp.where(
+                mine,
+                mine_ref[2 * head : 2 * head + 16].astype(F32),
+                other_ref[2 * head : 2 * head + 16].astype(F32),
+            )
+            sums = both[8 * scale : 8 * scale + 1]
+            diag = jnp.where(eye, jnp.broadcast_to(sums, (BLOCK, BLOCK)), 0.0)
+            ks = jnp.dot(
+                diag.astype(BF16), same.astype(BF16), preferred_element_type=F32
+            ).astype(BF16)
+            kv = kv.astype(BF16)
+            low = scale * channels + blk * BLOCK
+            for start, stop in bounds:
+                if scale:
+                    q = q_far_ref[blk, start:stop]
+                elif start < cells:
+                    q = jnp.maximum(proj_ref[blk, start:stop], 0)
+                else:
+                    q = q_edges[blk][...]
+                num = jnp.dot(q, kv, preferred_element_type=F32)
+                den = jnp.dot(q, ks, preferred_element_type=F32)
+                att[start:stop, low : low + BLOCK] = (num / (den + 1.0)).astype(BF16)
+
+    gain = gain_a_ref[...]
+    loads[3].wait()
+    loads[4].wait()
+    for start, stop in bounds:
+        branch = jnp.dot(att[start:stop], wp_ref[...], preferred_element_type=F32)
+        if start < cells:
+            value = rms_add(main_ref[start:stop], branch, gain)
+        else:
+            value = rms_add(edge[...], branch, gain)
+            index = lax.broadcasted_iota(jnp.int32, (stop - start, 1), 0)
+            side = index - 2 * cols
+            place = lax.rem(side + tall, tall)
+            in_rows = index < 2 * cols
+            is_top = (index < cols) | (~in_rows & (place == 0))
+            is_bottom = (in_rows & (index >= cols)) | (~in_rows & (place == rows + 1))
+            is_left = ~in_rows & (side < tall)
+            is_right = ~in_rows & (side >= tall)
+            dead = (
+                (is_top & (flags_ref[0] == 0))
+                | (is_bottom & (flags_ref[1] == 0))
+                | (is_left & (flags_ref[2] == 0))
+                | (is_right & (flags_ref[3] == 0))
+            )
+            value = jnp.where(dead, 0.0, value)
+        value = value.astype(BF16)
+        mid[start:stop] = value
+        half[start:stop] = value * jnp.asarray(0.5, BF16)
+
+    def expand(j, bufs):
+        for part, buf in enumerate(bufs):
+            w = we_ref[:, pl.ds(pl.multiple_of(part * hidden + j * BLOCK, BLOCK), BLOCK)]
+            for start, stop in bounds:
+                p = jnp.dot(half[start:stop], w, preferred_element_type=F32)
+                p = p * jnp.tanh(p) + p
+                for ch, lanes in enumerate(lane_chunks()):
+
+                    def put(row, low):
+                        at = PAD + (row + 1) * stride
+                        buf[ch, pl.ds(at, cols), :] = p[low : low + cols, lanes]
+
+                    if start < cells:
+                        for low in range(0, stop - start, cols):
+                            put((start + low) // cols, low)
+                    else:
+                        put(-1, 0)
+                        put(rows, cols)
+                        for side, col in enumerate((-1, cols)):
+                            low = 2 * cols + side * tall
+                            buf[ch, pl.ds(PAD + col, tall, stride=stride), :] = p[
+                                low : low + tall, lanes
+                            ]
+
+    def mix(j, bufs):
+        for ch in range(BLOCK // LANES):
+            col0 = pl.multiple_of(j * BLOCK + ch * LANES, LANES)
+            streams = []
+            for part, buf in enumerate(bufs):
+
+                def load(row_in, b, buf=buf, ch=ch):
+                    start = PAD + row_in * stride + b - 1
+                    return buf[ch, pl.ds(start, cols), :].astype(BF16)
+
+                at = pl.multiple_of(part * hidden + j * BLOCK + ch * LANES, LANES)
+                taps = tap_list(sp_ref, pl.ds(at, LANES), cols)
+                if part:
+                    taps = [t * jnp.asarray(0.5, BF16) for t in taps]
+                streams.append((load, taps))
+
+            def emit(row, value, gate, col0=col0):
+                gated[row * cols : (row + 1) * cols, pl.ds(col0, LANES)] = value * (
+                    gate * jnp.tanh(gate) + gate
                 )
-                kv = jnp.where(same, jnp.concatenate([packed] * (BLOCK // head), axis=0), 0.0)
-                both = jnp.where(
-                    mine,
-                    mine_ref[2 * head : 2 * head + 16].astype(F32),
-                    other_ref[2 * head : 2 * head + 16].astype(F32),
-                )
-                sums = both[8 * scale : 8 * scale + 1]
-                diag = jnp.where(eye, jnp.broadcast_to(sums, (BLOCK, BLOCK)), 0.0)
-                ks = jnp.dot(
-                    diag.astype(BF16), same.astype(BF16), preferred_element_type=F32
-                ).astype(BF16)
-                kv = kv.astype(BF16)
-                low = scale * channels + blk * BLOCK
-                for start, stop in bounds:
-                    if scale:
-                        q = q_far_ref[blk, start:stop]
-                    elif start < cells:
-                        q = jnp.maximum(proj_ref[blk, start:stop], 0)
-                    else:
-                        q = q_edge_ref[blk]
-                    num = jnp.dot(q, kv, preferred_element_type=F32)
-                    den = jnp.dot(q, ks, preferred_element_type=F32)
-                    att[start:stop, low : low + BLOCK] = (num / (den + 1.0)).astype(BF16)
-
-        edge[0:cols] = above_ref[(REACH - 1) * stride : (REACH - 1) * stride + cols].astype(F32)
-        edge[cols : 2 * cols] = below_ref[0:cols].astype(F32)
-        top_tail = above_ref[(REACH - 1) * stride + cols : REACH * stride].astype(F32)
-        low_tail = below_ref[cols:stride].astype(F32)
-        for side, (ref, near) in enumerate(((left_ref, REACH - 1), (right_ref, 0))):
-            base = 2 * cols + side * tall
-            pick = side * REACH + near
-            edge[base : base + 1] = top_tail[pick : pick + 1]
-            edge[base + 1 : base + 1 + rows] = ref[near * rows : (near + 1) * rows].astype(F32)
-            edge[base + 1 + rows : base + 2 + rows] = low_tail[pick : pick + 1]
-            edge[base + 2 + rows : base + tall] = jnp.zeros((tall - rows - 2, channels), F32)
-
-        gain = gain_a_ref[...]
-        for start, stop in bounds:
-            branch = jnp.dot(att[start:stop], wp_ref[...], preferred_element_type=F32)
-            if start < cells:
-                mid[start:stop] = rms_add(main_ref[start:stop], branch, gain).astype(BF16)
-            else:
-                value = rms_add(edge[...], branch, gain)
-                index = lax.broadcasted_iota(jnp.int32, (stop - start, 1), 0)
-                side = index - 2 * cols
-                place = lax.rem(side + tall, tall)
-                in_rows = index < 2 * cols
-                is_top = (index < cols) | (~in_rows & (place == 0))
-                is_bottom = (in_rows & (index >= cols)) | (~in_rows & (place == rows + 1))
-                is_left = ~in_rows & (side < tall)
-                is_right = ~in_rows & (side >= tall)
-                dead = (
-                    (is_top & (flags_ref[0] == 0))
-                    | (is_bottom & (flags_ref[1] == 0))
-                    | (is_left & (flags_ref[2] == 0))
-                    | (is_right & (flags_ref[3] == 0))
-                )
-                mid[start:stop] = jnp.where(dead, 0.0, value).astype(BF16)
-
-    for w_ref, buf in ((wev_ref, buf_v), (weg_ref, buf_g)):
-        w = w_ref[...]
-
-        def put(row, values, buf=buf):
-            start = PAD + (row + 1) * stride
-            for ch, lanes in enumerate(lane_chunks()):
-                buf[ch, pl.ds(start, cols), :] = values[:, lanes]
-
-        group = 4
-        for first in range(0, rows, group):
-            p = silu(
-                jnp.dot(
-                    mid[first * cols : (first + group) * cols], w, preferred_element_type=F32
-                )
-            )
-            for k in range(group):
-                put(first + k, p[k * cols : (k + 1) * cols])
-        p = silu(jnp.dot(mid[cells:], w, preferred_element_type=F32))
-        put(-1, p[:cols])
-        put(rows, p[cols : 2 * cols])
-        for side, col in enumerate((-1, cols)):
-            low = 2 * cols + side * tall
-            for ch, lanes in enumerate(lane_chunks()):
-                buf[ch, pl.ds(PAD + col, tall, stride=stride), :] = p[low : low + tall, lanes]
-
-    base = step_index * BLOCK
-    for ch, lanes in enumerate(lane_chunks()):
-        streams = []
-        for buf, sp_ref in ((buf_v, spv_ref), (buf_g, spg_ref)):
-
-            def load(row_in, b, buf=buf, ch=ch):
-                start = PAD + row_in * stride + b - 1
-                return buf[ch, pl.ds(start, cols), :].astype(BF16)
-
-            streams.append((load, tap_list(sp_ref, lanes, cols)))
-        col0 = pl.multiple_of(base + ch * LANES, LANES)
-
-        def emit(row, value, gate, col0=col0):
-            gated[row * cols : (row + 1) * cols, pl.ds(col0, LANES)] = (
-                value.astype(F32) * silu(gate.astype(F32))
-            ).astype(BF16)
-
-        depthwise_rows(streams, 3, rows, emit)
-
-    @pl.when(step_index == pl.num_programs(0) - 1)
-    def _():
-        gain = gain_f_ref[...]
-        for start in range(0, cells, 256):
-            reduced = jnp.dot(
-                gated[start : start + 256], wr_ref[...], preferred_element_type=F32
-            )
-            out_ref[start : start + 256] = rms_add(
-                mid[start : start + 256], reduced, gain
-            ).astype(BF16)
+
+            depthwise_rows(streams, 3, rows, emit)
+
+    loads[5].wait()
+    bufs_a, bufs_b = (buf_av, buf_ag), (buf_bv, buf_bg)
+    expand(0, bufs_a)
+
+    def pair(i, carry):
+        j = 2 * i
+        expand(j + 1, bufs_b)
+        mix(j, bufs_a)
+        expand(jnp.minimum(j + 2, steps - 1), bufs_a)
+        mix(j + 1, bufs_b)
+        return carry
+
+    lax.fori_loop(0, steps // 2, pair, 0)
+
+    loads[6].wait()
+    gain = gain_f_ref[...]
+    stores = []
+    for n, (start, stop) in enumerate(bounds[:2]):
+        reduced = jnp.dot(gated[start:stop], wr_ref[...], preferred_element_type=F32)
+        result[start:stop] = rms_add(mid[start:stop], reduced, gain).astype(BF16)
+        store = pltpu.make_async_copy(
+            result.at[start:stop], out_any.at[start:stop], sems.at[len(loads) + n]
+        )
+        store.start()
+        stores.append(store)
+    for store in stores:
+        store.wait()
 
 
 def neighbours(axis):
@@ -532,6 +602,19 @@
     flat_rows = PAD + (tall + 4) * stride
     flat_rows_ff = PAD + tall * stride
 
+    main = canvas.reshape(cells, channels)
+
+    def whole(shape):
+        return pl.BlockSpec(shape, lambda *_: (0,) * len(shape))
+
+    smem = pl.BlockSpec(memory_space=pltpu.SMEM)
+    params = pltpu.CompilerParams(
+        dimension_semantics=("arbitrary",), vmem_limit_bytes=VMEM_BYTES
+    )
+
+    def cost(macs, moved):
+        return pl.CostEstimate(flops=2 * macs, bytes_accessed=moved, transcendentals=0)
+
     col_index = lax.axis_index("col")
     col_count = lax.axis_size("col")
     row_index = lax.axis_index("row")
@@ -550,44 +633,6 @@
         right_way, left_way = neighbours("col")
         left = lax.ppermute(strip(cols - REACH), "col", right_way)
         right = lax.ppermute(strip(0), "col", left_way)
-
-    def wide(low):
-        return jnp.concatenate(
-            [
-                canvas[low : low + REACH],
-                left[:, low : low + REACH].transpose(1, 0, 2),
-                right[:, low : low + REACH].transpose(1, 0, 2),
-                jnp.zeros((REACH, PAD - 2 * REACH, channels), canvas.dtype),
-            ],
-            axis=1,
-        )
-
-    down, up = neighbours("row")
-    above = lax.ppermute(wide(rows - REACH), "row", down).reshape(REACH * stride, channels)
-    below = lax.ppermute(wide(0), "row", up).reshape(REACH * stride, channels)
-    left = left.reshape(REACH * rows, channels)
-    right = right.reshape(REACH * rows, channels)
-    main = canvas.reshape(cells, channels)
-    flags = jnp.stack(
-        [
-            (row_index > 0).astype(jnp.int32),
-            (row_index < row_count - 1).astype(jnp.int32),
-            (col_index > 0).astype(jnp.int32),
-            (col_index < col_count - 1).astype(jnp.int32),
-            col_index.astype(jnp.int32) if paired else jnp.int32(0),
-        ]
-    )
-
-    def whole(shape):
-        return pl.BlockSpec(shape, lambda *_: (0,) * len(shape))
-
-    smem = pl.BlockSpec(memory_space=pltpu.SMEM)
-    params = pltpu.CompilerParams(
-        dimension_semantics=("arbitrary",), vmem_limit_bytes=VMEM_BYTES
-    )
-
-    def cost(macs, moved):
-        return pl.CostEstimate(flops=2 * macs, bytes_accessed=moved, transcendentals=0)
 
     proj_kv, early = pl.pallas_call(
         functools.partial(early_kernel, head),
@@ -612,6 +657,34 @@
         name="early",
     )(main, keep_mask, w_qkv, w_qkv)
 
+    left, right, early = lax.optimization_barrier((left, right, early))
+
+    def wide(low):
+        return jnp.concatenate(
+            [
+                canvas[low : low + REACH],
+                left[:, low : low + REACH].transpose(1, 0, 2),
+                right[:, low : low + REACH].transpose(1, 0, 2),
+                jnp.zeros((REACH, PAD - 2 * REACH, channels), canvas.dtype),
+            ],
+            axis=1,
+        )
+
+    down, up = neighbours("row")
+    above = lax.ppermute(wide(rows - REACH), "row", down).reshape(REACH * stride, channels)
+    below = lax.ppermute(wide(0), "row", up).reshape(REACH * stride, channels)
+    left = left.reshape(REACH * rows, channels)
+    right = right.reshape(REACH * rows, channels)
+    flags = jnp.stack(
+        [
+            (row_index > 0).astype(jnp.int32),
+            (row_index < row_count - 1).astype(jnp.int32),
+            (col_index > 0).astype(jnp.int32),
+            (col_index < col_count - 1).astype(jnp.int32),
+            col_index.astype(jnp.int32) if paired else jnp.int32(0),
+        ]
+    )
+
     proj_q = pl.pallas_call(
         query_project_kernel,
         grid=(blocks,),
@@ -628,7 +701,7 @@
 
     halos = (above, below, left, right)
     halo_specs = [whole(h.shape) for h in halos]
-    stats = pl.pallas_call(
+    mine, sent = pl.pallas_call(
         functools.partial(key_value_kernel, tile, head),
         grid=(blocks,),
         in_specs=[
@@ -644,8 +717,8 @@
             pl.BlockSpec((per, head, head), lambda j: (blocks + j, 0, 0)),
             pl.BlockSpec((per, head, head), lambda j: (2 * blocks + j, 0, 0)),
         ],
-        out_specs=pl.BlockSpec((1, 2 * head + 16, BLOCK), lambda j: (j, 0, 0)),
-        out_shape=jax.ShapeDtypeStruct((blocks, 2 * head + 16, BLOCK), BF16),
+        out_specs=[whole((2 * head + 16, BLOCK))] * 2,
+        out_shape=[jax.ShapeDtypeStruct((2 * head + 16, BLOCK), BF16)] * 2,
         scratch_shapes=[
             pltpu.VMEM((BLOCK // LANES, flat_rows, LANES), F32),
             pltpu.VMEM((BLOCK // LANES, flat_rows, LANES), F32),
@@ -672,92 +745,103 @@
         w_group,
     )
     if paired:
-        sent = lax.dynamic_index_in_dim(stats, 1 - col_index, keepdims=False)
-        kept = lax.dynamic_index_in_dim(stats, col_index, keepdims=False)
         got = lax.ppermute(sent, "col", swap)
-        mine = total_over((kept.astype(F32) + got.astype(F32)).astype(BF16), "row")
+        mine = total_over((mine.astype(F32) + got.astype(F32)).astype(BF16), "row")
         other = lax.ppermute(mine, "col", swap)
     else:
-        stats = total_over(total_over(stats, "col"), "row")
-        mine, other = stats[0], stats[blocks - 1]
+        mine = total_over(total_over(mine, "col"), "row")
+        other = total_over(total_over(sent, "col"), "row")
 
     count = cells + 2 * cols + 2 * tall
-    q_edge, q_far = pl.pallas_call(
-        functools.partial(query_kernel, tile),
-        grid=(blocks,),
+    far = []
+    for blk in range(blocks):
+        far.append(
+            pl.pallas_call(
+                functools.partial(query_kernel, tile),
+                grid=(1,),
+                in_specs=[
+                    smem,
+                    pl.BlockSpec((1, cells, BLOCK), lambda j, blk=blk: (blk, 0, 0)),
+                    *halo_specs,
+                    pl.BlockSpec((channels, BLOCK), lambda j, blk=blk: (0, blk)),
+                    pl.BlockSpec((5, 5, BLOCK), lambda j, blk=blk: (0, 0, blk)),
+                    pl.BlockSpec((per, head, head), lambda j, blk=blk: (blk, 0, 0)),
+                ],
+                out_specs=[whole((count - cells, BLOCK)), whole((count, BLOCK))],
+                out_shape=[
+                    jax.ShapeDtypeStruct((count - cells, BLOCK), BF16),
+                    jax.ShapeDtypeStruct((count, BLOCK), BF16),
+                ],
+                scratch_shapes=[
+                    pltpu.VMEM((BLOCK // LANES, flat_rows, LANES), F32),
+                    pltpu.VMEM((count, BLOCK), BF16),
+                ],
+                compiler_params=params,
+                cost_estimate=cost(3 * cells * channels * channels, 3 * cells * channels),
+                name=f"query_{blk}",
+            )(flags, proj_q, *halos, w_qkv, w_spread, w_group)
+        )
+
+    hbm = pl.BlockSpec(memory_space=pl.ANY)
+    vmem = pl.BlockSpec(memory_space=pltpu.VMEM)
+    buf = pltpu.VMEM((BLOCK // LANES, flat_rows_ff, LANES), F32)
+    decoded = pl.pallas_call(
+        functools.partial(feed_kernel, tile, head),
         in_specs=[
             smem,
-            pl.BlockSpec((1, cells, BLOCK), lambda j: (j, 0, 0)),
-            *halo_specs,
-            pl.BlockSpec((channels, BLOCK), lambda j: (0, j)),
-            pl.BlockSpec((5, 5, BLOCK), lambda j: (0, 0, j)),
-            pl.BlockSpec((per, head, head), lambda j: (j, 0, 0)),
+            hbm,
+            *[vmem] * 4,
+            hbm,
+            vmem,
+            vmem,
+            hbm,
+            hbm,
+            vmem,
+            vmem,
+            hbm,
+            vmem,
+            hbm,
+            vmem,
+            hbm,
+            vmem,
         ],
-        out_specs=[
-            pl.BlockSpec((1, count - cells, BLOCK), lambda j: (j, 0, 0)),
-            pl.BlockSpec((1, count, BLOCK), lambda j: (j, 0, 0)),
-        ],
-        out_shape=[
-            jax.ShapeDtypeStruct((blocks, count - cells, BLOCK), BF16),
-            jax.ShapeDtypeStruct((blocks, count, BLOCK), BF16),
-        ],
-        scratch_shapes=[
-            pltpu.VMEM((BLOCK // LANES, flat_rows, LANES), F32),
-            pltpu.VMEM((count, BLOCK), BF16),
-        ],
-        compiler_params=params,
-        cost_estimate=cost(5 * cells * channels * channels, 6 * cells * channels),
-        name="query",
-    )(flags, proj_q, *halos, w_qkv, w_spread, w_group)
-
-    steps = hidden // BLOCK
-    decoded = pl.pallas_call(
-        functools.partial(feed_kernel, tile, head),
-        grid=(steps,),
-        in_specs=[
-            smem,
-            whole(main.shape),
-            *halo_specs,
-            whole(proj_q.shape),
-            whole(q_edge.shape),
-            whole(q_far.shape),
-            whole(mine.shape),
-            whole(other.shape),
-            whole(w_proj.shape),
-            whole((1, channels)),
-            pl.BlockSpec((channels, BLOCK), lambda j: (0, j)),
-            pl.BlockSpec((channels, BLOCK), lambda j: (0, steps + j)),
-            pl.BlockSpec((3, 3, BLOCK), lambda j: (0, 0, j)),
-            pl.BlockSpec((3, 3, BLOCK), lambda j: (0, 0, steps + j)),
-            whole(w_reduce.shape),
-            whole((1, channels)),
-        ],
-        out_specs=whole(main.shape),
+        out_specs=hbm,
         out_shape=jax.ShapeDtypeStruct(main.shape, BF16),
         scratch_shapes=[
+            pltpu.VMEM(main.shape, BF16),
+            pltpu.VMEM(proj_q.shape, BF16),
+            pltpu.VMEM((blocks, count, BLOCK), BF16),
+            pltpu.VMEM(w_proj.shape, BF16),
+            pltpu.VMEM(w_expand.shape, BF16),
+            pltpu.VMEM(w_reduce.shape, BF16),
+            pltpu.VMEM((count, channels), BF16),
             pltpu.VMEM((count, channels), BF16),
             pltpu.VMEM((count, 2 * channels), BF16),
             pltpu.VMEM((count - cells, channels), F32),
-            pltpu.VMEM((BLOCK // LANES, flat_rows_ff, LANES), F32),
-            pltpu.VMEM((BLOCK // LANES, flat_rows_ff, LANES), F32),
+            buf,
+            buf,
+            buf,
+            buf,
             pltpu.VMEM((cells, hidden), BF16),
+            pltpu.VMEM(main.shape, BF16),
+            pltpu.SemaphoreType.DMA((9,)),
         ],
-        compiler_params=params,
+        compiler_params=pltpu.CompilerParams(vmem_limit_bytes=VMEM_BYTES),
         name="feed",
     )(
         flags,
         main,
         *halos,
         proj_q,
-        q_edge,
-        q_far,
+        far[0][0],
+        far[1][0],
+        far[0][1],
+        far[1][1],
         mine,
         other,
         w_proj,
         gain_attn.reshape(1, channels),
         w_expand,
-        w_expand,
-        w_spatial,
         w_spatial,
         w_reduce,
         gain_ff.reshape(1, channels),

time: 80.4 us -> 76.1 us (0.947)
  Pallas kernels: 51.2 us -> 49.7 us
  waiting for transfers between devices: 5.38 us -> 4.18 us
  local copies, waits for them, and re-layouts: 7.63 us -> 6.55 us
    ppermute x4, waiting for transfers between devices: 4.15 us -> 1.2 us  [total_over(): total = total + lax.ppermute(x, axis, pairs).astype(F32)]
    ppermute x1, waiting for transfers between devices: 0.01 us -> 1.59 us  [body(): lax.ppermute(wide(rows - REACH), 'row', down)]
    optimization_barrier x0 -> x2, local copies, waits for them, and re-layouts: none -> 1.31 us  [body(): left, right, early = lax.optimization_barrier((left, right, early))]
    pallas_call x2 -> x3, Pallas kernels: 33.2 us -> 31.9 us  [the longest x1 23.4 us: body(): pl.pallas_call(functools.partial(feed_kernel, tile, head), in_specs=[smem...]
    unnamed x9 -> x11, local copies, waits for them, and re-layouts: 3.56 us -> 2.58 us
  transfers between devices with their start and end apart: 9 -> 9, of which waited for: 3 -> 3; matrix products, arithmetic and copies ran while one was open for 6% -> 6% of each run, Pallas kernels for 18% -> 22%
where the time goes in v3:
time: 76.1 us; the launch traced here: 75.7 us
  Pallas kernels  49.7 us (65%)
  starting transfers between devices  14.1 us (19%)
  local copies, waits for them, and re-layouts  6.55 us (9%)
  waiting for transfers between devices  4.18 us (5%)
  other arithmetic  0.94 us (1%)
    pallas_call x1, Pallas kernels, body(): pl.pallas_call(functools.partial(feed_kernel, tile, head), in_specs=[smem...  23.4 us
    pallas_call x1, Pallas kernels, body(): pl.pallas_call(functools.partial(key_value_kernel, tile, head), grid=(blo...  9.8 us
    pallas_call x2, Pallas kernels, body(): pl.pallas_call(functools.partial(query_kernel, tile), grid=(1,), in_specs...  8.52 us
    ppermute x4, starting transfers between devices, total_over(): total = total + lax.ppermute(x, axis, pairs).astype(F32)  6.98 us
    ppermute x1, starting transfers between devices, body(): lax.ppermute(wide(rows - REACH), 'row', down)  5.06 us
    pallas_call x1, Pallas kernels, body(): pl.pallas_call(functools.partial(early_kernel, head), grid=(blocks,), in_...  4.93 us
    pallas_call x1, Pallas kernels, body(): pl.pallas_call(query_project_kernel, grid=(blocks,), in_specs=[whole(main...  3.01 us
    unnamed x11, local copies, waits for them, and re-layouts  2.58 us
  transfers between devices with their start and end apart: 9, of which 3 were waited for; matrix products, arithmetic and copies ran while one was open for 6% of the time, Pallas kernels for 22%

profile of v3, /device:TPU:0, one launch (start us, length us, event | category | flops | bytes accessed | tf_op | source)
XLA Modules:
  0.0 75.7 jit_solution(7282059471908485395)
XLA Ops:
  0.0 1.0 %dynamic-slice_bitcast_fusion = bf16[3,32,512]{2,0,1:T(4,128)(2,1)S(1)} fusion(bf16[32,32,512]{2,1,0:T(8,128)(2,1)} %param.11, s32[]{:T(128)S(6)} %select_n.5), kind=kLoop, calls=%fused_computation | loop fusion | bytes 196612 | tf_op jit(solution)/shard_map/transpose | solution.py:630
  1.0 0.6 collective-permute-start
  1.6 1.0 %fusion = (bf16[3,32,512]{2,1,0:T(8,128)(2,1)S(1)}, bf16[3,32,512]{2,1,0:T(8,128)(2,1)S(1)}) fusion(bf16[32,32,512]{2,1,0:T(8,128)(2,1)} %param.11), kind=kLoop, calls=%fused_computation.10 | loop fusion | bytes 393216 | tf_op jit(solution)/shard_map/slice | solution.py:665
  2.6 4.9 %early.1 = (bf16[2,2,1024,256]{3,2,1,0:T(8,128)(2,1)}, f32[2,40,256]{2,1,0:T(8,128)}) custom-call(bf16[1024,512]{1,0:T(8,128)(2,1)} %bitcast.23, s32[32,32]{1,0:T(8,128)} %keep_ref.3, bf16[512,1536]{1,0:T(8,128)(2,1)} %wv_ref.3, bf16[512,1536]{1,0:T(8,128)(2,1)} %wv_ref.3), custom_call_target="tpu_custom_call" | custom-call | flops 1073741824 | bytes 3145728 | tf_op jit(solution)/shard_map/early/pallas_call | solution.py:637
  7.7 1.3 %collective-permute-start.2 = (bf16[3,40,512]{2,1,0:T(8,128)(2,1)S(1)}, bf16[3,40,512]{2,1,0:T(8,128)(2,1)S(1)}, u32[]{:S(2)}, u32[]{:S(2)}) collective-permute-start(bf16[3,40,512]{2,1,0:T(8,128)(2,1)S(1)} %get-tuple-element.33), channel_id=1, source_target_pairs={{2,0},{4,2},{6,4},{8,6},{10,8},{12,10},{14,12},{3,1},{5,3},{7,5},{... | collective-permute-start | bytes 368648 | tf_op jit(solution)/shard_map/ppermute | solution.py:675
  9.0 5.1 %collective-permute-start.1 = (bf16[3,40,512]{2,1,0:T(8,128)(2,1)S(1)}, bf16[3,40,512]{2,1,0:T(8,128)(2,1)S(1)}, u32[]{:S(2)}, u32[]{:S(2)}) collective-permute-start(bf16[3,40,512]{2,1,0:T(8,128)(2,1)S(1)} %get-tuple-element.34), channel_id=1, source_target_pairs={{0,2},{2,4},{4,6},{6,8},{8,10},{10,12},{12,14},{1,3},{3,5},{5,7},{... | collective-permute-start | bytes 368648 | tf_op jit(solution)/shard_map/ppermute | solution.py:674
  14.1 1.3 %copy.14.g_ref.gk_ref.gv_ref = bf16[48,32,32]{2,1,0:T(8,128)(2,1)} copy(bf16[48,32,32]{0,2,1:T(8,128)(2,1)S(1)} %copy-done) | data formatting | bytes 196608 | tf_op args[4]
  15.4 0.6 stack.39.flags_ref
  16.0 0.7 copy.12
  16.7 0.7 copy.13
  17.3 1.6 %collective-permute-done.1 = bf16[3,40,512]{2,1,0:T(8,128)(2,1)S(1)} collective-permute-done((bf16[3,40,512]{2,1,0:T(8,128)(2,1)S(1)}, bf16[3,40,512]{2,1,0:T(8,128)(2,1)S(1)}, u32[]{:S(2)}, u32[]{:S(2)}) %collective-permute-start.1) | collective-permute-done | bytes 122912 | tf_op jit(solution)/shard_map/ppermute | solution.py:674
  18.9 0.6 copy-done.3
  19.6 9.8 %key_value.1 = (bf16[80,256]{1,0:T(8,128)(2,1)}, bf16[80,256]{1,0:T(8,128)(2,1)}) custom-call(s32[5]{0:T(128)} %stack.39.flags_ref, bf16[2,2,1024,256]{3,2,1,0:T(8,128)(2,1)} %get-tuple-element.23.proj_ref, bf16[120,512]{1,0:T(8,128)(2,1)} %bitcast.38, bf16[120,512]{1,0:T(8,128)(2,1)} %bitcast.34, bf16[96,512]{1,0:T(8,128)(2,1)} %bitcast.26, ...), custom_call_target="tpu_custom_call" | custom-call | flops 4294967296 | bytes 4194304 | tf_op jit(solution)/shard_map/key_value/pallas_call | solution.py:704
  29.5 1.4 %collective-permute-done.3 = bf16[80,256]{1,0:T(8,128)(2,1)S(1)} collective-permute-done((bf16[80,256]{1,0:T(8,128)(2,1)}, bf16[80,256]{1,0:T(8,128)(2,1)S(1)}, u32[]{:S(2)}, u32[]{:S(2)}) %collective-permute-start.3) | collective-permute-done | bytes 40992 | tf_op jit(solution)/shard_map/ppermute | solution.py:748
  30.8 0.8 %add_convert_fusion.2 = bf16[80,256]{1,0:T(8,128)(2,1)S(1)} fusion(bf16[80,256]{1,0:T(8,128)(2,1)S(1)} %collective-permute-done.3, bf16[80,256]{1,0:T(8,128)(2,1)} %get-tuple-element.25), kind=kLoop, calls=%fused_computation.5 | loop fusion | flops 81920 | bytes 122880 | tf_op jit(solution)/shard_map/convert_element_type | solution.py:749
  31.6 2.5 %collective-permute-start.4 = (bf16[80,256]{1,0:T(8,128)(2,1)S(1)}, bf16[80,256]{1,0:T(8,128)(2,1)S(1)}, u32[]{:S(2)}, u32[]{:S(2)}) collective-permute-start(bf16[80,256]{1,0:T(8,128)(2,1)S(1)} %add_convert_fusion.2), channel_id=1, source_target_pairs={{0,2},{2,0},{4,6},{6,4},{8,10},{10,8},{12,14},{14,12},{1,3},{3,1},... | collective-permute-start | bytes 122888 | tf_op jit(solution)/shard_map/ppermute | solution.py:574
  34.2 3.0 %query_project.1.proj_ref.proj_any = bf16[2,1024,256]{2,1,0:T(8,128)(2,1)} custom-call(bf16[1024,512]{1,0:T(8,128)(2,1)} %bitcast.24, bf16[512,1536]{1,0:T(8,128)(2,1)} %wv_ref.3), custom_call_target="tpu_custom_call" | custom-call | flops 536870912 | bytes 2097152 | tf_op jit(solution)/shard_map/query_project/pallas_call | solution.py:688
  37.2 1.6 %collective-permute-start.5 = (bf16[80,256]{1,0:T(8,128)(2,1)S(1)}, bf16[80,256]{1,0:T(8,128)(2,1)S(1)}, u32[]{:S(2)}, u32[]{:S(2)}) collective-permute-start(bf16[80,256]{1,0:T(8,128)(2,1)S(1)} %add_convert_fusion.1), channel_id=1, source_target_pairs={{0,4},{2,6},{4,0},{6,2},{8,12},{10,14},{12,8},{14,10},{1,5},{3,7},... | collective-permute-start | bytes 122888 | tf_op jit(solution)/shard_map/ppermute | solution.py:574
  38.8 2.5 %collective-permute-start.6 = (bf16[80,256]{1,0:T(8,128)(2,1)S(1)}, bf16[80,256]{1,0:T(8,128)(2,1)S(1)}, u32[]{:S(2)}, u32[]{:S(2)}) collective-permute-start(bf16[80,256]{1,0:T(8,128)(2,1)S(1)} %add_convert_fusion.1), channel_id=1, source_target_pairs={{0,8},{2,10},{4,12},{6,14},{8,0},{10,2},{12,4},{14,6},{1,9},{3,11}... | collective-permute-start | bytes 122888 | tf_op jit(solution)/shard_map/ppermute | solution.py:574
  41.6 4.2 %query_1.1 = (bf16[144,256]{1,0:T(8,128)(2,1)}, bf16[1168,256]{1,0:T(8,128)(2,1)}) custom-call(s32[5]{0:T(128)} %stack.39.flags_ref, bf16[2,1024,256]{2,1,0:T(8,128)(2,1)} %query_project.1.proj_ref.proj_any, bf16[120,512]{1,0:T(8,128)(2,1)} %bitcast.39, bf16[120,512]{1,0:T(8,128)(2,1)} %bitcast.35, bf16[96,512]{1,0:T(8,128)(2,1)} %bitcast.27, ...), custom_call_target="tpu_custom_call" | custom-call | flops 1610612736 | bytes 1572864 | tf_op jit(solution)/shard_map/query_1/pallas_call | solution.py:759
  45.9 1.2 %collective-permute-done.7 = bf16[80,256]{1,0:T(8,128)(2,1)S(1)} collective-permute-done((bf16[80,256]{1,0:T(8,128)(2,1)S(1)}, bf16[80,256]{1,0:T(8,128)(2,1)S(1)}, u32[]{:S(2)}, u32[]{:S(2)}) %collective-permute-start.7) | collective-permute-done | bytes 40992 | tf_op jit(solution)/shard_map/ppermute | solution.py:574
  47.2 4.3 %query_0.1 = (bf16[144,256]{1,0:T(8,128)(2,1)}, bf16[1168,256]{1,0:T(8,128)(2,1)}) custom-call(s32[5]{0:T(128)} %stack.39.flags_ref, bf16[2,1024,256]{2,1,0:T(8,128)(2,1)} %query_project.1.proj_ref.proj_any, bf16[120,512]{1,0:T(8,128)(2,1)} %bitcast.40, bf16[120,512]{1,0:T(8,128)(2,1)} %bitcast.36, bf16[96,512]{1,0:T(8,128)(2,1)} %bitcast.28, ...), custom_call_target="tpu_custom_call" | custom-call | flops 1610612736 | bytes 1572864 | tf_op jit(solution)/shard_map/query_0/pallas_call | solution.py:759
  51.5 0.6 copy-done.4
  52.1 23.4 %feed.1 = bf16[1024,512]{1,0:T(8,128)(2,1)} custom-call(s32[5]{0:T(128)} %stack.39.flags_ref, bf16[1024,512]{1,0:T(8,128)(2,1)} %bitcast.25, bf16[120,512]{1,0:T(8,128)(2,1)} %bitcast.41, bf16[120,512]{1,0:T(8,128)(2,1)} %bitcast.37, bf16[96,512]{1,0:T(8,128)(2,1)} %bitcast.29, bf16[96,512]{1,0:T(8,128)(2,1)} %bitcast.33, ...), custom_call_target="tpu_custom_call" | custom-call | tf_op jit(solution)/shard_map/feed/pallas_call | solution.py:788
  (23 shorter events, 0.8 us)
Async XLA Ops:
  1.0 6.5 %collective-permute-start = (bf16[3,32,512]{2,0,1:T(4,128)(2,1)S(1)}, bf16[3,32,512]{2,0,1:T(4,128)(2,1)S(1)}, u32[]{:S(2)}, u32[]{:S(2)}) collective-permute-start(bf16[3,32,512]{2,0,1:T(4,128)(2,1)S(1)} %dynamic-slice_bitcast_fusion), channel_id=1, source_target_pairs={{0,1},{1,0},{2,3},{3,2},{4,5},{5,4},{6,7},{7,6},{8,9},{9,8},{10,11... | collective-permute-start | bytes 294920 | tf_op jit(solution)/shard_map/ppermute | solution.py:631
  2.6 11.5 %copy-start = (bf16[48,32,32]{0,2,1:T(8,128)(2,1)S(1)}, bf16[48,32,32]{0,2,1:T(8,128)(2,1)}, u32[]{:S(2)}) copy-start(bf16[48,32,32]{0,2,1:T(8,128)(2,1)} %param.15) | copy-start | bytes 294916
  7.7 9.6 %collective-permute-start.2 = (bf16[3,40,512]{2,1,0:T(8,128)(2,1)S(1)}, bf16[3,40,512]{2,1,0:T(8,128)(2,1)S(1)}, u32[]{:S(2)}, u32[]{:S(2)}) collective-permute-start(bf16[3,40,512]{2,1,0:T(8,128)(2,1)S(1)} %get-tuple-element.33), channel_id=1, source_target_pairs={{2,0},{4,2},{6,4},{8,6},{10,8},{12,10},{14,12},{3,1},{5,3},{7,5},{... | collective-permute-start | bytes 368648 | tf_op jit(solution)/shard_map/ppermute | solution.py:675
  9.0 9.9 %collective-permute-start.1 = (bf16[3,40,512]{2,1,0:T(8,128)(2,1)S(1)}, bf16[3,40,512]{2,1,0:T(8,128)(2,1)S(1)}, u32[]{:S(2)}, u32[]{:S(2)}) collective-permute-start(bf16[3,40,512]{2,1,0:T(8,128)(2,1)S(1)} %get-tuple-element.34), channel_id=1, source_target_pairs={{0,2},{2,4},{4,6},{6,8},{8,10},{10,12},{12,14},{1,3},{3,5},{5,7},{... | collective-permute-start | bytes 368648 | tf_op jit(solution)/shard_map/ppermute | solution.py:674
  17.3 1.6 %copy-start.2 = (bf16[3,40,512]{2,1,0:T(8,128)(2,1)}, bf16[3,40,512]{2,1,0:T(8,128)(2,1)S(1)}, u32[]{:S(2)}) copy-start(bf16[3,40,512]{2,1,0:T(8,128)(2,1)S(1)} %collective-permute-done.2) | copy-start | bytes 368644
  18.9 0.6 copy-start.3
  29.3 1.5 %collective-permute-start.3 = (bf16[80,256]{1,0:T(8,128)(2,1)}, bf16[80,256]{1,0:T(8,128)(2,1)S(1)}, u32[]{:S(2)}, u32[]{:S(2)}) collective-permute-start(bf16[80,256]{1,0:T(8,128)(2,1)} %get-tuple-element.26), channel_id=1, source_target_pairs={{0,1},{1,0},{2,3},{3,2},{4,5},{5,4},{6,7},{7,6},{8,9},{9,8},{10,11... | collective-permute-start | bytes 122888 | tf_op jit(solution)/shard_map/ppermute | solution.py:748
  31.6 5.5 %collective-permute-start.4 = (bf16[80,256]{1,0:T(8,128)(2,1)S(1)}, bf16[80,256]{1,0:T(8,128)(2,1)S(1)}, u32[]{:S(2)}, u32[]{:S(2)}) collective-permute-start(bf16[80,256]{1,0:T(8,128)(2,1)S(1)} %add_convert_fusion.2), channel_id=1, source_target_pairs={{0,2},{2,0},{4,6},{6,4},{8,10},{10,8},{12,14},{14,12},{1,3},{3,1},... | collective-permute-start | bytes 122888 | tf_op jit(solution)/shard_map/ppermute | solution.py:574
  37.2 8.7 %collective-permute-start.5 = (bf16[80,256]{1,0:T(8,128)(2,1)S(1)}, bf16[80,256]{1,0:T(8,128)(2,1)S(1)}, u32[]{:S(2)}, u32[]{:S(2)}) collective-permute-start(bf16[80,256]{1,0:T(8,128)(2,1)S(1)} %add_convert_fusion.1), channel_id=1, source_target_pairs={{0,4},{2,6},{4,0},{6,2},{8,12},{10,14},{12,8},{14,10},{1,5},{3,7},... | collective-permute-start | bytes 122888 | tf_op jit(solution)/shard_map/ppermute | solution.py:574
  38.8 7.1 %collective-permute-start.6 = (bf16[80,256]{1,0:T(8,128)(2,1)S(1)}, bf16[80,256]{1,0:T(8,128)(2,1)S(1)}, u32[]{:S(2)}, u32[]{:S(2)}) collective-permute-start(bf16[80,256]{1,0:T(8,128)(2,1)S(1)} %add_convert_fusion.1), channel_id=1, source_target_pairs={{0,8},{2,10},{4,12},{6,14},{8,0},{10,2},{12,4},{14,6},{1,9},{3,11}... | collective-permute-start | bytes 122888 | tf_op jit(solution)/shard_map/ppermute | solution.py:574
  41.3 5.8 %collective-permute-start.7 = (bf16[80,256]{1,0:T(8,128)(2,1)S(1)}, bf16[80,256]{1,0:T(8,128)(2,1)S(1)}, u32[]{:S(2)}, u32[]{:S(2)}) collective-permute-start(bf16[80,256]{1,0:T(8,128)(2,1)S(1)} %add_convert_fusion.1), channel_id=1, source_target_pairs={{0,12},{2,14},{4,8},{6,10},{8,4},{10,6},{12,0},{14,2},{1,13},{3,15... | collective-permute-start | bytes 122888 | tf_op jit(solution)/shard_map/ppermute | solution.py:574
  47.1 4.4 %copy-start.1 = (bf16[80,256]{1,0:T(8,128)(2,1)}, bf16[80,256]{1,0:T(8,128)(2,1)S(1)}, u32[]{:S(2)}) copy-start(bf16[80,256]{1,0:T(8,128)(2,1)S(1)} %add_convert_fusion.mine_ref) | copy-start | bytes 122884
  47.1 4.4 %collective-permute-start.8 = (bf16[80,256]{1,0:T(8,128)(2,1)S(1)}, bf16[80,256]{1,0:T(8,128)(2,1)S(1)}, u32[]{:S(2)}, u32[]{:S(2)}) collective-permute-start(bf16[80,256]{1,0:T(8,128)(2,1)S(1)} %add_convert_fusion.mine_ref), channel_id=1, source_target_pairs={{0,1},{1,0},{2,3},{3,2},{4,5},{5,4},{6,7},{7,6},{8,9},{9,8},{10,11... | collective-permute-start | bytes 122888 | tf_op jit(solution)/shard_map/ppermute | solution.py:750
  51.5 0.6 copy-start.4

commit v4 on v3

--- a/solution.py
+++ b/solution.py
@@ -11,7 +11,8 @@
 BLOCK = 256
 PAD = 8
 REACH = 3
-VMEM_BYTES = 60 * 1024 * 1024
+SMALL_VMEM = 24 * 1024 * 1024
+FEED_VMEM = 40 * 1024 * 1024
 BF16 = jnp.bfloat16
 F32 = jnp.float32
 
@@ -93,59 +94,16 @@
     return packed, jnp.broadcast_to(total, (8, BLOCK))
 
 
-def early_kernel(head, main_ref, keep_ref, wk_ref, wv_ref, proj_ref, stats_ref, keep, mat_k):
-    @pl.when(pl.program_id(0) == 0)
-    def _():
-        fill_keep(keep_ref, keep)
-
-    cells = main_ref.shape[0]
-    step = 256
-    for index, w_ref in enumerate((wk_ref, wv_ref)):
-        w = w_ref[...]
-        for start in range(0, cells, step):
-            p = jnp.dot(main_ref[start : start + step], w, preferred_element_type=F32).astype(BF16)
-            proj_ref[0, index, start : start + step] = p
-            if index == 0:
-                for lanes in lane_chunks():
-                    mat_k[start : start + step, lanes] = (
-                        jnp.maximum(p[:, lanes], 0) * keep[start : start + step]
-                    )
-    packed, total = summarise(mat_k, proj_ref.at[0, 1], head)
-    stats_ref[0, 0:head] = packed
-    stats_ref[0, head : head + 8] = total
-
-
-def query_project_kernel(main_ref, w_ref, proj_ref):
-    cells = main_ref.shape[0]
-    step = 256
-    w = w_ref[...]
-    for start in range(0, cells, step):
-        proj_ref[0, start : start + step] = jnp.dot(
-            main_ref[start : start + step], w, preferred_element_type=F32
-        ).astype(BF16)
-
-
-def fill_projected(tile, flags, main, halos, w_ref, buf):
+def put_row(buf, stride, row, col, values):
+    for ch, lanes in enumerate(lane_chunks()):
+        start = PAD + (row + REACH) * stride + col
+        buf[ch, pl.ds(start, values.shape[0]), :] = values[:, lanes]
+
+
+def fill_sides(tile, flags, sides, w, buf):
     rows, cols = tile
     stride = cols + PAD
-    above_ref, below_ref, left_ref, right_ref = halos
-    w = w_ref[...]
-
-    def put(row, col, values):
-        for ch, lanes in enumerate(lane_chunks()):
-            start = PAD + (row + REACH) * stride + col
-            buf[ch, pl.ds(start, values.shape[0]), :] = values[:, lanes]
-
-    for row in range(rows):
-        put(row, 0, main(slice(row * cols, (row + 1) * cols)).astype(F32))
-    for halo_ref, row0 in ((above_ref, -REACH), (below_ref, rows)):
-        p = jnp.dot(halo_ref[...], w, preferred_element_type=F32)
-        for k in range(REACH):
-            low = k * stride
-            put(row0 + k, 0, p[low : low + cols])
-            tail = p[low + cols : low + stride]
-            put(row0 + k, -REACH, jnp.where(flags[0], tail, 0.0)[0:REACH])
-            put(row0 + k, cols, jnp.where(flags[1], tail, 0.0)[REACH : 2 * REACH])
+    left_ref, right_ref = sides
     for halo_ref, col0, flag in ((left_ref, -REACH, flags[0]), (right_ref, cols, flags[1])):
         p = jnp.where(flag, jnp.dot(halo_ref[...], w, preferred_element_type=F32), 0.0)
         for k in range(REACH):
@@ -154,17 +112,102 @@
                 buf[ch, pl.ds(start, rows, stride=stride), :] = p[k * rows : (k + 1) * rows, lanes]
 
 
-def key_value_kernel(
+def fill_ends(tile, flags, ends, w, buf):
+    rows, cols = tile
+    stride = cols + PAD
+    for halo_ref, row0 in zip(ends, (-REACH, rows)):
+        p = jnp.dot(halo_ref[...], w, preferred_element_type=F32)
+        for k in range(REACH):
+            low = k * stride
+            put_row(buf, stride, row0 + k, 0, p[low : low + cols])
+            tail = p[low + cols : low + stride]
+            put_row(buf, stride, row0 + k, -REACH, jnp.where(flags[0], tail, 0.0)[0:REACH])
+            put_row(
+                buf, stride, row0 + k, cols, jnp.where(flags[1], tail, 0.0)[REACH : 2 * REACH]
+            )
+
+
+def conv_rows(buf, s_ref, cols, row_first, row_count, out, out_row):
+    stride = cols + PAD
+    for ch, lanes in enumerate(lane_chunks()):
+        taps = tap_list(s_ref, lanes, cols)
+
+        def load(row_in, b, ch=ch):
+            start = PAD + (row_first + row_in - 2 + REACH) * stride + b - 2
+            return buf[ch, pl.ds(start, cols), :].astype(BF16)
+
+        def emit(row, value, lanes=lanes):
+            low = (out_row + row) * cols
+            out[low : low + cols, lanes] = value
+
+        depthwise_rows([(load, taps)], 5, row_count, emit)
+
+
+def keep_keys(values, keep):
+    values = jnp.maximum(values, 0)
+    return jnp.concatenate([values[:, lanes] * keep for lanes in lane_chunks()], axis=1)
+
+
+def interior_kernel(tile, head, first, *refs):
+    if first:
+        (flags_ref, main_ref, keep_in_ref, left_ref, right_ref, *weights, part_ref, keep_ref) = (
+            refs[:13]
+        )
+        fill_keep(keep_in_ref, keep_ref)
+        scratch = refs[13:]
+    else:
+        (flags_ref, main_ref, keep_ref, left_ref, right_ref, *weights, part_ref) = refs[:12]
+        scratch = refs[12:]
+    wk_ref, wv_ref, sk_ref, sv_ref, gk_ref, gv_ref = weights
+    buf_k, buf_v, mat_k, mat_v, sp_k, sp_v, agg_k, agg_v = scratch
+    rows, cols = tile
+    stride = cols + PAD
+    flags = (flags_ref[2] != 0, flags_ref[3] != 0)
+    step = main_ref.shape[0] // 2
+    for w_ref, buf, mat, is_key in ((wk_ref, buf_k, mat_k, True), (wv_ref, buf_v, mat_v, False)):
+        w = w_ref[...]
+        for start in range(0, 2 * step, step):
+            p = jnp.dot(main_ref[start : start + step], w, preferred_element_type=F32)
+            for low in range(0, step, cols):
+                put_row(buf, stride, (start + low) // cols, 0, p[low : low + cols])
+            p = p.astype(BF16)
+            if is_key:
+                p = keep_keys(p, keep_ref[start : start + step])
+            mat[start : start + step] = p
+        fill_sides(tile, flags, (left_ref, right_ref), w, buf)
+    packed, total = summarise(mat_k, mat_v, head)
+    part_ref[0:head] = packed
+    part_ref[2 * head : 2 * head + 8] = total
+    for s_ref, g_ref, buf, spread, out, is_key in (
+        (sk_ref, gk_ref, buf_k, sp_k, agg_k, True),
+        (sv_ref, gv_ref, buf_v, sp_v, agg_v, False),
+    ):
+        conv_rows(buf, s_ref, cols, 2, rows - 4, spread, 0)
+        blocks = spread_blocks(g_ref)
+        count = spread.shape[0]
+        for start in range(0, count, count // 2):
+            stop = start + count // 2
+            agg = jnp.dot(spread[start:stop], blocks, preferred_element_type=F32).astype(BF16)
+            if is_key:
+                agg = keep_keys(agg, keep_ref[2 * cols + start : 2 * cols + stop])
+            out[start:stop] = agg
+    packed, total = summarise(agg_k, agg_v, head)
+    part_ref[head : 2 * head] = packed
+    part_ref[2 * head + 8 : 2 * head + 16] = total
+
+
+def border_kernel(
     tile,
     head,
     flags_ref,
-    proj_ref,
+    main_ref,
     above_ref,
     below_ref,
     left_ref,
     right_ref,
     keep_ref,
-    early_ref,
+    part_a_ref,
+    part_b_ref,
     wk_ref,
     wv_ref,
     sk_ref,
@@ -175,59 +218,48 @@
     sent_ref,
     buf_k,
     buf_v,
-    keep,
-    mat_k,
-    mat_v,
+    sp_k,
+    sp_v,
     agg_k,
     agg_v,
 ):
     rows, cols = tile
     stride = cols + PAD
-
-    @pl.when(pl.program_id(0) == 0)
-    def _():
-        fill_keep(keep_ref, keep)
-
     flags = (flags_ref[2] != 0, flags_ref[3] != 0)
-    halos = (above_ref, below_ref, left_ref, right_ref)
-    parts = (
-        (0, wk_ref, sk_ref, gk_ref, buf_k, mat_k, agg_k),
-        (1, wv_ref, sv_ref, gv_ref, buf_v, mat_v, agg_v),
-    )
-    for index, w_ref, s_ref, g_ref, buf, mat, agg_out in parts:
-        fill_projected(tile, flags, lambda at, i=index: proj_ref[0, i, at], halos, w_ref, buf)
-    for index, w_ref, s_ref, g_ref, buf, mat, agg_out in parts:
-        for ch, lanes in enumerate(lane_chunks()):
-            taps = tap_list(s_ref, lanes, cols)
-
-            def load(row_in, b, buf=buf, ch=ch):
-                start = PAD + (row_in + 1) * stride + b - 2
-                return buf[ch, pl.ds(start, cols), :].astype(BF16)
-
-            def emit(row, value, out=mat, lanes=lanes):
-                out[row * cols : (row + 1) * cols, lanes] = value
-
-            depthwise_rows([(load, taps)], 5, rows, emit)
-        blocks = spread_blocks(g_ref)
-        step = 256
-        for start in range(0, mat.shape[0], step):
-            agg = jnp.dot(mat[start : start + step], blocks, preferred_element_type=F32)
-            agg = agg.astype(BF16)
-            if index == 0:
-                for lanes in lane_chunks():
-                    agg_out[start : start + step, lanes] = (
-                        jnp.maximum(agg[:, lanes], 0) * keep[start : start + step]
-                    )
-            else:
-                agg_out[start : start + step] = agg
+    for w_ref, buf in ((wk_ref, buf_k), (wv_ref, buf_v)):
+        w = w_ref[...]
+        for row0 in (0, rows - 4):
+            p = jnp.dot(
+                main_ref[row0 * cols : (row0 + 4) * cols], w, preferred_element_type=F32
+            )
+            for k in range(4):
+                put_row(buf, stride, row0 + k, 0, p[k * cols : (k + 1) * cols])
+        fill_sides(tile, flags, (left_ref, right_ref), w, buf)
+        fill_ends(tile, flags, (above_ref, below_ref), w, buf)
+    for s_ref, g_ref, buf, spread, out, is_key in (
+        (sk_ref, gk_ref, buf_k, sp_k, agg_k, True),
+        (sv_ref, gv_ref, buf_v, sp_v, agg_v, False),
+    ):
+        conv_rows(buf, s_ref, cols, 0, 2, spread, 0)
+        conv_rows(buf, s_ref, cols, rows - 2, 2, spread, 2)
+        agg = jnp.dot(spread[...], spread_blocks(g_ref), preferred_element_type=F32).astype(BF16)
+        if is_key:
+            keep = jnp.concatenate(
+                [keep_ref[0 : 2 * cols], keep_ref[(rows - 2) * cols : rows * cols]], axis=0
+            )
+            agg = keep_keys(agg, keep)
+        out[...] = agg
     packed, total = summarise(agg_k, agg_v, head)
-    own = pl.program_id(0) == flags_ref[4]
+    step = pl.program_id(0)
+    part = jnp.where(step == 0, part_a_ref[...], part_b_ref[...])
+    own = step == flags_ref[4]
 
     def store(out_ref):
-        out_ref[0:head] = early_ref[0, 0:head].astype(BF16)
-        out_ref[head : 2 * head] = packed.astype(BF16)
-        out_ref[2 * head :] = jnp.concatenate(
-            [early_ref[0, head : head + 8], total], axis=0
+        out_ref[0:head] = part[0:head].astype(BF16)
+        out_ref[head : 2 * head] = (part[head : 2 * head] + packed).astype(BF16)
+        low = 2 * head
+        out_ref[low : low + 16] = jnp.concatenate(
+            [part[low : low + 8], part[low + 8 : low + 16] + total], axis=0
         ).astype(BF16)
 
     @pl.when(own)
@@ -237,6 +269,26 @@
     @pl.when(jnp.logical_not(own))
     def _():
         store(sent_ref)
+
+
+def query_project_kernel(main_ref, w_ref, proj_ref):
+    cells = main_ref.shape[0]
+    step = 256
+    w = w_ref[...]
+    for start in range(0, cells, step):
+        proj_ref[0, start : start + step] = jnp.dot(
+            main_ref[start : start + step], w, preferred_element_type=F32
+        ).astype(BF16)
+
+
+def fill_projected(tile, flags, main, halos, w_ref, buf):
+    rows, cols = tile
+    w = w_ref[...]
+    for row in range(rows):
+        values = main(slice(row * cols, (row + 1) * cols)).astype(F32)
+        put_row(buf, cols + PAD, row, 0, values)
+    fill_ends(tile, flags, halos[:2], w, buf)
+    fill_sides(tile, flags, halos[2:], w, buf)
 
 
 def query_kernel(
@@ -554,6 +606,19 @@
         store.wait()
 
 
+def wide(canvas, left, right, low):
+    channels = canvas.shape[2]
+    return jnp.concatenate(
+        [
+            canvas[low : low + REACH],
+            left[:, low : low + REACH].transpose(1, 0, 2),
+            right[:, low : low + REACH].transpose(1, 0, 2),
+            jnp.zeros((REACH, PAD - 2 * REACH, channels), canvas.dtype),
+        ],
+        axis=1,
+    )
+
+
 def neighbours(axis):
     count = lax.axis_size(axis)
     forward = [(i, i + 1) for i in range(count - 1)]
@@ -566,8 +631,7 @@
         return lax.psum(x.astype(F32), axis).astype(BF16)
     step = 1
     while step < count:
-        rest = count // step
-        radix = 4 if rest % 4 == 0 and rest != 8 else 2
+        radix = 2
         total = x.astype(F32)
         for k in range(1, radix):
             pairs = [(i, i ^ (k * step)) for i in range(count)]
@@ -609,7 +673,7 @@
 
     smem = pl.BlockSpec(memory_space=pltpu.SMEM)
     params = pltpu.CompilerParams(
-        dimension_semantics=("arbitrary",), vmem_limit_bytes=VMEM_BYTES
+        dimension_semantics=("arbitrary",), vmem_limit_bytes=SMALL_VMEM
     )
 
     def cost(macs, moved):
@@ -634,47 +698,6 @@
         left = lax.ppermute(strip(cols - REACH), "col", right_way)
         right = lax.ppermute(strip(0), "col", left_way)
 
-    proj_kv, early = pl.pallas_call(
-        functools.partial(early_kernel, head),
-        grid=(blocks,),
-        in_specs=[
-            whole(main.shape),
-            whole(keep_mask.shape),
-            pl.BlockSpec((channels, BLOCK), lambda j: (0, blocks + j)),
-            pl.BlockSpec((channels, BLOCK), lambda j: (0, 2 * blocks + j)),
-        ],
-        out_specs=[
-            pl.BlockSpec((1, 2, cells, BLOCK), lambda j: (j, 0, 0, 0)),
-            pl.BlockSpec((1, head + 8, BLOCK), lambda j: (j, 0, 0)),
-        ],
-        out_shape=[
-            jax.ShapeDtypeStruct((blocks, 2, cells, BLOCK), BF16),
-            jax.ShapeDtypeStruct((blocks, head + 8, BLOCK), F32),
-        ],
-        scratch_shapes=[pltpu.VMEM((cells, LANES), BF16), pltpu.VMEM((cells, BLOCK), BF16)],
-        compiler_params=params,
-        cost_estimate=cost(2 * cells * channels * channels, 6 * cells * channels),
-        name="early",
-    )(main, keep_mask, w_qkv, w_qkv)
-
-    left, right, early = lax.optimization_barrier((left, right, early))
-
-    def wide(low):
-        return jnp.concatenate(
-            [
-                canvas[low : low + REACH],
-                left[:, low : low + REACH].transpose(1, 0, 2),
-                right[:, low : low + REACH].transpose(1, 0, 2),
-                jnp.zeros((REACH, PAD - 2 * REACH, channels), canvas.dtype),
-            ],
-            axis=1,
-        )
-
-    down, up = neighbours("row")
-    above = lax.ppermute(wide(rows - REACH), "row", down).reshape(REACH * stride, channels)
-    below = lax.ppermute(wide(0), "row", up).reshape(REACH * stride, channels)
-    left = left.reshape(REACH * rows, channels)
-    right = right.reshape(REACH * rows, channels)
     flags = jnp.stack(
         [
             (row_index > 0).astype(jnp.int32),
@@ -685,6 +708,75 @@
         ]
     )
 
+    def cell_scratch(count, copies):
+        return [pltpu.VMEM((count, BLOCK), BF16)] * copies
+
+    flat_buf = pltpu.VMEM((BLOCK // LANES, flat_rows, LANES), F32)
+    part_shape = (2 * head + 16, BLOCK)
+
+    def interior(blk, keep_in):
+        first = blk == 0
+        out_specs = [whole(part_shape)]
+        out_shape = [jax.ShapeDtypeStruct(part_shape, F32)]
+        if first:
+            out_specs.append(whole((cells, LANES)))
+            out_shape.append(jax.ShapeDtypeStruct((cells, LANES), BF16))
+        k_at, v_at = blocks + blk, 2 * blocks + blk
+        return pl.pallas_call(
+            functools.partial(interior_kernel, tile, head, first),
+            grid=(1,),
+            in_specs=[
+                smem,
+                whole(main.shape),
+                whole(keep_in.shape),
+                whole((REACH * rows, channels)),
+                whole((REACH * rows, channels)),
+                pl.BlockSpec((channels, BLOCK), lambda j: (0, k_at)),
+                pl.BlockSpec((channels, BLOCK), lambda j: (0, v_at)),
+                pl.BlockSpec((5, 5, BLOCK), lambda j: (0, 0, k_at)),
+                pl.BlockSpec((5, 5, BLOCK), lambda j: (0, 0, v_at)),
+                pl.BlockSpec((per, head, head), lambda j: (k_at, 0, 0)),
+                pl.BlockSpec((per, head, head), lambda j: (v_at, 0, 0)),
+            ],
+            out_specs=out_specs,
+            out_shape=out_shape,
+            scratch_shapes=[
+                flat_buf,
+                flat_buf,
+                *cell_scratch(cells, 2),
+                *cell_scratch(cells - 4 * cols, 4),
+            ],
+            compiler_params=params,
+            cost_estimate=cost(5 * cells * channels * channels, 4 * cells * channels),
+            name=f"interior_{blk}",
+        )(
+            flags,
+            main,
+            keep_in,
+            left.reshape(REACH * rows, channels),
+            right.reshape(REACH * rows, channels),
+            w_qkv,
+            w_qkv,
+            w_spread,
+            w_spread,
+            w_group,
+            w_group,
+        )
+
+    down, up = neighbours("row")
+    with jax.named_scope("row_down"):
+        above = lax.ppermute(wide(canvas, left, right, rows - REACH), "row", down)
+    with jax.named_scope("inner_a"):
+        part_a, keep = interior(0, keep_mask)
+    edges, part_a = lax.optimization_barrier((wide(canvas, left, right, 0), part_a))
+    with jax.named_scope("row_up"):
+        below = lax.ppermute(edges, "row", up)
+    with jax.named_scope("inner_b"):
+        (part_b,) = interior(1, keep)
+    above = above.reshape(REACH * stride, channels)
+    below = below.reshape(REACH * stride, channels)
+    left = left.reshape(REACH * rows, channels)
+    right = right.reshape(REACH * rows, channels)
     proj_q = pl.pallas_call(
         query_project_kernel,
         grid=(blocks,),
@@ -702,14 +794,15 @@
     halos = (above, below, left, right)
     halo_specs = [whole(h.shape) for h in halos]
     mine, sent = pl.pallas_call(
-        functools.partial(key_value_kernel, tile, head),
+        functools.partial(border_kernel, tile, head),
         grid=(blocks,),
         in_specs=[
             smem,
-            pl.BlockSpec((1, 2, cells, BLOCK), lambda j: (j, 0, 0, 0)),
+            whole(main.shape),
             *halo_specs,
-            whole(keep_mask.shape),
-            pl.BlockSpec((1, head + 8, BLOCK), lambda j: (j, 0, 0)),
+            whole(keep.shape),
+            whole(part_shape),
+            whole(part_shape),
             pl.BlockSpec((channels, BLOCK), lambda j: (0, blocks + j)),
             pl.BlockSpec((channels, BLOCK), lambda j: (0, 2 * blocks + j)),
             pl.BlockSpec((5, 5, BLOCK), lambda j: (0, 0, blocks + j)),
@@ -717,26 +810,19 @@
             pl.BlockSpec((per, head, head), lambda j: (blocks + j, 0, 0)),
             pl.BlockSpec((per, head, head), lambda j: (2 * blocks + j, 0, 0)),
         ],
-        out_specs=[whole((2 * head + 16, BLOCK))] * 2,
-        out_shape=[jax.ShapeDtypeStruct((2 * head + 16, BLOCK), BF16)] * 2,
-        scratch_shapes=[
-            pltpu.VMEM((BLOCK // LANES, flat_rows, LANES), F32),
-            pltpu.VMEM((BLOCK // LANES, flat_rows, LANES), F32),
-            pltpu.VMEM((cells, LANES), BF16),
-            pltpu.VMEM((cells, BLOCK), BF16),
-            pltpu.VMEM((cells, BLOCK), BF16),
-            pltpu.VMEM((cells, BLOCK), BF16),
-            pltpu.VMEM((cells, BLOCK), BF16),
-        ],
+        out_specs=[whole(part_shape)] * 2,
+        out_shape=[jax.ShapeDtypeStruct(part_shape, BF16)] * 2,
+        scratch_shapes=[flat_buf, flat_buf, *cell_scratch(4 * cols, 4)],
         compiler_params=params,
-        cost_estimate=cost(8 * cells * channels * channels, 8 * cells * channels),
-        name="key_value",
+        cost_estimate=cost(cells * channels * channels, 2 * cells * channels),
+        name="border",
     )(
         flags,
-        proj_kv,
+        main,
         *halos,
-        keep_mask,
-        early,
+        keep,
+        part_a,
+        part_b,
         w_qkv,
         w_qkv,
         w_spread,
@@ -826,7 +912,7 @@
             pltpu.VMEM(main.shape, BF16),
             pltpu.SemaphoreType.DMA((9,)),
         ],
-        compiler_params=pltpu.CompilerParams(vmem_limit_bytes=VMEM_BYTES),
+        compiler_params=pltpu.CompilerParams(vmem_limit_bytes=FEED_VMEM),
         name="feed",
     )(
         flags,

time: 76.1 us -> 66.4 us (0.87)
  Pallas kernels: 49.7 us -> 40.5 us
  waiting for transfers between devices: 4.18 us -> 6.56 us
  local copies, waits for them, and re-layouts: 6.55 us -> 5.13 us
  starting transfers between devices: 14.1 us -> 13.2 us
  other arithmetic: 0.94 us -> 0.16 us
    pallas_call x2 -> x3, Pallas kernels: 14.7 us -> 11.6 us  [the longest x2 8.19 us: interior(): pl.pallas_call(functools.partial(interior_kernel, tile, head, first), gri...]
    pallas_call x2, Pallas kernels: 8.52 us -> 5.38 us  [body(): pl.pallas_call(functools.partial(query_kernel, tile), grid=(1,), in_specs...]
    ppermute x4 -> x3, waiting for transfers between devices: 1.2 us -> 3.45 us  [total_over(): total = total + lax.ppermute(x, axis, pairs).astype(F32)]
    pallas_call x1, Pallas kernels: 3.01 us -> 0.95 us  [body(): pl.pallas_call(query_project_kernel, grid=(blocks,), in_specs=[whole(main...]
    optimization_barrier x2 -> x0, local copies, waits for them, and re-layouts: 1.31 us -> none  [body(): left, right, early = lax.optimization_barrier((left, right, early))]
    convert_element_type x1, other arithmetic: 0.79 us -> 0.01 us  [body(): mine = total_over((mine.astype(F32) + got.astype(F32)).astype(BF16), 'row')]
    unnamed x11 -> x23, local copies, waits for them, and re-layouts: 2.58 us -> 2.83 us
    ppermute x4 -> x3, starting transfers between devices: 6.98 us -> 6.79 us  [total_over(): total = total + lax.ppermute(x, axis, pairs).astype(F32)]
  transfers between devices with their start and end apart: 9 -> 8, of which waited for: 3 -> 4; matrix products, arithmetic and copies ran while one was open for 6% -> 4% of each run, Pallas kernels for 22% -> 22%
where the time goes in v4:
time: 66.4 us; the launch traced here: 66.1 us
  Pallas kernels  40.5 us (61%)
  starting transfers between devices  13.2 us (20%)
  waiting for transfers between devices  6.56 us (10%)
  local copies, waits for them, and re-layouts  5.13 us (8%)
    pallas_call x1, Pallas kernels, body(): pl.pallas_call(functools.partial(feed_kernel, tile, head), in_specs=[smem...  22.7 us
    pallas_call x2, Pallas kernels, interior(): pl.pallas_call(functools.partial(interior_kernel, tile, head, first), gri...  8.19 us
    ppermute x3, starting transfers between devices, total_over(): total = total + lax.ppermute(x, axis, pairs).astype(F32)  6.79 us
    pallas_call x2, Pallas kernels, body(): pl.pallas_call(functools.partial(query_kernel, tile), grid=(1,), in_specs...  5.38 us
    ppermute x1, starting transfers between devices, body(): above = lax.ppermute(wide(canvas, left, right, rows - REACH), 'row', down)  4.43 us
    ppermute x3, waiting for transfers between devices, total_over(): total = total + lax.ppermute(x, axis, pairs).astype(F32)  3.45 us
    pallas_call x1, Pallas kernels, body(): pl.pallas_call(functools.partial(border_kernel, tile, head), grid=(blocks...  3.38 us
    unnamed x23, local copies, waits for them, and re-layouts  2.83 us
  transfers between devices with their start and end apart: 8, of which 4 were waited for; matrix products, arithmetic and copies ran while one was open for 4% of the time, Pallas kernels for 22%

profile of v4, /device:TPU:0, one launch (start us, length us, event | category | flops | bytes accessed | tf_op | source)
XLA Modules:
  0.0 66.1 jit_solution(16037965985047114835)
XLA Ops:
  0.0 1.1 %dynamic-slice_bitcast_fusion = bf16[3,32,512]{2,0,1:T(4,128)(2,1)S(1)} fusion(bf16[32,32,512]{2,1,0:T(8,128)(2,1)} %param.11, s32[]{:T(128)S(6)} %select_n.5), kind=kLoop, calls=%fused_computation | loop fusion | bytes 196612 | tf_op jit(solution)/shard_map/transpose | solution.py:694
  1.2 0.6 collective-permute-start
  1.7 1.0 %fusion = (bf16[3,32,512]{2,1,0:T(8,128)(2,1)S(1)}, bf16[3,32,512]{2,1,0:T(8,128)(2,1)S(1)}) fusion(bf16[32,32,512]{2,1,0:T(8,128)(2,1)} %param.11), kind=kLoop, calls=%fused_computation.9 | loop fusion | bytes 393216 | tf_op jit(solution)/shard_map/slice | solution.py:613
  2.7 1.6 %copy.13.refs_9_.refs_10_.g_ref.gk_ref.gv_ref = bf16[48,32,32]{2,1,0:T(8,128)(2,1)S(1)} copy(bf16[48,32,32]{0,2,1:T(8,128)(2,1)} %param.15) | data formatting | bytes 196608 | tf_op args[4]
  4.3 0.1 pad.7.clone
  4.4 0.1 stack.39.refs_0_.flags_ref
  4.5 0.1 maximum_maximum_fusion.1
  4.6 4.4 %collective-permute-start.1 = (bf16[3,40,512]{2,1,0:T(8,128)(2,1)S(1)}, bf16[3,40,512]{2,1,0:T(8,128)(2,1)S(1)}, u32[]{:S(2)}, u32[]{:S(2)}) collective-permute-start(bf16[3,40,512]{2,1,0:T(8,128)(2,1)S(1)} %get-tuple-element.30), channel_id=1, source_target_pairs={{0,2},{2,4},{4,6},{6,8},{8,10},{10,12},{12,14},{1,3},{3,5},{5,7},{... | collective-permute-start | bytes 368648 | tf_op jit(solution)/shard_map/row_down/ppermute | solution.py:768
  9.1 1.2 %copy-done.1 = bf16[32,32,512]{2,1,0:T(8,128)(2,1)S(1)} copy-done((bf16[32,32,512]{2,1,0:T(8,128)(2,1)S(1)}, bf16[32,32,512]{2,1,0:T(8,128)(2,1)}, u32[]{:S(2)}) %copy-start.1) | copy-done | bytes 1048600
  10.3 4.1 %interior_0.1 = (f32[80,256]{1,0:T(8,128)S(1)}, bf16[1024,128]{1,0:T(8,128)(2,1)S(1)}) custom-call(s32[5]{0:T(128)S(1)} %stack.39.refs_0_.flags_ref, bf16[1024,512]{1,0:T(8,128)(2,1)S(1)} %bitcast.18, s32[32,32]{1,0:T(8,128)S(1)} %copy-done.10, bf16[96,512]{1,0:T(8,128)(2,1)S(1)} %bitcast.23, bf16[96,512]{1,0:T(8,128)(2,1)S(1)} %bitcast.24, ...), custom_call_target="tpu_custom_call" | custom-call | flops 2684354560 | bytes 2097152 | tf_op jit(solution)/shard_map/inner_a/interior_0/pallas_call | solution.py:725
  14.4 1.3 %collective-permute-start.2 = (bf16[3,40,512]{2,1,0:T(8,128)(2,1)S(1)}, bf16[3,40,512]{2,1,0:T(8,128)(2,1)S(1)}, u32[]{:S(2)}, u32[]{:S(2)}) collective-permute-start(bf16[3,40,512]{2,1,0:T(8,128)(2,1)S(1)} %get-tuple-element.16), channel_id=1, source_target_pairs={{2,0},{4,2},{6,4},{8,6},{10,8},{12,10},{14,12},{3,1},{5,3},{7,5},{... | collective-permute-start | bytes 368648 | tf_op jit(solution)/shard_map/row_up/ppermute | solution.py:773
  15.7 4.1 %interior_1.1.part_b_ref = f32[80,256]{1,0:T(8,128)S(1)} custom-call(s32[5]{0:T(128)S(1)} %stack.39.refs_0_.flags_ref, bf16[1024,512]{1,0:T(8,128)(2,1)S(1)} %bitcast.19, bf16[1024,128]{1,0:T(8,128)(2,1)S(1)} %get-tuple-element.21.refs_2_.keep_ref, bf16[96,512]{1,0:T(8,128)(2,1)S(1)} %bitcast.25, bf16[96,512]{1,0:T(8,128)(2,1)S(1)} %bitcast.26, ...), custom_call_target="tpu_custom_call" | custom-call | flops 2684354560 | bytes 2097152 | tf_op jit(solution)/shard_map/inner_b/interior_1/pallas_call | solution.py:725
  19.8 1.9 %collective-permute-done.2 = bf16[3,40,512]{2,1,0:T(8,128)(2,1)S(1)} collective-permute-done((bf16[3,40,512]{2,1,0:T(8,128)(2,1)S(1)}, bf16[3,40,512]{2,1,0:T(8,128)(2,1)S(1)}, u32[]{:S(2)}, u32[]{:S(2)}) %collective-permute-start.2) | collective-permute-done | bytes 122912 | tf_op jit(solution)/shard_map/row_up/ppermute | solution.py:773
  21.7 3.4 %border.1 = (bf16[80,256]{1,0:T(8,128)(2,1)S(1)}, bf16[80,256]{1,0:T(8,128)(2,1)S(1)}) custom-call(s32[5]{0:T(128)S(1)} %stack.39.refs_0_.flags_ref, bf16[1024,512]{1,0:T(8,128)(2,1)S(1)} %bitcast.20, bf16[120,512]{1,0:T(8,128)(2,1)S(1)} %bitcast.35, bf16[120,512]{1,0:T(8,128)(2,1)S(1)} %bitcast.39, bf16[96,512]{1,0:T(8,128)(2,1)S(1)} %bitcast.27, ...), custom_call_target="tpu_custom_call" | custom-call | flops 536870912 | bytes 1048576 | tf_op jit(solution)/shard_map/border/pallas_call | solution.py:796
  25.2 1.2 %collective-permute-done.3 = bf16[80,256]{1,0:T(8,128)(2,1)S(1)} collective-permute-done((bf16[80,256]{1,0:T(8,128)(2,1)S(1)}, bf16[80,256]{1,0:T(8,128)(2,1)S(1)}, u32[]{:S(2)}, u32[]{:S(2)}) %collective-permute-start.3) | collective-permute-done | bytes 40992 | tf_op jit(solution)/shard_map/ppermute | solution.py:834
  26.4 2.5 %collective-permute-start.4 = (bf16[80,256]{1,0:T(8,128)(2,1)S(1)}, bf16[80,256]{1,0:T(8,128)(2,1)S(1)}, u32[]{:S(2)}, u32[]{:S(2)}) collective-permute-start(bf16[80,256]{1,0:T(8,128)(2,1)S(1)} %add_convert_fusion.3), channel_id=1, source_target_pairs={{0,2},{2,0},{4,6},{6,4},{8,10},{10,8},{12,14},{14,12},{1,3},{3,1},... | collective-permute-start | bytes 122888 | tf_op jit(solution)/shard_map/ppermute | solution.py:638
  28.9 2.0 %collective-permute-done.4 = bf16[80,256]{1,0:T(8,128)(2,1)S(1)} collective-permute-done((bf16[80,256]{1,0:T(8,128)(2,1)S(1)}, bf16[80,256]{1,0:T(8,128)(2,1)S(1)}, u32[]{:S(2)}, u32[]{:S(2)}) %collective-permute-start.4) | collective-permute-done | bytes 40992 | tf_op jit(solution)/shard_map/ppermute | solution.py:638
  30.9 1.6 %collective-permute-start.5 = (bf16[80,256]{1,0:T(8,128)(2,1)S(1)}, bf16[80,256]{1,0:T(8,128)(2,1)S(1)}, u32[]{:S(2)}, u32[]{:S(2)}) collective-permute-start(bf16[80,256]{1,0:T(8,128)(2,1)S(1)} %add_convert_fusion.2), channel_id=1, source_target_pairs={{0,4},{2,6},{4,0},{6,2},{8,12},{10,14},{12,8},{14,10},{1,5},{3,7},... | collective-permute-start | bytes 122888 | tf_op jit(solution)/shard_map/ppermute | solution.py:638
  32.5 0.9 %query_project.1.proj_ref.proj_any = bf16[2,1024,256]{2,1,0:T(8,128)(2,1)S(1)} custom-call(bf16[1024,512]{1,0:T(8,128)(2,1)S(1)} %bitcast.21, bf16[512,1536]{1,0:T(8,128)(2,1)S(1)} %copy-done), custom_call_target="tpu_custom_call" | custom-call | flops 536870912 | bytes 2097152 | tf_op jit(solution)/shard_map/query_project/pallas_call | solution.py:780
  33.5 1.5 %collective-permute-done.5 = bf16[80,256]{1,0:T(8,128)(2,1)S(1)} collective-permute-done((bf16[80,256]{1,0:T(8,128)(2,1)S(1)}, bf16[80,256]{1,0:T(8,128)(2,1)S(1)}, u32[]{:S(2)}, u32[]{:S(2)}) %collective-permute-start.5) | collective-permute-done | bytes 40992 | tf_op jit(solution)/shard_map/ppermute | solution.py:638
  35.0 2.7 %collective-permute-start.6 = (bf16[80,256]{1,0:T(8,128)(2,1)S(1)}, bf16[80,256]{1,0:T(8,128)(2,1)S(1)}, u32[]{:S(2)}, u32[]{:S(2)}) collective-permute-start(bf16[80,256]{1,0:T(8,128)(2,1)S(1)} %add_convert_fusion.1), channel_id=1, source_target_pairs={{0,8},{2,10},{4,12},{6,14},{8,0},{10,2},{12,4},{14,6},{1,9},{3,11}... | collective-permute-start | bytes 122888 | tf_op jit(solution)/shard_map/ppermute | solution.py:638
  37.6 2.7 %query_1.1 = (bf16[144,256]{1,0:T(8,128)(2,1)S(1)}, bf16[1168,256]{1,0:T(8,128)(2,1)S(1)}) custom-call(s32[5]{0:T(128)S(1)} %stack.39.refs_0_.flags_ref, bf16[2,1024,256]{2,1,0:T(8,128)(2,1)S(1)} %query_project.1.proj_ref.proj_any, bf16[120,512]{1,0:T(8,128)(2,1)S(1)} %bitcast.36, bf16[120,512]{1,0:T(8,128)(2,1)S(1)} %bitcast.40, ...), custom_call_target="tpu_custom_call" | custom-call | flops 1610612736 | bytes 1572864 | tf_op jit(solution)/shard_map/query_1/pallas_call | solution.py:845
  40.5 2.7 %query_0.1 = (bf16[144,256]{1,0:T(8,128)(2,1)S(1)}, bf16[1168,256]{1,0:T(8,128)(2,1)S(1)}) custom-call(s32[5]{0:T(128)S(1)} %stack.39.refs_0_.flags_ref, bf16[2,1024,256]{2,1,0:T(8,128)(2,1)S(1)} %query_project.1.proj_ref.proj_any, bf16[120,512]{1,0:T(8,128)(2,1)S(1)} %bitcast.37, bf16[120,512]{1,0:T(8,128)(2,1)S(1)} %bitcast.41, ...), custom_call_target="tpu_custom_call" | custom-call | flops 1610612736 | bytes 1572864 | tf_op jit(solution)/shard_map/query_0/pallas_call | solution.py:845
  43.3 22.7 %feed.1 = bf16[1024,512]{1,0:T(8,128)(2,1)} custom-call(s32[5]{0:T(128)S(1)} %stack.39.refs_0_.flags_ref, bf16[1024,512]{1,0:T(8,128)(2,1)S(1)} %bitcast.22, bf16[120,512]{1,0:T(8,128)(2,1)S(1)} %bitcast.38, bf16[120,512]{1,0:T(8,128)(2,1)S(1)} %bitcast.42, bf16[96,512]{1,0:T(8,128)(2,1)S(1)} %bitcast.33, bf16[96,512]{1,0:T(8,128)(2,1)S(1)} %bitcast.34, ...), custom_call_target="tpu_custom_call" | custom-call | tf_op jit(solution)/shard_map/feed/pallas_call | solution.py:874
  (34 shorter events, 0.3 us)
Async XLA Ops:
  0.0 9.0 %copy-start = (bf16[512,1536]{1,0:T(8,128)(2,1)S(1)}, bf16[512,1536]{1,0:T(8,128)(2,1)}, u32[]{:S(2)}) copy-start(bf16[512,1536]{1,0:T(8,128)(2,1)} %wv_ref.1) | copy-start | bytes 4718596
  0.0 9.1 %copy-start.6 = (bf16[5,5,1536]{2,1,0:T(8,128)(2,1)S(1)}, bf16[5,5,1536]{2,1,0:T(8,128)(2,1)}, u32[]{:S(2)}) copy-start(bf16[5,5,1536]{2,1,0:T(8,128)(2,1)} %sv_ref.1) | copy-start | bytes 230404
  0.0 9.1 %copy-start.10 = (s32[32,32]{1,0:T(8,128)S(1)}, s32[32,32]{1,0:T(8,128)}, u32[]{:S(2)}) copy-start(s32[32,32]{1,0:T(8,128)} %refs_2_.1) | copy-start | bytes 12292
  1.2 3.3 %collective-permute-start = (bf16[3,32,512]{2,0,1:T(4,128)(2,1)S(1)}, bf16[3,32,512]{2,0,1:T(4,128)(2,1)S(1)}, u32[]{:S(2)}, u32[]{:S(2)}) collective-permute-start(bf16[3,32,512]{2,0,1:T(4,128)(2,1)S(1)} %dynamic-slice_bitcast_fusion), channel_id=1, source_target_pairs={{0,1},{1,0},{2,3},{3,2},{4,5},{5,4},{6,7},{7,6},{8,9},{9,8},{10,11... | collective-permute-start | bytes 294920 | tf_op jit(solution)/shard_map/ppermute | solution.py:695
  4.6 15.2 %collective-permute-start.1 = (bf16[3,40,512]{2,1,0:T(8,128)(2,1)S(1)}, bf16[3,40,512]{2,1,0:T(8,128)(2,1)S(1)}, u32[]{:S(2)}, u32[]{:S(2)}) collective-permute-start(bf16[3,40,512]{2,1,0:T(8,128)(2,1)S(1)} %get-tuple-element.30), channel_id=1, source_target_pairs={{0,2},{2,4},{4,6},{6,8},{8,10},{10,12},{12,14},{1,3},{3,5},{5,7},{... | collective-permute-start | bytes 368648 | tf_op jit(solution)/shard_map/row_down/ppermute | solution.py:768
  9.1 1.2 %copy-start.1 = (bf16[32,32,512]{2,1,0:T(8,128)(2,1)S(1)}, bf16[32,32,512]{2,1,0:T(8,128)(2,1)}, u32[]{:S(2)}) copy-start(bf16[32,32,512]{2,1,0:T(8,128)(2,1)} %param.11) | copy-start | bytes 3145732
  14.4 7.3 %collective-permute-start.2 = (bf16[3,40,512]{2,1,0:T(8,128)(2,1)S(1)}, bf16[3,40,512]{2,1,0:T(8,128)(2,1)S(1)}, u32[]{:S(2)}, u32[]{:S(2)}) collective-permute-start(bf16[3,40,512]{2,1,0:T(8,128)(2,1)S(1)} %get-tuple-element.16), channel_id=1, source_target_pairs={{2,0},{4,2},{6,4},{8,6},{10,8},{12,10},{14,12},{3,1},{5,3},{7,5},{... | collective-permute-start | bytes 368648 | tf_op jit(solution)/shard_map/row_up/ppermute | solution.py:773
  25.1 1.3 %collective-permute-start.3 = (bf16[80,256]{1,0:T(8,128)(2,1)S(1)}, bf16[80,256]{1,0:T(8,128)(2,1)S(1)}, u32[]{:S(2)}, u32[]{:S(2)}) collective-permute-start(bf16[80,256]{1,0:T(8,128)(2,1)S(1)} %get-tuple-element.24), channel_id=1, source_target_pairs={{0,1},{1,0},{2,3},{3,2},{4,5},{5,4},{6,7},{7,6},{8,9},{9,8},{10,11... | collective-permute-start | bytes 122888 | tf_op jit(solution)/shard_map/ppermute | solution.py:834
  26.4 4.5 %collective-permute-start.4 = (bf16[80,256]{1,0:T(8,128)(2,1)S(1)}, bf16[80,256]{1,0:T(8,128)(2,1)S(1)}, u32[]{:S(2)}, u32[]{:S(2)}) collective-permute-start(bf16[80,256]{1,0:T(8,128)(2,1)S(1)} %add_convert_fusion.3), channel_id=1, source_target_pairs={{0,2},{2,0},{4,6},{6,4},{8,10},{10,8},{12,14},{14,12},{1,3},{3,1},... | collective-permute-start | bytes 122888 | tf_op jit(solution)/shard_map/ppermute | solution.py:638
  30.9 4.1 %collective-permute-start.5 = (bf16[80,256]{1,0:T(8,128)(2,1)S(1)}, bf16[80,256]{1,0:T(8,128)(2,1)S(1)}, u32[]{:S(2)}, u32[]{:S(2)}) collective-permute-start(bf16[80,256]{1,0:T(8,128)(2,1)S(1)} %add_convert_fusion.2), channel_id=1, source_target_pairs={{0,4},{2,6},{4,0},{6,2},{8,12},{10,14},{12,8},{14,10},{1,5},{3,7},... | collective-permute-start | bytes 122888 | tf_op jit(solution)/shard_map/ppermute | solution.py:638
  35.0 5.4 %collective-permute-start.6 = (bf16[80,256]{1,0:T(8,128)(2,1)S(1)}, bf16[80,256]{1,0:T(8,128)(2,1)S(1)}, u32[]{:S(2)}, u32[]{:S(2)}) collective-permute-start(bf16[80,256]{1,0:T(8,128)(2,1)S(1)} %add_convert_fusion.1), channel_id=1, source_target_pairs={{0,8},{2,10},{4,12},{6,14},{8,0},{10,2},{12,4},{14,6},{1,9},{3,11}... | collective-permute-start | bytes 122888 | tf_op jit(solution)/shard_map/ppermute | solution.py:638
  37.6 5.6 %copy-start.4 = (bf16[2048,512]{1,0:T(8,128)(2,1)S(1)}, bf16[2048,512]{1,0:T(8,128)(2,1)}, u32[]{:S(2)}) copy-start(bf16[2048,512]{1,0:T(8,128)(2,1)} %wr_any.1) | copy-start | bytes 6291460
  37.6 5.6 %copy-start.5 = (bf16[1024,512]{1,0:T(8,128)(2,1)S(1)}, bf16[1024,512]{1,0:T(8,128)(2,1)}, u32[]{:S(2)}) copy-start(bf16[1024,512]{1,0:T(8,128)(2,1)} %wp_any.1) | copy-start | bytes 3145732
  40.4 2.9 %copy-start.2 = (bf16[32,32,512]{2,1,0:T(8,128)(2,1)S(1)}, bf16[32,32,512]{2,1,0:T(8,128)(2,1)}, u32[]{:S(2)}) copy-start(bf16[32,32,512]{2,1,0:T(8,128)(2,1)} %param.11) | copy-start | bytes 3145732
  40.4 2.9 %copy-start.3 = (bf16[512,4096]{1,0:T(8,128)(2,1)S(1)}, bf16[512,4096]{1,0:T(8,128)(2,1)}, u32[]{:S(2)}) copy-start(bf16[512,4096]{1,0:T(8,128)(2,1)} %we_any.1) | copy-start | bytes 12582916
  40.4 2.9 %copy-start.7 = (bf16[3,3,4096]{2,1,0:T(4,128)(2,1)S(1)}, bf16[3,3,4096]{2,1,0:T(4,128)(2,1)}, u32[]{:S(2)}) copy-start(bf16[3,3,4096]{2,1,0:T(4,128)(2,1)} %sp_ref.1) | copy-start | bytes 221188
  40.4 2.9 %copy-start.8 = (f32[512]{0:T(512)S(1)}, f32[512]{0:T(512)}, u32[]{:S(2)}) copy-start(f32[512]{0:T(512)} %param.17) | copy-start | bytes 6148
  40.4 2.9 %copy-start.9 = (f32[512]{0:T(512)S(1)}, f32[512]{0:T(512)}, u32[]{:S(2)}) copy-start(f32[512]{0:T(512)} %param.21) | copy-start | bytes 6148
  40.4 2.8 %collective-permute-start.7 = (bf16[80,256]{1,0:T(8,128)(2,1)S(1)}, bf16[80,256]{1,0:T(8,128)(2,1)S(1)}, u32[]{:S(2)}, u32[]{:S(2)}) collective-permute-start(bf16[80,256]{1,0:T(8,128)(2,1)S(1)} %add_convert_fusion.mine_ref), channel_id=1, source_target_pairs={{0,1},{1,0},{2,3},{3,2},{4,5},{5,4},{6,7},{7,6},{8,9},{9,8},{10,11... | collective-permute-start | bytes 122888 | tf_op jit(solution)/shard_map/ppermute | solution.py:836

commit v5 on v4

v5 whole, which is shorter than its diff:
```python
import functools

import jax
import jax.numpy as jnp
from jax import lax
from jax.experimental import pallas as pl
from jax.experimental.pallas import tpu as pltpu
from jax.sharding import PartitionSpec as P


LANES = 128
BLOCK = 256
PAD = 8
REACH = 3
PIECE = 16
END_ROWS = 128
FINE = 4
SMALL_VMEM = 24 * 1024 * 1024
FEED_VMEM = 40 * 1024 * 1024
BF16 = jnp.bfloat16
F32 = jnp.float32


def lane_chunks(width=BLOCK):
    return [slice(low, low + LANES) for low in range(0, width, LANES)]


def depthwise_rows(streams, span, out_rows, pieces, emit, between=None):
    sums = [{} for _ in streams]
    for row_in in range(out_rows + span - 1):
        for side, (load, taps) in enumerate(streams):
            for piece in range(pieces):
                views = [load(row_in, b, piece * PIECE) for b in range(span)]
                for a in range(span):
                    row_out = row_in - a
                    if not 0 <= row_out < out_rows:
                        continue
                    part = views[0] * taps[a * span]
                    for b in range(1, span):
                        part = part + views[b] * taps[a * span + b]
                    key = (row_out, piece)
                    sums[side][key] = part if a == 0 else sums[side][key] + part
        done = row_in - span + 1
        if done >= 0:
            for piece in range(pieces):
                emit(done, piece * PIECE, *[s.pop((done, piece)) for s in sums])
        if between is not None:
            between()


def aligned(value, size):
    return value if isinstance(value, int) else pl.multiple_of(value, size)


def paced(tasks, slots):
    queue = list(tasks)
    state = [0]

    def between():
        state[0] += 1
        while queue and (len(tasks) - len(queue)) * slots < state[0] * len(tasks):
            queue.pop(0)()

    def flush():
        while queue:
            queue.pop(0)()

    return between, flush


def tap_list(weight_ref, lanes, rows):
    span = weight_ref.shape[0]
    return [
        jnp.broadcast_to(weight_ref[a, b : b + 1, lanes].astype(F32), (rows, LANES)).astype(BF16)
        for a in range(span)
        for b in range(span)
    ]


def head_mask(size, head):
    return (
        lax.broadcasted_iota(jnp.int32, (size, size), 0) // head
        == lax.broadcasted_iota(jnp.int32, (size, size), 1) // head
    )


def spread_blocks(group_ref):
    count, head, _ = group_ref.shape
    size = count * head
    rows = group_ref[...].reshape(size, head)
    pick = (
        lax.broadcasted_iota(jnp.int32, (head, size), 1) % head
        == lax.broadcasted_iota(jnp.int32, (head, size), 0)
    ).astype(BF16)
    wide = jnp.dot(rows, pick, preferred_element_type=F32)
    return jnp.where(head_mask(size, head), wide, 0.0).astype(BF16)


def fill_keep(keep_ref, out):
    rows, cols = keep_ref.shape
    cell = lax.broadcasted_iota(jnp.int32, (rows * cols, rows), 0)
    own_row = cell // cols == lax.broadcasted_iota(jnp.int32, (rows * cols, rows), 1)
    lines = jnp.dot(
        own_row.astype(BF16), keep_ref[...].astype(F32).astype(BF16), preferred_element_type=F32
    )
    cell = lax.broadcasted_iota(jnp.int32, (rows * cols, cols), 0)
    own_col = cell % cols == lax.broadcasted_iota(jnp.int32, (rows * cols, cols), 1)
    picked = jnp.where(own_col, lines, 0.0).astype(BF16)
    out[...] = jnp.dot(picked, jnp.ones((cols, LANES), BF16), preferred_element_type=F32).astype(
        BF16
    )


def summarise(keys, values, head):
    kv = lax.dot_general(
        keys[...], values[...], (((0,), (0,)), ((), ())), preferred_element_type=F32
    )
    lane_head = lax.broadcasted_iota(jnp.int32, (head, BLOCK), 1) // head
    packed = jnp.zeros((head, BLOCK), F32)
    for h in range(BLOCK // head):
        packed = packed + jnp.where(lane_head == h, kv[h * head : (h + 1) * head], 0.0)
    total = jnp.sum(keys[...].astype(F32), axis=0, keepdims=True)
    return packed, jnp.broadcast_to(total, (8, BLOCK))


def put_row(buf, stride, row, col, values):
    for ch, lanes in enumerate(lane_chunks()):
        start = PAD + (row + REACH) * stride + col
        buf[ch, pl.ds(start, values.shape[0]), :] = values[:, lanes]


def stack_halos(flags_ref, even_ref, odd_ref, sides, out):
    low = 0
    for ref in sides:
        out[low : low + ref.shape[0]] = ref[...]
        low += ref.shape[0]
    count = even_ref.shape[0]

    def ends(above_ref, below_ref):
        out[low : low + count] = above_ref[...]
        out[low + END_ROWS : low + END_ROWS + count] = below_ref[...]

    @pl.when(flags_ref[5] == 0)
    def _():
        ends(odd_ref, even_ref)

    @pl.when(flags_ref[5] != 0)
    def _():
        ends(even_ref, odd_ref)

    return low + 2 * END_ROWS


def fill_sides(tile, flags, count, p, buf):
    rows, cols = tile
    stride = cols + PAD
    for side, (col0, flag) in enumerate(((-REACH, flags[0]), (cols, flags[1]))):
        base = (side % count) * REACH * rows
        q = jnp.where(flag, p[base : base + REACH * rows], 0.0)
        for k in range(REACH):
            for ch, lanes in enumerate(lane_chunks()):
                start = PAD + REACH * stride + col0 + k
                buf[ch, pl.ds(start, rows, stride=stride), :] = q[k * rows : (k + 1) * rows, lanes]


def fill_ends(tile, flags, p, buf):
    rows, cols = tile
    stride = cols + PAD
    for end, row0 in enumerate((-REACH, rows)):
        for k in range(REACH):
            low = end * END_ROWS + k * stride
            put_row(buf, stride, row0 + k, 0, p[low : low + cols])
            tail = p[low + cols : low + stride]
            put_row(buf, stride, row0 + k, -REACH, jnp.where(flags[0], tail, 0.0)[0:REACH])
            put_row(
                buf, stride, row0 + k, cols, jnp.where(flags[1], tail, 0.0)[REACH : 2 * REACH]
            )


def conv_rows(buf, s_ref, cols, row_first, row_count, out, out_row, tasks=()):
    stride = cols + PAD
    between, flush = paced(tasks, (row_count + 4) * (BLOCK // LANES))
    for ch, lanes in enumerate(lane_chunks()):
        taps = tap_list(s_ref, lanes, PIECE)

        def load(row_in, b, at, ch=ch):
            start = PAD + (row_first + row_in - 2 + REACH) * stride + b - 2 + at
            return buf[ch, pl.ds(start, PIECE), :].astype(BF16)

        def emit(row, at, value, lanes=lanes):
            low = (out_row + row) * cols + at
            out[low : low + PIECE, lanes] = value

        depthwise_rows([(load, taps)], 5, row_count, cols // PIECE, emit, between)
    flush()


def keep_keys(values, keep):
    values = jnp.maximum(values, 0)
    return jnp.concatenate([values[:, lanes] * keep for lanes in lane_chunks()], axis=1)


def interior_kernel(tile, head, first, side_count, *refs):
    flags_ref, main_ref, keep_in_ref, *refs = refs
    sides, refs = refs[:side_count], refs[side_count:]
    wk_ref, wv_ref, sk_ref, sv_ref, gk_ref, gv_ref, part_ref, *refs = refs
    keep_ref = keep_in_ref
    if first:
        keep_ref, *refs = refs
        fill_keep(keep_in_ref, keep_ref)
    buf_k, buf_v, mat_k, mat_v, sp_k, sp_v, agg_k, agg_v, stack = refs
    rows, cols = tile
    stride = cols + PAD
    flags = (flags_ref[2] != 0, flags_ref[3] != 0)
    step = main_ref.shape[0] // 2
    for n, ref in enumerate(sides):
        stack[n * REACH * rows : (n + 1) * REACH * rows] = ref[...]

    def project_task(w_ref, buf, mat, is_key, start):
        p = jnp.dot(main_ref[start : start + step], w_ref[...], preferred_element_type=F32)
        for low in range(0, step, cols):
            put_row(buf, stride, (start + low) // cols, 0, p[low : low + cols])
        p = p.astype(BF16)
        if is_key:
            p = keep_keys(p, keep_ref[start : start + step])
        mat[start : start + step] = p

    def side_task(w_ref, buf):
        p = jnp.dot(stack[...], w_ref[...], preferred_element_type=F32)
        fill_sides(tile, flags, side_count, p, buf)

    def group_task(g_ref, spread, out, is_key, start, stop):
        blocks = spread_blocks(g_ref)
        agg = jnp.dot(spread[start:stop], blocks, preferred_element_type=F32).astype(BF16)
        if is_key:
            agg = keep_keys(agg, keep_ref[2 * cols + start : 2 * cols + stop])
        out[start:stop] = agg

    def stats_task(keys, values, row, total_row):
        packed, total = summarise(keys, values, head)
        part_ref[row : row + head] = packed
        part_ref[total_row : total_row + 8] = total

    half = sp_k.shape[0] // 2
    task = functools.partial
    project_task(wk_ref, buf_k, mat_k, True, 0)
    project_task(wk_ref, buf_k, mat_k, True, step)
    side_task(wk_ref, buf_k)
    conv_rows(
        buf_k,
        sk_ref,
        cols,
        2,
        rows - 4,
        sp_k,
        0,
        [
            task(project_task, wv_ref, buf_v, mat_v, False, 0),
            task(project_task, wv_ref, buf_v, mat_v, False, step),
            task(side_task, wv_ref, buf_v),
        ],
    )
    conv_rows(
        buf_v,
        sv_ref,
        cols,
        2,
        rows - 4,
        sp_v,
        0,
        [
            task(stats_task, mat_k, mat_v, 0, 2 * head),
            task(group_task, gk_ref, sp_k, agg_k, True, 0, half),
            task(group_task, gk_ref, sp_k, agg_k, True, half, 2 * half),
        ],
    )
    group_task(gv_ref, sp_v, agg_v, False, 0, half)
    group_task(gv_ref, sp_v, agg_v, False, half, 2 * half)
    stats_task(agg_k, agg_v, head, 2 * head + 8)


def border_kernel(tile, head, side_count, flags_ref, top_ref, bottom_ref, *refs):
    even_ref, odd_ref, *refs = refs
    sides, refs = refs[:side_count], refs[side_count:]
    keep_ref, part_a_ref, part_b_ref, *refs = refs
    wk_ref, wv_ref, sk_ref, sv_ref, gk_ref, gv_ref, mine_ref, sent_ref, *refs = refs
    buf_k, buf_v, sp_k, sp_v, agg_k, agg_v, stack = refs
    rows, cols = tile
    stride = cols + PAD
    flags = (flags_ref[2] != 0, flags_ref[3] != 0)
    edge = 4 * cols

    @pl.when(pl.program_id(0) == 0)
    def _():
        stack[0:edge] = top_ref[...]
        stack[edge : 2 * edge] = bottom_ref[...]
        stack_halos(flags_ref, even_ref, odd_ref, sides, stack.at[2 * edge :])

    side_rows = side_count * REACH * rows
    for w_ref, buf in ((wk_ref, buf_k), (wv_ref, buf_v)):
        p = jnp.dot(stack[...], w_ref[...], preferred_element_type=F32)
        for end, row0 in enumerate((0, rows - 4)):
            for k in range(4):
                low = end * edge + k * cols
                put_row(buf, stride, row0 + k, 0, p[low : low + cols])
        fill_sides(tile, flags, side_count, p[2 * edge : 2 * edge + side_rows], buf)
        fill_ends(tile, flags, p[2 * edge + side_rows :], buf)
    for s_ref, g_ref, buf, spread, out, is_key in (
        (sk_ref, gk_ref, buf_k, sp_k, agg_k, True),
        (sv_ref, gv_ref, buf_v, sp_v, agg_v, False),
    ):
        conv_rows(buf, s_ref, cols, 0, 2, spread, 0)
        conv_rows(buf, s_ref, cols, rows - 2, 2, spread, 2)
        agg = jnp.dot(spread[...], spread_blocks(g_ref), preferred_element_type=F32).astype(BF16)
        if is_key:
            keep = jnp.concatenate(
                [keep_ref[0 : 2 * cols], keep_ref[(rows - 2) * cols : rows * cols]], axis=0
            )
            agg = keep_keys(agg, keep)
        out[...] = agg
    packed, total = summarise(agg_k, agg_v, head)
    step = pl.program_id(0)
    part = jnp.where(step == 0, part_a_ref[...], part_b_ref[...])
    own = step == flags_ref[4]

    def store(out_ref):
        out_ref[0:head] = part[0:head].astype(BF16)
        out_ref[head : 2 * head] = (part[head : 2 * head] + packed).astype(BF16)
        low = 2 * head
        out_ref[low : low + 16] = jnp.concatenate(
            [part[low : low + 8], part[low + 8 : low + 16] + total], axis=0
        ).astype(BF16)

    @pl.when(own)
    def _():
        store(mine_ref)

    @pl.when(jnp.logical_not(own))
    def _():
        store(sent_ref)


def query_project_kernel(main_ref, w_ref, proj_ref):
    cells = main_ref.shape[0]
    step = 256
    w = w_ref[...]
    for start in range(0, cells, step):
        proj_ref[0, start : start + step] = jnp.dot(
            main_ref[start : start + step], w, preferred_element_type=F32
        ).astype(BF16)


def query_kernel(tile, side_count, flags_ref, proj_ref, even_ref, odd_ref, *refs):
    sides, refs = refs[:side_count], refs[side_count:]
    w_ref, s_ref, g_ref, edge_ref, q_ref, buf, spread, stack = refs
    rows, cols = tile
    stride = cols + PAD
    cells = rows * cols
    tall = rows + PAD
    flags = (flags_ref[2] != 0, flags_ref[3] != 0)
    stack_halos(flags_ref, even_ref, odd_ref, sides, stack)
    for row in range(rows):
        values = proj_ref[0, row * cols : (row + 1) * cols].astype(F32)
        put_row(buf, stride, row, 0, values)
    p = jnp.dot(stack[...], w_ref[...], preferred_element_type=F32)
    side_rows = side_count * REACH * rows
    fill_sides(tile, flags, side_count, p[0:side_rows], buf)
    fill_ends(tile, flags, p[side_rows:], buf)
    side0 = cells + 2 * cols

    def slot(row):
        if row < 0:
            return cells
        if row >= rows:
            return cells + cols
        return row * cols

    for ch, lanes in enumerate(lane_chunks()):
        for row in (-1, rows):
            start = PAD + (row + REACH) * stride
            value = buf[ch, pl.ds(start, cols), :].astype(BF16)
            low = slot(row) - cells
            edge_ref[low : low + cols, lanes] = jnp.maximum(value, 0)
        for side, col in enumerate((-1, cols)):
            start = PAD + (REACH - 1) * stride + col
            value = buf[ch, pl.ds(start, tall, stride=stride), :].astype(BF16)
            low = 2 * cols + side * tall
            edge_ref[low : low + tall, lanes] = jnp.maximum(value, 0)

        taps = tap_list(s_ref, lanes, PIECE)

        def load(row_in, b, at, ch=ch):
            start = PAD + row_in * stride + b - 2 + at
            return buf[ch, pl.ds(start, PIECE), :].astype(BF16)

        def emit(row, at, value, lanes=lanes):
            low = slot(row - 1) + at
            spread[low : low + PIECE, lanes] = value

        depthwise_rows([(load, taps)], 5, rows + 2, cols // PIECE, emit)
        taps = tap_list(s_ref, lanes, tall)
        for side, col in enumerate((-1, cols)):
            total = None
            for a in range(5):
                part = None
                for b in range(5):
                    start = PAD + a * stride + col + b - 2
                    view = buf[ch, pl.ds(start, tall, stride=stride), :].astype(BF16)
                    term = view * taps[a * 5 + b]
                    part = term if part is None else part + term
                total = part if total is None else total + part
            low = side0 + side * tall
            spread[low : low + tall, lanes] = total

    blocks = spread_blocks(g_ref)
    count = spread.shape[0]
    for start in range(0, count, 256):
        stop = min(count, start + 256)
        agg = jnp.dot(spread[start:stop], blocks, preferred_element_type=F32)
        q_ref[start:stop] = jnp.maximum(agg.astype(BF16), 0)


def rms_add(residual, branch, gain):
    scale = lax.rsqrt(jnp.mean(branch * branch, axis=-1, keepdims=True) + 1e-05)
    return residual.astype(F32) + branch * scale * gain


def feed_kernel(tile, head, side_count, flags_ref, main_any, even_ref, odd_ref, *refs):
    sides, refs = refs[:side_count], refs[side_count:]
    (
        proj_any,
        q_edge_a_ref,
        q_edge_b_ref,
        q_far_a_any,
        q_far_b_any,
        mine_ref,
        other_ref,
        wp_any,
        gain_a_ref,
        we_any,
        sp_ref,
        wr_any,
        gain_f_ref,
        out_any,
        main_ref,
        proj_ref,
        q_far_ref,
        wp_ref,
        we_ref,
        wr_ref,
        mid,
        half,
        att,
        edge,
        buf_av,
        buf_ag,
        buf_bv,
        buf_bg,
        gated,
        folded,
        reduced,
        result,
        sems,
    ) = refs
    rows, cols = tile
    stride = cols + PAD
    cells = rows * cols
    tall = rows + PAD
    blocks = proj_ref.shape[0]
    channels = main_ref.shape[1]
    hidden = wr_ref.shape[0]
    steps = hidden // BLOCK
    count = mid.shape[0]
    big = cells // 2
    bounds = [(0, big), (big, cells), (cells, count)]

    loads = [
        pltpu.make_async_copy(src, dst, sems.at[i])
        for i, (src, dst) in enumerate(
            (
                (proj_any, proj_ref),
                (q_far_a_any, q_far_ref.at[0]),
                (q_far_b_any, q_far_ref.at[1]),
                (wp_any, wp_ref),
                (main_any, main_ref),
                (we_any, we_ref),
                (wr_any, wr_ref),
            )
        )
    ]
    for load in loads:
        load.start()
    q_edges = (q_edge_a_ref, q_edge_b_ref)

    def ends(above_ref, below_ref):
        edge[0:cols] = above_ref[(REACH - 1) * stride : (REACH - 1) * stride + cols].astype(F32)
        edge[cols : 2 * cols] = below_ref[0:cols].astype(F32)
        top_tail = above_ref[(REACH - 1) * stride + cols : REACH * stride].astype(F32)
        low_tail = below_ref[cols:stride].astype(F32)
        for side, near in enumerate((REACH - 1, 0)):
            base = 2 * cols + side * tall
            pick = side * REACH + near
            edge[base : base + 1] = top_tail[pick : pick + 1]
            edge[base + 1 + rows : base + 2 + rows] = low_tail[pick : pick + 1]

    @pl.when(flags_ref[5] == 0)
    def _():
        ends(odd_ref, even_ref)

    @pl.when(flags_ref[5] != 0)
    def _():
        ends(even_ref, odd_ref)

    for side, near in enumerate((REACH - 1, 0)):
        ref = sides[side % len(sides)]
        base = 2 * cols + side * tall
        edge[base + 1 : base + 1 + rows] = ref[near * rows : (near + 1) * rows].astype(F32)
        edge[base + 2 + rows : base + tall] = jnp.zeros((tall - rows - 2, channels), F32)

    same = head_mask(BLOCK, head)
    eye = lax.broadcasted_iota(jnp.int32, (BLOCK, BLOCK), 0) == lax.broadcasted_iota(
        jnp.int32, (BLOCK, BLOCK), 1
    )
    loads[3].wait()
    sums_of = {}
    for scale in range(2):
        for blk in range(blocks):
            mine = flags_ref[4] == blk
            low = scale * head
            packed = jnp.where(
                mine,
                mine_ref[low : low + head].astype(F32),
                other_ref[low : low + head].astype(F32),
            )
            kv = jnp.where(same, jnp.concatenate([packed] * (BLOCK // head), axis=0), 0.0)
            both = jnp.where(
                mine,
                mine_ref[2 * head : 2 * head + 16].astype(F32),
                other_ref[2 * head : 2 * head + 16].astype(F32),
            )
            sums = both[8 * scale : 8 * scale + 1]
            diag = jnp.where(eye, jnp.broadcast_to(sums, (BLOCK, BLOCK)), 0.0)
            sums_of[scale, blk] = jnp.dot(
                diag.astype(BF16), same.astype(BF16), preferred_element_type=F32
            ).astype(BF16)
            low = scale * channels + blk * BLOCK
            folded[low : low + BLOCK] = jnp.dot(
                kv.astype(BF16), wp_ref[low : low + BLOCK], preferred_element_type=F32
            ).astype(BF16)

    def expand_task(j, part, buf, start, stop):
        w = we_ref[:, pl.ds(aligned(part * hidden + j * BLOCK, BLOCK), BLOCK)]
        p = jnp.dot(half[start:stop], w, preferred_element_type=F32)
        p = p * jnp.tanh(p) + p
        for ch, lanes in enumerate(lane_chunks()):

            def put(row, low):
                at = PAD + (row + 1) * stride
                buf[ch, pl.ds(at, cols), :] = p[low : low + cols, lanes]

            if start < cells:
                for low in range(0, stop - start, cols):
                    put((start + low) // cols, low)
            else:
                put(-1, 0)
                put(rows, cols)
                for side, col in enumerate((-1, cols)):
                    low = 2 * cols + side * tall
                    buf[ch, pl.ds(PAD + col, tall, stride=stride), :] = p[low : low + tall, lanes]

    def reduce_task(k, start, stop):
        width = 2 * BLOCK
        part = jnp.dot(
            gated[start:stop, k * width : (k + 1) * width],
            wr_ref[k * width : (k + 1) * width],
            preferred_element_type=F32,
        )
        reduced[start:stop] = part if k == 0 else reduced[start:stop] + part

    def mix(j, bufs, tasks):
        between, flush = paced(tasks, (rows + 2) * (BLOCK // LANES))
        for ch in range(BLOCK // LANES):
            col0 = aligned(j * BLOCK + ch * LANES, LANES)
            streams = []
            for part, buf in enumerate(bufs):

                def load(row_in, b, at, buf=buf, ch=ch):
                    start = PAD + row_in * stride + b - 1 + at
                    return buf[ch, pl.ds(start, PIECE), :].astype(BF16)

                at = aligned(part * hidden + col0, LANES)
                taps = tap_list(sp_ref, pl.ds(at, LANES), PIECE)
                if part:
                    taps = [t * jnp.asarray(0.5, BF16) for t in taps]
                streams.append((load, taps))

            def emit(row, at, value, gate, col0=col0):
                low = row * cols + at
                gated[low : low + PIECE, pl.ds(col0, LANES)] = value * (
                    gate * jnp.tanh(gate) + gate
                )

            depthwise_rows(streams, 3, rows, cols // PIECE, emit, between)
        flush()

    bufs = ((buf_av, buf_ag), (buf_bv, buf_bg))
    gain = gain_a_ref[...]
    for n, (start, stop) in enumerate(bounds):
        if n == 0:
            for load in loads[:3]:
                load.wait()
        for scale in range(2):
            for blk in range(blocks):
                if scale:
                    q = q_far_ref[blk, start:stop]
                elif start < cells:
                    q = jnp.maximum(proj_ref[blk, start:stop], 0)
                else:
                    q = q_edges[blk][...]
                den = jnp.dot(q, sums_of[scale, blk], preferred_element_type=F32)
                low = scale * channels + blk * BLOCK
                att[start:stop, low : low + BLOCK] = (q.astype(F32) / (den + 1.0)).astype(BF16)
        branch = jnp.dot(att[start:stop], folded[...], preferred_element_type=F32)
        if n == 0:
            loads[4].wait()
        if start < cells:
            value = rms_add(main_ref[start:stop], branch, gain)
        else:
            value = rms_add(edge[...], branch, gain)
            index = lax.broadcasted_iota(jnp.int32, (stop - start, 1), 0)
            side = index - 2 * cols
            place = lax.rem(side + tall, tall)
            in_rows = index < 2 * cols
            is_top = (index < cols) | (~in_rows & (place == 0))
            is_bottom = (in_rows & (index >= cols)) | (~in_rows & (place == rows + 1))
            is_left = ~in_rows & (side < tall)
            is_right = ~in_rows & (side >= tall)
            dead = (
                (is_top & (flags_ref[0] == 0))
                | (is_bottom & (flags_ref[1] == 0))
                | (is_left & (flags_ref[2] == 0))
                | (is_right & (flags_ref[3] == 0))
            )
            value = jnp.where(dead, 0.0, value)
        value = value.astype(BF16)
        mid[start:stop] = value
        half[start:stop] = value * jnp.asarray(0.5, BF16)
        if n == 0:
            loads[5].wait()
        for part, buf in enumerate(bufs[0]):
            expand_task(0, part, buf, start, stop)

    loads[6].wait()
    fine = cells // FINE
    fine_bounds = [(s, s + fine) for s in range(0, cells, fine)] + [(cells, count)]

    def expansions(j, buf_pair):
        return [
            functools.partial(expand_task, j, part, buf, start, stop)
            for part, buf in enumerate(buf_pair)
            for start, stop in fine_bounds
        ]

    def pair(i, carry):
        mix(2 * i, bufs[0], expansions(2 * i + 1, bufs[1]))
        mix(2 * i + 1, bufs[1], expansions(2 * i + 2, bufs[0]))
        return carry

    last = steps // 2 - 1
    lax.fori_loop(0, last, pair, 0)
    mix(2 * last, bufs[0], expansions(2 * last + 1, bufs[1]))
    mix(
        2 * last + 1,
        bufs[1],
        [functools.partial(reduce_task, k, *at) for k in range(last) for at in bounds[:2]],
    )

    gain = gain_f_ref[...]
    stores = []
    for n, (start, stop) in enumerate(bounds[:2]):
        reduce_task(steps // 2 - 1, start, stop)
        result[start:stop] = rms_add(mid[start:stop], reduced[start:stop], gain).astype(BF16)
        store = pltpu.make_async_copy(
            result.at[start:stop], out_any.at[start:stop], sems.at[len(loads) + n]
        )
        store.start()
        stores.append(store)
    for store in stores:
        store.wait()


def wide(canvas, left, right, low):
    channels = canvas.shape[2]

    def take(x, axis):
        return lax.dynamic_slice_in_dim(x, low, REACH, axis=axis)

    return jnp.concatenate(
        [
            take(canvas, 0),
            take(left, 1).transpose(1, 0, 2),
            take(right, 1).transpose(1, 0, 2),
            jnp.zeros((REACH, PAD - 2 * REACH, channels), canvas.dtype),
        ],
        axis=1,
    )


def swaps(axis, first):
    count = lax.axis_size(axis)
    pairs = []
    for i in range(first, count - 1, 2):
        pairs += [(i, i + 1), (i + 1, i)]
    return pairs


def neighbours(axis):
    count = lax.axis_size(axis)
    forward = [(i, i + 1) for i in range(count - 1)]
    return forward, [(b, a) for a, b in forward]


def total_over(x, axis):
    count = lax.axis_size(axis)
    if count & (count - 1):
        return lax.psum(x.astype(F32), axis).astype(BF16)
    step = 1
    while step < count:
        radix = 2
        total = x.astype(F32)
        for k in range(1, radix):
            pairs = [(i, i ^ (k * step)) for i in range(count)]
            total = total + lax.ppermute(x, axis, pairs).astype(F32)
        x = total.astype(BF16)
        step *= radix
    return x


def body(
    canvas,
    keep_mask,
    w_qkv,
    w_spread,
    w_group,
    w_proj,
    gain_attn,
    w_expand,
    w_spatial,
    w_reduce,
    gain_ff,
):
    rows, cols, channels = canvas.shape
    cells = rows * cols
    head = w_group.shape[1]
    hidden = w_reduce.shape[0]
    blocks = channels // BLOCK
    per = BLOCK // head
    tall = rows + PAD
    stride = cols + PAD
    tile = (rows, cols)
    flat_rows = PAD + (tall + 4) * stride
    flat_rows_ff = PAD + tall * stride

    main = canvas.reshape(cells, channels)

    def whole(shape):
        return pl.BlockSpec(shape, lambda *_: (0,) * len(shape))

    smem = pl.BlockSpec(memory_space=pltpu.SMEM)
    params = pltpu.CompilerParams(
        dimension_semantics=("arbitrary",), vmem_limit_bytes=SMALL_VMEM
    )

    def cost(macs, moved):
        return pl.CostEstimate(flops=2 * macs, bytes_accessed=moved, transcendentals=0)

    col_index = lax.axis_index("col")
    col_count = lax.axis_size("col")
    row_index = lax.axis_index("row")
    row_count = lax.axis_size("row")
    swap = [(0, 1), (1, 0)]
    paired = col_count == 2 and blocks == 2

    def strip(low):
        return canvas[:, low : low + REACH].transpose(1, 0, 2)

    if col_count == 2:
        low = jnp.where(col_index == 0, cols - REACH, 0)
        mine = lax.dynamic_slice_in_dim(canvas, low, REACH, axis=1).transpose(1, 0, 2)
        left = right = lax.ppermute(mine, "col", swap)
    else:
        right_way, left_way = neighbours("col")
        left = lax.ppermute(strip(cols - REACH), "col", right_way)
        right = lax.ppermute(strip(0), "col", left_way)

    flags = jnp.stack(
        [
            (row_index > 0).astype(jnp.int32),
            (row_index < row_count - 1).astype(jnp.int32),
            (col_index > 0).astype(jnp.int32),
            (col_index < col_count - 1).astype(jnp.int32),
            col_index.astype(jnp.int32) if paired else jnp.int32(0),
            (row_index % 2).astype(jnp.int32),
        ]
    )

    sides = [left.reshape(REACH * rows, channels)]
    if col_count != 2:
        sides.append(right.reshape(REACH * rows, channels))
    side_count = len(sides)
    side_rows = side_count * REACH * rows

    def cell_scratch(count, copies):
        return [pltpu.VMEM((count, BLOCK), BF16)] * copies

    flat_buf = pltpu.VMEM((BLOCK // LANES, flat_rows, LANES), F32)
    part_shape = (2 * head + 16, BLOCK)

    def interior(blk, keep_in):
        first = blk == 0
        out_specs = [whole(part_shape)]
        out_shape = [jax.ShapeDtypeStruct(part_shape, F32)]
        if first:
            out_specs.append(whole((cells, LANES)))
            out_shape.append(jax.ShapeDtypeStruct((cells, LANES), BF16))
        k_at, v_at = blocks + blk, 2 * blocks + blk
        return pl.pallas_call(
            functools.partial(interior_kernel, tile, head, first, side_count),
            grid=(1,),
            in_specs=[
                smem,
                whole(main.shape),
                whole(keep_in.shape),
                *[whole(side.shape) for side in sides],
                pl.BlockSpec((channels, BLOCK), lambda j: (0, k_at)),
                pl.BlockSpec((channels, BLOCK), lambda j: (0, v_at)),
                pl.BlockSpec((5, 5, BLOCK), lambda j: (0, 0, k_at)),
                pl.BlockSpec((5, 5, BLOCK), lambda j: (0, 0, v_at)),
                pl.BlockSpec((per, head, head), lambda j: (k_at, 0, 0)),
                pl.BlockSpec((per, head, head), lambda j: (v_at, 0, 0)),
            ],
            out_specs=out_specs,
            out_shape=out_shape,
            scratch_shapes=[
                flat_buf,
                flat_buf,
                *cell_scratch(cells, 2),
                *cell_scratch(cells - 4 * cols, 4),
                pltpu.VMEM((side_rows, channels), BF16),
            ],
            compiler_params=params,
            cost_estimate=cost(5 * cells * channels * channels, 4 * cells * channels),
        )(
            flags,
            main,
            keep_in,
            *sides,
            w_qkv,
            w_qkv,
            w_spread,
            w_spread,
            w_group,
            w_group,
        )

    parity = row_index % 2
    low_even = jnp.where(parity == 0, rows - REACH, 0)
    low_odd = jnp.where(parity == 0, 0, rows - REACH)
    even = lax.ppermute(wide(canvas, left, right, low_even), "row", swaps("row", 0))
    part_a, keep = interior(0, keep_mask)
    edges, part_a = lax.optimization_barrier((wide(canvas, left, right, low_odd), part_a))
    odd = lax.ppermute(edges, "row", swaps("row", 1))
    (part_b,) = interior(1, keep)
    even = even.reshape(REACH * stride, channels)
    odd = odd.reshape(REACH * stride, channels)
    project_queries = pl.pallas_call(
        query_project_kernel,
        grid=(blocks,),
        in_specs=[
            whole(main.shape),
            pl.BlockSpec((channels, BLOCK), lambda j: (0, j)),
        ],
        out_specs=pl.BlockSpec((1, cells, BLOCK), lambda j: (j, 0, 0)),
        out_shape=jax.ShapeDtypeStruct((blocks, cells, BLOCK), BF16),
        compiler_params=params,
        cost_estimate=cost(cells * channels * channels, 4 * cells * channels),
        name="query_project",
    )
    proj_q = project_queries(main, w_qkv)

    halos = (even, odd, *sides)
    halo_specs = [whole(h.shape) for h in halos]
    mine, sent = pl.pallas_call(
        functools.partial(border_kernel, tile, head, side_count),
        grid=(blocks,),
        in_specs=[
            smem,
            pl.BlockSpec((4 * cols, channels), lambda j: (0, 0)),
            pl.BlockSpec((4 * cols, channels), lambda j: (rows // 4 - 1, 0)),
            *halo_specs,
            whole(keep.shape),
            whole(part_shape),
            whole(part_shape),
            pl.BlockSpec((channels, BLOCK), lambda j: (0, blocks + j)),
            pl.BlockSpec((channels, BLOCK), lambda j: (0, 2 * blocks + j)),
            pl.BlockSpec((5, 5, BLOCK), lambda j: (0, 0, blocks + j)),
            pl.BlockSpec((5, 5, BLOCK), lambda j: (0, 0, 2 * blocks + j)),
            pl.BlockSpec((per, head, head), lambda j: (blocks + j, 0, 0)),
            pl.BlockSpec((per, head, head), lambda j: (2 * blocks + j, 0, 0)),
        ],
        out_specs=[whole(part_shape)] * 2,
        out_shape=[jax.ShapeDtypeStruct(part_shape, BF16)] * 2,
        scratch_shapes=[
            flat_buf,
            flat_buf,
            *cell_scratch(4 * cols, 4),
            pltpu.VMEM((8 * cols + side_rows + 2 * END_ROWS, channels), BF16),
        ],
        compiler_params=params,
        cost_estimate=cost(cells * channels * channels, 2 * cells * channels),
        name="border",
    )(
        flags,
        main,
        main,
        *halos,
        keep,
        part_a,
        part_b,
        w_qkv,
        w_qkv,
        w_spread,
        w_spread,
        w_group,
        w_group,
    )
    if paired:
        got = lax.ppermute(sent, "col", swap)
        mine = total_over((mine.astype(F32) + got.astype(F32)).astype(BF16), "row")
        other = lax.ppermute(mine, "col", swap)
    else:
        mine = total_over(total_over(mine, "col"), "row")
        other = total_over(total_over(sent, "col"), "row")

    count = cells + 2 * cols + 2 * tall
    far = []
    for blk in range(blocks):
        query = pl.pallas_call(
            functools.partial(query_kernel, tile, side_count),
            grid=(1,),
            in_specs=[
                smem,
                pl.BlockSpec((1, cells, BLOCK), lambda j, blk=blk: (blk, 0, 0)),
                *halo_specs,
                pl.BlockSpec((channels, BLOCK), lambda j, blk=blk: (0, blk)),
                pl.BlockSpec((5, 5, BLOCK), lambda j, blk=blk: (0, 0, blk)),
                pl.BlockSpec((per, head, head), lambda j, blk=blk: (blk, 0, 0)),
            ],
            out_specs=[whole((count - cells, BLOCK)), whole((count, BLOCK))],
            out_shape=[
                jax.ShapeDtypeStruct((count - cells, BLOCK), BF16),
                jax.ShapeDtypeStruct((count, BLOCK), BF16),
            ],
            scratch_shapes=[
                flat_buf,
                pltpu.VMEM((count, BLOCK), BF16),
                pltpu.VMEM((side_rows + 2 * END_ROWS, channels), BF16),
            ],
            compiler_params=params,
            cost_estimate=cost(3 * cells * channels * channels, 3 * cells * channels),
        )
        far.append(query(flags, proj_q, *halos, w_qkv, w_spread, w_group))

    hbm = pl.BlockSpec(memory_space=pl.ANY)
    vmem = pl.BlockSpec(memory_space=pltpu.VMEM)
    buf = pltpu.VMEM((BLOCK // LANES, flat_rows_ff, LANES), F32)
    decoded = pl.pallas_call(
        functools.partial(feed_kernel, tile, head, side_count),
        in_specs=[
            smem,
            hbm,
            *[vmem] * len(halos),
            hbm,
            vmem,
            vmem,
            hbm,
            hbm,
            vmem,
            vmem,
            hbm,
            vmem,
            hbm,
            vmem,
            hbm,
            vmem,
        ],
        out_specs=hbm,
        out_shape=jax.ShapeDtypeStruct(main.shape, BF16),
        scratch_shapes=[
            pltpu.VMEM(main.shape, BF16),
            pltpu.VMEM(proj_q.shape, BF16),
            pltpu.VMEM((blocks, count, BLOCK), BF16),
            pltpu.VMEM(w_proj.shape, BF16),
            pltpu.VMEM(w_expand.shape, BF16),
            pltpu.VMEM(w_reduce.shape, BF16),
            pltpu.VMEM((count, channels), BF16),
            pltpu.VMEM((count, channels), BF16),
            pltpu.VMEM((count, 2 * channels), BF16),
            pltpu.VMEM((count - cells, channels), F32),
            buf,
            buf,
            buf,
            buf,
            pltpu.VMEM((cells, hidden), BF16),
            pltpu.VMEM(w_proj.shape, BF16),
            pltpu.VMEM(main.shape, F32),
            pltpu.VMEM(main.shape, BF16),
            pltpu.SemaphoreType.DMA((9,)),
        ],
        compiler_params=pltpu.CompilerParams(vmem_limit_bytes=FEED_VMEM),
        name="feed",
    )(
        flags,
        main,
        *halos,
        proj_q,
        far[0][0],
        far[1][0],
        far[0][1],
        far[1][1],
        mine,
        other,
        w_proj,
        gain_attn.reshape(1, channels),
        w_expand,
        w_spatial,
        w_reduce,
        gain_ff.reshape(1, channels),
    )
    return decoded.reshape(rows, cols, channels)


def solution(mesh):
    tile = P(("groups", "row"), "col", None)
    return jax.shard_map(
        body,
        mesh=mesh,
        in_specs=(tile, P(("groups", "row"), "col")) + (P(),) * 9,
        out_specs=tile,
        check_vma=False,
    )
```

time: 66.4 us -> 63.5 us (0.956)
  waiting for transfers between devices: 6.56 us -> 4.06 us
  Pallas kernels: 40.5 us -> 38.8 us
  starting transfers between devices: 13.2 us -> 14.5 us
    ppermute x3, starting transfers between devices: 6.79 us -> 10.4 us  [total_over(): total = total + lax.ppermute(x, axis, pairs).astype(F32)]
    ppermute x2, starting transfers between devices: 5.72 us -> 3.28 us  [the longest x1 2.61 us: body(): lax.ppermute(wide(canvas, left, right, low_even), 'row', swaps('row', 0))]
    ppermute x2, waiting for transfers between devices: 1.89 us -> 0.01 us  [the longest x1 0.01 us: body(): odd = lax.ppermute(edges, 'row', swaps('row', 1))]
    pallas_call x7, Pallas kernels: 40.5 us -> 38.8 us  [the longest x1 20.9 us: body(): pl.pallas_call(functools.partial(feed_kernel, tile, head, side_count), in...]
    dynamic_slice x0 -> x1, local copies, waits for them, and re-layouts: none -> 0.96 us  [take(): return lax.dynamic_slice_in_dim(x, low, REACH, axis=axis)]
    slice x1 -> x0, local copies, waits for them, and re-layouts: 0.95 us -> none  [wide(): canvas[low:low + REACH]]
    unnamed x23 -> x21, local copies, waits for them, and re-layouts: 2.83 us -> 3.01 us
  transfers between devices with their start and end apart: 8 -> 8, of which waited for: 4 -> 3; matrix products, arithmetic and copies ran while one was open for 4% -> 4% of each run, Pallas kernels for 22% -> 23%
where the time goes in v5:
time: 63.5 us; the launch traced here: 63.3 us
  Pallas kernels  38.8 us (61%)
  starting transfers between devices  14.5 us (23%)
  local copies, waits for them, and re-layouts  5.29 us (8%)
  waiting for transfers between devices  4.06 us (6%)
    pallas_call x1, Pallas kernels, body(): pl.pallas_call(functools.partial(feed_kernel, tile, head, side_count), in...  20.9 us
    ppermute x3, starting transfers between devices, total_over(): total = total + lax.ppermute(x, axis, pairs).astype(F32)  10.4 us
    pallas_call x2, Pallas kernels, interior(): pl.pallas_call(functools.partial(interior_kernel, tile, head, first, side...  7.92 us
    pallas_call x2, Pallas kernels, body(): far.append(query(flags, proj_q, *halos, w_qkv, w_spread, w_group))  5.69 us
    pallas_call x1, Pallas kernels, body(): pl.pallas_call(functools.partial(border_kernel, tile, head, side_count),...  3.4 us
    ppermute x3, waiting for transfers between devices, total_over(): total = total + lax.ppermute(x, axis, pairs).astype(F32)  3.01 us
    unnamed x21, local copies, waits for them, and re-layouts  3.01 us
    ppermute x1, starting transfers between devices, body(): lax.ppermute(wide(canvas, left, right, low_even), 'row', swaps('row', 0))  2.61 us
  transfers between devices with their start and end apart: 8, of which 3 were waited for; matrix products, arithmetic and copies ran while one was open for 4% of the time, Pallas kernels for 23%

profile of v5, /device:TPU:0, one launch (start us, length us, event | category | flops | bytes accessed | tf_op | source)
XLA Modules:
  0.0 63.3 jit_solution(7770395836824673390)
XLA Ops:
  0.0 1.1 %dynamic-slice_bitcast_fusion = bf16[3,32,512]{2,0,1:T(4,128)(2,1)S(1)} fusion(bf16[32,32,512]{2,1,0:T(8,128)(2,1)} %param.11, s32[]{:T(128)S(6)} %select_n.28), kind=kLoop, calls=%fused_computation | loop fusion | bytes 196612 | tf_op jit(solution)/shard_map/transpose | solution.py:789
  1.1 0.6 collective-permute-start
  1.7 1.6 %copy.13.refs_8_.refs_9_.refs_3_.refs_10_.refs_11_ = bf16[48,32,32]{2,1,0:T(8,128)(2,1)S(1)} copy(bf16[48,32,32]{0,2,1:T(8,128)(2,1)} %param.15) | data formatting | bytes 196608 | tf_op args[4]
  3.3 0.1 pad.7.clone
  3.4 0.1 stack.43.refs_0_.flags_ref
  3.4 1.0 %constant_dynamic-slice_fusion = (bf16[3,32,512]{2,1,0:T(8,128)(2,1)S(1)}, bf16[3,32,512]{2,1,0:T(8,128)(2,1)S(1)}) fusion(bf16[32,32,512]{2,1,0:T(8,128)(2,1)} %param.11, s32[]{:T(128)S(6)} %select_n.29, s32[]{:T(128)S(6)} %select_n.27), kind=kLoop, calls=%fused_computation.9 | loop fusion | bytes 393224 | tf_op jit(solution)/shard_map/dynamic_slice | solution.py:696
  4.4 0.1 maximum_maximum_fusion.1
  4.5 2.6 %collective-permute-start.1 = (bf16[3,40,512]{2,1,0:T(8,128)(2,1)S(1)}, bf16[3,40,512]{2,1,0:T(8,128)(2,1)S(1)}, u32[]{:S(2)}, u32[]{:S(2)}) collective-permute-start(bf16[3,40,512]{2,1,0:T(8,128)(2,1)S(1)} %get-tuple-element.30), channel_id=1, source_target_pairs={{0,2},{2,0},{4,6},{6,4},{8,10},{10,8},{12,14},{14,12},{1,3},{3,1},... | collective-permute-start | bytes 368648 | tf_op jit(solution)/shard_map/ppermute | solution.py:869
  7.2 1.4 %copy-done.1 = bf16[512,1536]{1,0:T(8,128)(2,1)S(1)} copy-done((bf16[512,1536]{1,0:T(8,128)(2,1)S(1)}, bf16[512,1536]{1,0:T(8,128)(2,1)}, u32[]{:S(2)}) %copy-start.1) | copy-done | bytes 1572888
  8.6 4.0 %shard_map.109 = (f32[80,256]{1,0:T(8,128)S(1)}, bf16[1024,128]{1,0:T(8,128)(2,1)S(1)}) custom-call(s32[6]{0:T(128)S(1)} %stack.43.refs_0_.flags_ref, bf16[1024,512]{1,0:T(8,128)(2,1)S(1)} %bitcast.19, s32[32,32]{1,0:T(8,128)S(1)} %copy-done.9, bf16[96,512]{1,0:T(8,128)(2,1)S(1)} %bitcast.25, bf16[512,1536]{1,0:T(8,128)(2,1)S(1)} %copy-done.1, ...), custom_call_target="tpu_custom_call" | custom-call | flops 2684354560 | bytes 2097152 | tf_op jit(solution)/shard_map/pallas_call | solution.py:827
  12.6 0.7 %collective-permute-start.2 = (bf16[3,40,512]{2,1,0:T(8,128)(2,1)S(1)}, bf16[3,40,512]{2,1,0:T(8,128)(2,1)S(1)}, u32[]{:S(2)}, u32[]{:S(2)}) collective-permute-start(bf16[3,40,512]{2,1,0:T(8,128)(2,1)S(1)} %get-tuple-element.16), channel_id=1, source_target_pairs={{2,4},{4,2},{6,8},{8,6},{10,12},{12,10},{3,5},{5,3},{7,9},{9,7},{1... | collective-permute-start | bytes 368648 | tf_op jit(solution)/shard_map/ppermute | solution.py:872
  13.3 3.9 %shard_map.112.refs_5_ = f32[80,256]{1,0:T(8,128)S(1)} custom-call(s32[6]{0:T(128)S(1)} %stack.43.refs_0_.flags_ref, bf16[1024,512]{1,0:T(8,128)(2,1)S(1)} %bitcast.20, bf16[1024,128]{1,0:T(8,128)(2,1)S(1)} %get-tuple-element.21.refs_2_.refs_3_, bf16[96,512]{1,0:T(8,128)(2,1)S(1)} %bitcast.26, bf16[512,1536]{1,0:T(8,128)(2,1)S(1)} %copy-done.1, ...), custom_call_target="tpu_custom_call" | custom-call | flops 2684354560 | bytes 2097152 | tf_op jit(solution)/shard_map/pallas_call | solution.py:827
  17.3 3.4 %border.1 = (bf16[80,256]{1,0:T(8,128)(2,1)S(1)}, bf16[80,256]{1,0:T(8,128)(2,1)S(1)}) custom-call(s32[6]{0:T(128)S(1)} %stack.43.refs_0_.flags_ref, bf16[1024,512]{1,0:T(8,128)(2,1)S(1)} %bitcast.21, bf16[1024,512]{1,0:T(8,128)(2,1)S(1)} %bitcast.22, bf16[120,512]{1,0:T(8,128)(2,1)S(1)} %bitcast.31, bf16[120,512]{1,0:T(8,128)(2,1)S(1)} %bitcast.35, ...), custom_call_target="tpu_custom_call" | custom-call | flops 536870912 | bytes 1048576 | tf_op jit(solution)/shard_map/border/pallas_call | solution.py:893
  20.7 0.2 collective-permute-start.3
  20.9 1.0 %collective-permute-done.3 = bf16[80,256]{1,0:T(8,128)(2,1)S(1)} collective-permute-done((bf16[80,256]{1,0:T(8,128)(2,1)S(1)}, bf16[80,256]{1,0:T(8,128)(2,1)S(1)}, u32[]{:S(2)}, u32[]{:S(2)}) %collective-permute-start.3) | collective-permute-done | bytes 40992 | tf_op jit(solution)/shard_map/ppermute | solution.py:938
  22.0 4.4 %collective-permute-start.4 = (bf16[80,256]{1,0:T(8,128)(2,1)S(1)}, bf16[80,256]{1,0:T(8,128)(2,1)S(1)}, u32[]{:S(2)}, u32[]{:S(2)}) collective-permute-start(bf16[80,256]{1,0:T(8,128)(2,1)S(1)} %add_convert_fusion.3), channel_id=1, source_target_pairs={{0,2},{2,0},{4,6},{6,4},{8,10},{10,8},{12,14},{14,12},{1,3},{3,1},... | collective-permute-start | bytes 122888 | tf_op jit(solution)/shard_map/ppermute | solution.py:733
  26.3 2.0 %collective-permute-done.4 = bf16[80,256]{1,0:T(8,128)(2,1)S(1)} collective-permute-done((bf16[80,256]{1,0:T(8,128)(2,1)S(1)}, bf16[80,256]{1,0:T(8,128)(2,1)S(1)}, u32[]{:S(2)}, u32[]{:S(2)}) %collective-permute-start.4) | collective-permute-done | bytes 40992 | tf_op jit(solution)/shard_map/ppermute | solution.py:733
  28.3 2.9 %collective-permute-start.5 = (bf16[80,256]{1,0:T(8,128)(2,1)S(1)}, bf16[80,256]{1,0:T(8,128)(2,1)S(1)}, u32[]{:S(2)}, u32[]{:S(2)}) collective-permute-start(bf16[80,256]{1,0:T(8,128)(2,1)S(1)} %add_convert_fusion.2), channel_id=1, source_target_pairs={{0,4},{2,6},{4,0},{6,2},{8,12},{10,14},{12,8},{14,10},{1,5},{3,7},... | collective-permute-start | bytes 122888 | tf_op jit(solution)/shard_map/ppermute | solution.py:733
  31.2 0.9 %query_project.1.proj_ref.refs_1_ = bf16[2,1024,256]{2,1,0:T(8,128)(2,1)S(1)} custom-call(bf16[1024,512]{1,0:T(8,128)(2,1)S(1)} %bitcast.23, bf16[512,1536]{1,0:T(8,128)(2,1)S(1)} %copy-done.1), custom_call_target="tpu_custom_call" | custom-call | flops 536870912 | bytes 2097152 | tf_op jit(solution)/shard_map/query_project/pallas_call | solution.py:889
  32.2 1.0 %collective-permute-done.5 = bf16[80,256]{1,0:T(8,128)(2,1)S(1)} collective-permute-done((bf16[80,256]{1,0:T(8,128)(2,1)S(1)}, bf16[80,256]{1,0:T(8,128)(2,1)S(1)}, u32[]{:S(2)}, u32[]{:S(2)}) %collective-permute-start.5) | collective-permute-done | bytes 40992 | tf_op jit(solution)/shard_map/ppermute | solution.py:733
  33.2 3.1 %collective-permute-start.6 = (bf16[80,256]{1,0:T(8,128)(2,1)S(1)}, bf16[80,256]{1,0:T(8,128)(2,1)S(1)}, u32[]{:S(2)}, u32[]{:S(2)}) collective-permute-start(bf16[80,256]{1,0:T(8,128)(2,1)S(1)} %add_convert_fusion.1), channel_id=1, source_target_pairs={{0,8},{2,10},{4,12},{6,14},{8,0},{10,2},{12,4},{14,6},{1,9},{3,11}... | collective-permute-start | bytes 122888 | tf_op jit(solution)/shard_map/ppermute | solution.py:733
  36.3 2.8 %shard_map.111 = (bf16[144,256]{1,0:T(8,128)(2,1)S(1)}, bf16[1168,256]{1,0:T(8,128)(2,1)S(1)}) custom-call(s32[6]{0:T(128)S(1)} %stack.43.refs_0_.flags_ref, bf16[2,1024,256]{2,1,0:T(8,128)(2,1)S(1)} %query_project.1.proj_ref.refs_1_, bf16[120,512]{1,0:T(8,128)(2,1)S(1)} %bitcast.32, bf16[120,512]{1,0:T(8,128)(2,1)S(1)} %bitcast.36, ...), custom_call_target="tpu_custom_call" | custom-call | flops 1610612736 | bytes 1572864 | tf_op jit(solution)/shard_map/pallas_call | solution.py:972
  39.3 2.9 %shard_map.110 = (bf16[144,256]{1,0:T(8,128)(2,1)S(1)}, bf16[1168,256]{1,0:T(8,128)(2,1)S(1)}) custom-call(s32[6]{0:T(128)S(1)} %stack.43.refs_0_.flags_ref, bf16[2,1024,256]{2,1,0:T(8,128)(2,1)S(1)} %query_project.1.proj_ref.refs_1_, bf16[120,512]{1,0:T(8,128)(2,1)S(1)} %bitcast.33, bf16[120,512]{1,0:T(8,128)(2,1)S(1)} %bitcast.37, ...), custom_call_target="tpu_custom_call" | custom-call | flops 1610612736 | bytes 1572864 | tf_op jit(solution)/shard_map/pallas_call | solution.py:972
  42.3 20.9 %feed.1 = bf16[1024,512]{1,0:T(8,128)(2,1)} custom-call(s32[6]{0:T(128)S(1)} %stack.43.refs_0_.flags_ref, bf16[1024,512]{1,0:T(8,128)(2,1)S(1)} %bitcast.24, bf16[120,512]{1,0:T(8,128)(2,1)S(1)} %bitcast.34, bf16[120,512]{1,0:T(8,128)(2,1)S(1)} %bitcast.38, bf16[96,512]{1,0:T(8,128)(2,1)S(1)} %bitcast.30, ...), custom_call_target="tpu_custom_call" | custom-call | tf_op jit(solution)/shard_map/feed/pallas_call | solution.py:977
  (32 shorter events, 0.2 us)
Async XLA Ops:
  0.0 7.2 %copy-start = (bf16[32,32,512]{2,1,0:T(8,128)(2,1)S(1)}, bf16[32,32,512]{2,1,0:T(8,128)(2,1)}, u32[]{:S(2)}) copy-start(bf16[32,32,512]{2,1,0:T(8,128)(2,1)} %param.11) | copy-start | bytes 3145732
  0.0 7.2 %copy-start.5 = (bf16[5,5,1536]{2,1,0:T(8,128)(2,1)S(1)}, bf16[5,5,1536]{2,1,0:T(8,128)(2,1)}, u32[]{:S(2)}) copy-start(bf16[5,5,1536]{2,1,0:T(8,128)(2,1)} %refs_9_.3) | copy-start | bytes 230404
  0.0 7.2 %copy-start.9 = (s32[32,32]{1,0:T(8,128)S(1)}, s32[32,32]{1,0:T(8,128)}, u32[]{:S(2)}) copy-start(s32[32,32]{1,0:T(8,128)} %refs_2_.3) | copy-start | bytes 12292
  1.1 3.3 %collective-permute-start = (bf16[3,32,512]{2,0,1:T(4,128)(2,1)S(1)}, bf16[3,32,512]{2,0,1:T(4,128)(2,1)S(1)}, u32[]{:S(2)}, u32[]{:S(2)}) collective-permute-start(bf16[3,32,512]{2,0,1:T(4,128)(2,1)S(1)} %dynamic-slice_bitcast_fusion), channel_id=1, source_target_pairs={{0,1},{1,0},{2,3},{3,2},{4,5},{5,4},{6,7},{7,6},{8,9},{9,8},{10,11... | collective-permute-start | bytes 294920 | tf_op jit(solution)/shard_map/ppermute | solution.py:790
  4.5 12.7 %collective-permute-start.1 = (bf16[3,40,512]{2,1,0:T(8,128)(2,1)S(1)}, bf16[3,40,512]{2,1,0:T(8,128)(2,1)S(1)}, u32[]{:S(2)}, u32[]{:S(2)}) collective-permute-start(bf16[3,40,512]{2,1,0:T(8,128)(2,1)S(1)} %get-tuple-element.30), channel_id=1, source_target_pairs={{0,2},{2,0},{4,6},{6,4},{8,10},{10,8},{12,14},{14,12},{1,3},{3,1},... | collective-permute-start | bytes 368648 | tf_op jit(solution)/shard_map/ppermute | solution.py:869
  7.2 1.4 %copy-start.1 = (bf16[512,1536]{1,0:T(8,128)(2,1)S(1)}, bf16[512,1536]{1,0:T(8,128)(2,1)}, u32[]{:S(2)}) copy-start(bf16[512,1536]{1,0:T(8,128)(2,1)} %refs_7_.5) | copy-start | bytes 4718596
  12.6 4.6 %collective-permute-start.2 = (bf16[3,40,512]{2,1,0:T(8,128)(2,1)S(1)}, bf16[3,40,512]{2,1,0:T(8,128)(2,1)S(1)}, u32[]{:S(2)}, u32[]{:S(2)}) collective-permute-start(bf16[3,40,512]{2,1,0:T(8,128)(2,1)S(1)} %get-tuple-element.16), channel_id=1, source_target_pairs={{2,4},{4,2},{6,8},{8,6},{10,12},{12,10},{3,5},{5,3},{7,9},{9,7},{1... | collective-permute-start | bytes 368648 | tf_op jit(solution)/shard_map/ppermute | solution.py:872
  20.7 1.3 %collective-permute-start.3 = (bf16[80,256]{1,0:T(8,128)(2,1)S(1)}, bf16[80,256]{1,0:T(8,128)(2,1)S(1)}, u32[]{:S(2)}, u32[]{:S(2)}) collective-permute-start(bf16[80,256]{1,0:T(8,128)(2,1)S(1)} %get-tuple-element.24), channel_id=1, source_target_pairs={{0,1},{1,0},{2,3},{3,2},{4,5},{5,4},{6,7},{7,6},{8,9},{9,8},{10,11... | collective-permute-start | bytes 122888 | tf_op jit(solution)/shard_map/ppermute | solution.py:938
  22.0 6.3 %collective-permute-start.4 = (bf16[80,256]{1,0:T(8,128)(2,1)S(1)}, bf16[80,256]{1,0:T(8,128)(2,1)S(1)}, u32[]{:S(2)}, u32[]{:S(2)}) collective-permute-start(bf16[80,256]{1,0:T(8,128)(2,1)S(1)} %add_convert_fusion.3), channel_id=1, source_target_pairs={{0,2},{2,0},{4,6},{6,4},{8,10},{10,8},{12,14},{14,12},{1,3},{3,1},... | collective-permute-start | bytes 122888 | tf_op jit(solution)/shard_map/ppermute | solution.py:733
  28.3 4.9 %collective-permute-start.5 = (bf16[80,256]{1,0:T(8,128)(2,1)S(1)}, bf16[80,256]{1,0:T(8,128)(2,1)S(1)}, u32[]{:S(2)}, u32[]{:S(2)}) collective-permute-start(bf16[80,256]{1,0:T(8,128)(2,1)S(1)} %add_convert_fusion.2), channel_id=1, source_target_pairs={{0,4},{2,6},{4,0},{6,2},{8,12},{10,14},{12,8},{14,10},{1,5},{3,7},... | collective-permute-start | bytes 122888 | tf_op jit(solution)/shard_map/ppermute | solution.py:733
  33.2 5.9 %collective-permute-start.6 = (bf16[80,256]{1,0:T(8,128)(2,1)S(1)}, bf16[80,256]{1,0:T(8,128)(2,1)S(1)}, u32[]{:S(2)}, u32[]{:S(2)}) collective-permute-start(bf16[80,256]{1,0:T(8,128)(2,1)S(1)} %add_convert_fusion.1), channel_id=1, source_target_pairs={{0,8},{2,10},{4,12},{6,14},{8,0},{10,2},{12,4},{14,6},{1,9},{3,11}... | collective-permute-start | bytes 122888 | tf_op jit(solution)/shard_map/ppermute | solution.py:733
  36.3 5.9 %copy-start.3 = (bf16[2048,512]{1,0:T(8,128)(2,1)S(1)}, bf16[2048,512]{1,0:T(8,128)(2,1)}, u32[]{:S(2)}) copy-start(bf16[2048,512]{1,0:T(8,128)(2,1)} %refs_12_.1) | copy-start | bytes 6291460
  39.1 3.1 %copy-start.2 = (bf16[512,4096]{1,0:T(8,128)(2,1)S(1)}, bf16[512,4096]{1,0:T(8,128)(2,1)}, u32[]{:S(2)}) copy-start(bf16[512,4096]{1,0:T(8,128)(2,1)} %refs_10_.2) | copy-start | bytes 12582916
  39.1 3.1 %copy-start.4 = (bf16[1024,512]{1,0:T(8,128)(2,1)S(1)}, bf16[1024,512]{1,0:T(8,128)(2,1)}, u32[]{:S(2)}) copy-start(bf16[1024,512]{1,0:T(8,128)(2,1)} %refs_8_.5) | copy-start | bytes 3145732
  39.1 3.1 %copy-start.6 = (bf16[3,3,4096]{2,1,0:T(4,128)(2,1)S(1)}, bf16[3,3,4096]{2,1,0:T(4,128)(2,1)}, u32[]{:S(2)}) copy-start(bf16[3,3,4096]{2,1,0:T(4,128)(2,1)} %refs_11_.2) | copy-start | bytes 221188
  39.2 3.1 %copy-start.7 = (f32[512]{0:T(512)S(1)}, f32[512]{0:T(512)}, u32[]{:S(2)}) copy-start(f32[512]{0:T(512)} %param.17) | copy-start | bytes 6148
  39.2 3.1 %copy-start.8 = (f32[512]{0:T(512)S(1)}, f32[512]{0:T(512)}, u32[]{:S(2)}) copy-start(f32[512]{0:T(512)} %param.21) | copy-start | bytes 6148
  39.2 3.0 %collective-permute-start.7 = (bf16[80,256]{1,0:T(8,128)(2,1)S(1)}, bf16[80,256]{1,0:T(8,128)(2,1)S(1)}, u32[]{:S(2)}, u32[]{:S(2)}) collective-permute-start(bf16[80,256]{1,0:T(8,128)(2,1)S(1)} %add_convert_fusion.refs_6_), channel_id=1, source_target_pairs={{0,1},{1,0},{2,3},{3,2},{4,5},{5,4},{6,7},{7,6},{8,9},{9,8},{10,11... | collective-permute-start | bytes 122888 | tf_op jit(solution)/shard_map/ppermute | solution.py:940

commit v6 on v5

--- a/solution.py
+++ b/solution.py
@@ -15,6 +15,7 @@
 PIECE = 16
 END_ROWS = 128
 FINE = 4
+SPLIT = 8
 SMALL_VMEM = 24 * 1024 * 1024
 FEED_VMEM = 40 * 1024 * 1024
 BF16 = jnp.bfloat16
@@ -140,11 +141,11 @@
         out[low : low + count] = above_ref[...]
         out[low + END_ROWS : low + END_ROWS + count] = below_ref[...]
 
-    @pl.when(flags_ref[5] == 0)
+    @pl.when(flags_ref[4] == 0)
     def _():
         ends(odd_ref, even_ref)
 
-    @pl.when(flags_ref[5] != 0)
+    @pl.when(flags_ref[4] != 0)
     def _():
         ends(even_ref, odd_ref)
 
@@ -212,7 +213,7 @@
     rows, cols = tile
     stride = cols + PAD
     flags = (flags_ref[2] != 0, flags_ref[3] != 0)
-    step = main_ref.shape[0] // 2
+    step = main_ref.shape[0] // SPLIT
     for n, ref in enumerate(sides):
         stack[n * REACH * rows : (n + 1) * REACH * rows] = ref[...]
 
@@ -243,8 +244,9 @@
 
     half = sp_k.shape[0] // 2
     task = functools.partial
-    project_task(wk_ref, buf_k, mat_k, True, 0)
-    project_task(wk_ref, buf_k, mat_k, True, step)
+    starts = range(0, main_ref.shape[0], step)
+    for start in starts:
+        project_task(wk_ref, buf_k, mat_k, True, start)
     side_task(wk_ref, buf_k)
     conv_rows(
         buf_k,
@@ -255,8 +257,7 @@
         sp_k,
         0,
         [
-            task(project_task, wv_ref, buf_v, mat_v, False, 0),
-            task(project_task, wv_ref, buf_v, mat_v, False, step),
+            *[task(project_task, wv_ref, buf_v, mat_v, False, start) for start in starts],
             task(side_task, wv_ref, buf_v),
         ],
     )
@@ -283,7 +284,7 @@
     even_ref, odd_ref, *refs = refs
     sides, refs = refs[:side_count], refs[side_count:]
     keep_ref, part_a_ref, part_b_ref, *refs = refs
-    wk_ref, wv_ref, sk_ref, sv_ref, gk_ref, gv_ref, mine_ref, sent_ref, *refs = refs
+    wk_ref, wv_ref, sk_ref, sv_ref, gk_ref, gv_ref, out_ref, *refs = refs
     buf_k, buf_v, sp_k, sp_v, agg_k, agg_v, stack = refs
     rows, cols = tile
     stride = cols + PAD
@@ -321,23 +322,12 @@
     packed, total = summarise(agg_k, agg_v, head)
     step = pl.program_id(0)
     part = jnp.where(step == 0, part_a_ref[...], part_b_ref[...])
-    own = step == flags_ref[4]
-
-    def store(out_ref):
-        out_ref[0:head] = part[0:head].astype(BF16)
-        out_ref[head : 2 * head] = (part[head : 2 * head] + packed).astype(BF16)
-        low = 2 * head
-        out_ref[low : low + 16] = jnp.concatenate(
-            [part[low : low + 8], part[low + 8 : low + 16] + total], axis=0
-        ).astype(BF16)
-
-    @pl.when(own)
-    def _():
-        store(mine_ref)
-
-    @pl.when(jnp.logical_not(own))
-    def _():
-        store(sent_ref)
+    out_ref[0:head] = part[0:head].astype(BF16)
+    out_ref[head : 2 * head] = (part[head : 2 * head] + packed).astype(BF16)
+    low = 2 * head
+    out_ref[low : low + 16] = jnp.concatenate(
+        [part[low : low + 8], part[low + 8 : low + 16] + total], axis=0
+    ).astype(BF16)
 
 
 def query_project_kernel(main_ref, w_ref, proj_ref):
@@ -433,8 +423,7 @@
         q_edge_b_ref,
         q_far_a_any,
         q_far_b_any,
-        mine_ref,
-        other_ref,
+        stats_ref,
         wp_any,
         gain_a_ref,
         we_any,
@@ -503,11 +492,11 @@
             edge[base : base + 1] = top_tail[pick : pick + 1]
             edge[base + 1 + rows : base + 2 + rows] = low_tail[pick : pick + 1]
 
-    @pl.when(flags_ref[5] == 0)
+    @pl.when(flags_ref[4] == 0)
     def _():
         ends(odd_ref, even_ref)
 
-    @pl.when(flags_ref[5] != 0)
+    @pl.when(flags_ref[4] != 0)
     def _():
         ends(even_ref, odd_ref)
 
@@ -525,19 +514,12 @@
     sums_of = {}
     for scale in range(2):
         for blk in range(blocks):
-            mine = flags_ref[4] == blk
-            low = scale * head
-            packed = jnp.where(
-                mine,
-                mine_ref[low : low + head].astype(F32),
-                other_ref[low : low + head].astype(F32),
-            )
+            base = blk * (2 * head + 16)
+            low = base + scale * head
+            packed = stats_ref[low : low + head].astype(F32)
             kv = jnp.where(same, jnp.concatenate([packed] * (BLOCK // head), axis=0), 0.0)
-            both = jnp.where(
-                mine,
-                mine_ref[2 * head : 2 * head + 16].astype(F32),
-                other_ref[2 * head : 2 * head + 16].astype(F32),
-            )
+            low = base + 2 * head
+            both = stats_ref[low : low + 16].astype(F32)
             sums = both[8 * scale : 8 * scale + 1]
             diag = jnp.where(eye, jnp.broadcast_to(sums, (BLOCK, BLOCK)), 0.0)
             sums_of[scale, blk] = jnp.dot(
@@ -779,7 +761,6 @@
     row_index = lax.axis_index("row")
     row_count = lax.axis_size("row")
     swap = [(0, 1), (1, 0)]
-    paired = col_count == 2 and blocks == 2
 
     def strip(low):
         return canvas[:, low : low + REACH].transpose(1, 0, 2)
@@ -799,7 +780,6 @@
             (row_index < row_count - 1).astype(jnp.int32),
             (col_index > 0).astype(jnp.int32),
             (col_index < col_count - 1).astype(jnp.int32),
-            col_index.astype(jnp.int32) if paired else jnp.int32(0),
             (row_index % 2).astype(jnp.int32),
         ]
     )
@@ -890,7 +870,7 @@
 
     halos = (even, odd, *sides)
     halo_specs = [whole(h.shape) for h in halos]
-    mine, sent = pl.pallas_call(
+    stats = pl.pallas_call(
         functools.partial(border_kernel, tile, head, side_count),
         grid=(blocks,),
         in_specs=[
@@ -908,8 +888,8 @@
             pl.BlockSpec((per, head, head), lambda j: (blocks + j, 0, 0)),
             pl.BlockSpec((per, head, head), lambda j: (2 * blocks + j, 0, 0)),
         ],
-        out_specs=[whole(part_shape)] * 2,
-        out_shape=[jax.ShapeDtypeStruct(part_shape, BF16)] * 2,
+        out_specs=pl.BlockSpec(part_shape, lambda j: (j, 0)),
+        out_shape=jax.ShapeDtypeStruct((blocks * part_shape[0], BLOCK), BF16),
         scratch_shapes=[
             flat_buf,
             flat_buf,
@@ -934,13 +914,7 @@
         w_group,
         w_group,
     )
-    if paired:
-        got = lax.ppermute(sent, "col", swap)
-        mine = total_over((mine.astype(F32) + got.astype(F32)).astype(BF16), "row")
-        other = lax.ppermute(mine, "col", swap)
-    else:
-        mine = total_over(total_over(mine, "col"), "row")
-        other = total_over(total_over(sent, "col"), "row")
+    stats = total_over(total_over(stats, "col"), "row")
 
     count = cells + 2 * cols + 2 * tall
     far = []
@@ -985,7 +959,6 @@
             vmem,
             hbm,
             hbm,
-            vmem,
             vmem,
             hbm,
             vmem,
@@ -1028,8 +1001,7 @@
         far[1][0],
         far[0][1],
         far[1][1],
-        mine,
-        other,
+        stats,
         w_proj,
         gain_attn.reshape(1, channels),
         w_expand,

time: 63.5 us -> 61.7 us (0.972)
  waiting for transfers between devices: 4.06 us -> 2.92 us
  starting transfers between devices: 14.5 us -> 13.8 us
    ppermute x2 -> x0, waiting for transfers between devices: 1.04 us -> none  [the longest x1 1.04 us: body(): got = lax.ppermute(sent, 'col', swap)]
    ppermute x3 -> x4, starting transfers between devices: 10.4 us -> 9.95 us  [total_over(): total = total + lax.ppermute(x, axis, pairs).astype(F32)]
    ppermute x3 -> x4, waiting for transfers between devices: 3.01 us -> 2.91 us  [total_over(): total = total + lax.ppermute(x, axis, pairs).astype(F32)]
  transfers between devices with their start and end apart: 8 -> 7, of which waited for: 3 -> 2; matrix products, arithmetic and copies ran while one was open for 4% -> 4% of each run, Pallas kernels for 23% -> 24%
where the time goes in v6:
time: 61.7 us; the launch traced here: 61.5 us
  Pallas kernels  38.8 us (63%)
  starting transfers between devices  13.8 us (22%)
  local copies, waits for them, and re-layouts  5.28 us (9%)
  waiting for transfers between devices  2.92 us (5%)
    pallas_call x1, Pallas kernels, body(): pl.pallas_call(functools.partial(feed_kernel, tile, head, side_count), in...  20.9 us
    ppermute x4, starting transfers between devices, total_over(): total = total + lax.ppermute(x, axis, pairs).astype(F32)  9.95 us
    pallas_call x2, Pallas kernels, interior(): pl.pallas_call(functools.partial(interior_kernel, tile, head, first, side...  7.92 us
    pallas_call x2, Pallas kernels, body(): far.append(query(flags, proj_q, *halos, w_qkv, w_spread, w_group))  5.68 us
    pallas_call x1, Pallas kernels, body(): pl.pallas_call(functools.partial(border_kernel, tile, head, side_count),...  3.39 us
    unnamed x21, local copies, waits for them, and re-layouts  3.01 us
    ppermute x4, waiting for transfers between devices, total_over(): total = total + lax.ppermute(x, axis, pairs).astype(F32)  2.91 us
    ppermute x1, starting transfers between devices, body(): lax.ppermute(wide(canvas, left, right, low_even), 'row', swaps('row', 0))  2.61 us
  transfers between devices with their start and end apart: 7, of which 2 were waited for; matrix products, arithmetic and copies ran while one was open for 4% of the time, Pallas kernels for 24%

profile of v6, /device:TPU:0, one launch (start us, length us, event | category | flops | bytes accessed | tf_op | source)
XLA Modules:
  0.0 61.5 jit_solution(3636508885750960948)
XLA Ops:
  0.0 1.1 %dynamic-slice_bitcast_fusion = bf16[3,32,512]{2,0,1:T(4,128)(2,1)S(1)} fusion(bf16[32,32,512]{2,1,0:T(8,128)(2,1)} %param.11, s32[]{:T(128)S(6)} %select_n.28), kind=kLoop, calls=%fused_computation.4 | loop fusion | bytes 196612 | tf_op jit(solution)/shard_map/transpose | solution.py:770
  1.1 0.6 collective-permute-start
  1.7 1.6 %copy.13.refs_8_.refs_9_.refs_3_.refs_10_.refs_11_ = bf16[48,32,32]{2,1,0:T(8,128)(2,1)S(1)} copy(bf16[48,32,32]{0,2,1:T(8,128)(2,1)} %param.15) | data formatting | bytes 196608 | tf_op args[4]
  3.3 0.1 pad.7.clone
  3.4 0.1 stack.39.refs_0_.flags_ref
  3.4 1.0 %constant_dynamic-slice_fusion = (bf16[3,32,512]{2,1,0:T(8,128)(2,1)S(1)}, bf16[3,32,512]{2,1,0:T(8,128)(2,1)S(1)}) fusion(bf16[32,32,512]{2,1,0:T(8,128)(2,1)} %param.11, s32[]{:T(128)S(6)} %select_n.29, s32[]{:T(128)S(6)} %select_n.27), kind=kLoop, calls=%fused_computation.9 | loop fusion | bytes 393224 | tf_op jit(solution)/shard_map/dynamic_slice | solution.py:678
  4.4 0.1 maximum_maximum_fusion.1
  4.5 2.6 %collective-permute-start.1 = (bf16[3,40,512]{2,1,0:T(8,128)(2,1)S(1)}, bf16[3,40,512]{2,1,0:T(8,128)(2,1)S(1)}, u32[]{:S(2)}, u32[]{:S(2)}) collective-permute-start(bf16[3,40,512]{2,1,0:T(8,128)(2,1)S(1)} %get-tuple-element.26), channel_id=1, source_target_pairs={{0,2},{2,0},{4,6},{6,4},{8,10},{10,8},{12,14},{14,12},{1,3},{3,1},... | collective-permute-start | bytes 368648 | tf_op jit(solution)/shard_map/ppermute | solution.py:849
  7.2 0.0 copy-start.1
  7.2 1.4 %copy-done.1 = bf16[512,1536]{1,0:T(8,128)(2,1)S(1)} copy-done((bf16[512,1536]{1,0:T(8,128)(2,1)S(1)}, bf16[512,1536]{1,0:T(8,128)(2,1)}, u32[]{:S(2)}) %copy-start.1) | copy-done | bytes 1572888
  8.6 4.0 %shard_map.109 = (f32[80,256]{1,0:T(8,128)S(1)}, bf16[1024,128]{1,0:T(8,128)(2,1)S(1)}) custom-call(s32[5]{0:T(128)S(1)} %stack.39.refs_0_.flags_ref, bf16[1024,512]{1,0:T(8,128)(2,1)S(1)} %bitcast.18, s32[32,32]{1,0:T(8,128)S(1)} %copy-done.9, bf16[96,512]{1,0:T(8,128)(2,1)S(1)} %bitcast.24, bf16[512,1536]{1,0:T(8,128)(2,1)S(1)} %copy-done.1, ...), custom_call_target="tpu_custom_call" | custom-call | flops 2684354560 | bytes 2097152 | tf_op jit(solution)/shard_map/pallas_call | solution.py:807
  12.6 0.7 %collective-permute-start.2 = (bf16[3,40,512]{2,1,0:T(8,128)(2,1)S(1)}, bf16[3,40,512]{2,1,0:T(8,128)(2,1)S(1)}, u32[]{:S(2)}, u32[]{:S(2)}) collective-permute-start(bf16[3,40,512]{2,1,0:T(8,128)(2,1)S(1)} %get-tuple-element.14), channel_id=1, source_target_pairs={{2,4},{4,2},{6,8},{8,6},{10,12},{12,10},{3,5},{5,3},{7,9},{9,7},{1... | collective-permute-start | bytes 368648 | tf_op jit(solution)/shard_map/ppermute | solution.py:852
  13.3 3.9 %shard_map.112.refs_5_ = f32[80,256]{1,0:T(8,128)S(1)} custom-call(s32[5]{0:T(128)S(1)} %stack.39.refs_0_.flags_ref, bf16[1024,512]{1,0:T(8,128)(2,1)S(1)} %bitcast.19, bf16[1024,128]{1,0:T(8,128)(2,1)S(1)} %get-tuple-element.19.refs_2_.refs_3_, bf16[96,512]{1,0:T(8,128)(2,1)S(1)} %bitcast.25, bf16[512,1536]{1,0:T(8,128)(2,1)S(1)} %copy-done.1, ...), custom_call_target="tpu_custom_call" | custom-call | flops 2684354560 | bytes 2097152 | tf_op jit(solution)/shard_map/pallas_call | solution.py:807
  17.3 3.4 %border.1 = bf16[160,256]{1,0:T(8,128)(2,1)S(1)} custom-call(s32[5]{0:T(128)S(1)} %stack.39.refs_0_.flags_ref, bf16[1024,512]{1,0:T(8,128)(2,1)S(1)} %bitcast.20, bf16[1024,512]{1,0:T(8,128)(2,1)S(1)} %bitcast.21, bf16[120,512]{1,0:T(8,128)(2,1)S(1)} %bitcast.30, bf16[120,512]{1,0:T(8,128)(2,1)S(1)} %bitcast.34, bf16[96,512]{1,0:T(8,128)(2,1)S(1)} %bitcast.26, ...), custom_call_target="tpu_custom_call" | custom-call | flops 536870912 | bytes 1048576 | tf_op jit(solution)/shard_map/border/pallas_call | solution.py:873
  20.7 0.2 collective-permute-start.3
  20.9 1.1 %collective-permute-done.3 = bf16[160,256]{1,0:T(8,128)(2,1)S(1)} collective-permute-done((bf16[160,256]{1,0:T(8,128)(2,1)S(1)}, bf16[160,256]{1,0:T(8,128)(2,1)S(1)}, u32[]{:S(2)}, u32[]{:S(2)}) %collective-permute-start.3) | collective-permute-done | bytes 81952 | tf_op jit(solution)/shard_map/ppermute | solution.py:715
  22.0 4.3 %collective-permute-start.4 = (bf16[160,256]{1,0:T(8,128)(2,1)S(1)}, bf16[160,256]{1,0:T(8,128)(2,1)S(1)}, u32[]{:S(2)}, u32[]{:S(2)}) collective-permute-start(bf16[160,256]{1,0:T(8,128)(2,1)S(1)} %add_convert_fusion.3), channel_id=1, source_target_pairs={{0,2},{2,0},{4,6},{6,4},{8,10},{10,8},{12,14},{14,12},{1,3},{3,1},... | collective-permute-start | bytes 245768 | tf_op jit(solution)/shard_map/ppermute | solution.py:715
  26.4 0.9 %query_project.1.proj_ref.refs_1_ = bf16[2,1024,256]{2,1,0:T(8,128)(2,1)S(1)} custom-call(bf16[1024,512]{1,0:T(8,128)(2,1)S(1)} %bitcast.22, bf16[512,1536]{1,0:T(8,128)(2,1)S(1)} %copy-done.1), custom_call_target="tpu_custom_call" | custom-call | flops 536870912 | bytes 2097152 | tf_op jit(solution)/shard_map/query_project/pallas_call | solution.py:869
  27.3 1.8 %collective-permute-done.4 = bf16[160,256]{1,0:T(8,128)(2,1)S(1)} collective-permute-done((bf16[160,256]{1,0:T(8,128)(2,1)S(1)}, bf16[160,256]{1,0:T(8,128)(2,1)S(1)}, u32[]{:S(2)}, u32[]{:S(2)}) %collective-permute-start.4) | collective-permute-done | bytes 81952 | tf_op jit(solution)/shard_map/ppermute | solution.py:715
  29.2 2.6 %collective-permute-start.5 = (bf16[160,256]{1,0:T(8,128)(2,1)S(1)}, bf16[160,256]{1,0:T(8,128)(2,1)S(1)}, u32[]{:S(2)}, u32[]{:S(2)}) collective-permute-start(bf16[160,256]{1,0:T(8,128)(2,1)S(1)} %add_convert_fusion.2), channel_id=1, source_target_pairs={{0,4},{2,6},{4,0},{6,2},{8,12},{10,14},{12,8},{14,10},{1,5},{3,7},... | collective-permute-start | bytes 245768 | tf_op jit(solution)/shard_map/ppermute | solution.py:715
  31.8 2.8 %shard_map.111 = (bf16[144,256]{1,0:T(8,128)(2,1)S(1)}, bf16[1168,256]{1,0:T(8,128)(2,1)S(1)}) custom-call(s32[5]{0:T(128)S(1)} %stack.39.refs_0_.flags_ref, bf16[2,1024,256]{2,1,0:T(8,128)(2,1)S(1)} %query_project.1.proj_ref.refs_1_, bf16[120,512]{1,0:T(8,128)(2,1)S(1)} %bitcast.31, bf16[120,512]{1,0:T(8,128)(2,1)S(1)} %bitcast.35, ...), custom_call_target="tpu_custom_call" | custom-call | flops 1610612736 | bytes 1572864 | tf_op jit(solution)/shard_map/pallas_call | solution.py:946
  34.7 2.7 %collective-permute-start.6 = (bf16[160,256]{1,0:T(8,128)(2,1)S(1)}, bf16[160,256]{1,0:T(8,128)(2,1)S(1)}, u32[]{:S(2)}, u32[]{:S(2)}) collective-permute-start(bf16[160,256]{1,0:T(8,128)(2,1)S(1)} %add_convert_fusion.1), channel_id=1, source_target_pairs={{0,8},{2,10},{4,12},{6,14},{8,0},{10,2},{12,4},{14,6},{1,9},{3,11}... | collective-permute-start | bytes 245768 | tf_op jit(solution)/shard_map/ppermute | solution.py:715
  37.4 2.9 %shard_map.110 = (bf16[144,256]{1,0:T(8,128)(2,1)S(1)}, bf16[1168,256]{1,0:T(8,128)(2,1)S(1)}) custom-call(s32[5]{0:T(128)S(1)} %stack.39.refs_0_.flags_ref, bf16[2,1024,256]{2,1,0:T(8,128)(2,1)S(1)} %query_project.1.proj_ref.refs_1_, bf16[120,512]{1,0:T(8,128)(2,1)S(1)} %bitcast.32, bf16[120,512]{1,0:T(8,128)(2,1)S(1)} %bitcast.36, ...), custom_call_target="tpu_custom_call" | custom-call | flops 1610612736 | bytes 1572864 | tf_op jit(solution)/shard_map/pallas_call | solution.py:946
  40.4 20.9 %feed.1 = bf16[1024,512]{1,0:T(8,128)(2,1)} custom-call(s32[5]{0:T(128)S(1)} %stack.39.refs_0_.flags_ref, bf16[1024,512]{1,0:T(8,128)(2,1)S(1)} %bitcast.23, bf16[120,512]{1,0:T(8,128)(2,1)S(1)} %bitcast.33, bf16[120,512]{1,0:T(8,128)(2,1)S(1)} %bitcast.37, bf16[96,512]{1,0:T(8,128)(2,1)S(1)} %bitcast.29, ...), custom_call_target="tpu_custom_call" | custom-call | tf_op jit(solution)/shard_map/feed/pallas_call | solution.py:951
  (30 shorter events, 0.2 us)
Async XLA Ops:
  0.0 7.2 %copy-start = (bf16[32,32,512]{2,1,0:T(8,128)(2,1)S(1)}, bf16[32,32,512]{2,1,0:T(8,128)(2,1)}, u32[]{:S(2)}) copy-start(bf16[32,32,512]{2,1,0:T(8,128)(2,1)} %param.11) | copy-start | bytes 3145732
  0.0 7.2 %copy-start.5 = (bf16[5,5,1536]{2,1,0:T(8,128)(2,1)S(1)}, bf16[5,5,1536]{2,1,0:T(8,128)(2,1)}, u32[]{:S(2)}) copy-start(bf16[5,5,1536]{2,1,0:T(8,128)(2,1)} %refs_9_.4) | copy-start | bytes 230404
  0.0 7.2 %copy-start.9 = (s32[32,32]{1,0:T(8,128)S(1)}, s32[32,32]{1,0:T(8,128)}, u32[]{:S(2)}) copy-start(s32[32,32]{1,0:T(8,128)} %refs_2_.3) | copy-start | bytes 12292
  1.1 3.3 %collective-permute-start = (bf16[3,32,512]{2,0,1:T(4,128)(2,1)S(1)}, bf16[3,32,512]{2,0,1:T(4,128)(2,1)S(1)}, u32[]{:S(2)}, u32[]{:S(2)}) collective-permute-start(bf16[3,32,512]{2,0,1:T(4,128)(2,1)S(1)} %dynamic-slice_bitcast_fusion), channel_id=1, source_target_pairs={{0,1},{1,0},{2,3},{3,2},{4,5},{5,4},{6,7},{7,6},{8,9},{9,8},{10,11... | collective-permute-start | bytes 294920 | tf_op jit(solution)/shard_map/ppermute | solution.py:771
  4.5 12.7 %collective-permute-start.1 = (bf16[3,40,512]{2,1,0:T(8,128)(2,1)S(1)}, bf16[3,40,512]{2,1,0:T(8,128)(2,1)S(1)}, u32[]{:S(2)}, u32[]{:S(2)}) collective-permute-start(bf16[3,40,512]{2,1,0:T(8,128)(2,1)S(1)} %get-tuple-element.26), channel_id=1, source_target_pairs={{0,2},{2,0},{4,6},{6,4},{8,10},{10,8},{12,14},{14,12},{1,3},{3,1},... | collective-permute-start | bytes 368648 | tf_op jit(solution)/shard_map/ppermute | solution.py:849
  7.2 1.4 %copy-start.1 = (bf16[512,1536]{1,0:T(8,128)(2,1)S(1)}, bf16[512,1536]{1,0:T(8,128)(2,1)}, u32[]{:S(2)}) copy-start(bf16[512,1536]{1,0:T(8,128)(2,1)} %refs_7_.6) | copy-start | bytes 4718596
  12.6 4.6 %collective-permute-start.2 = (bf16[3,40,512]{2,1,0:T(8,128)(2,1)S(1)}, bf16[3,40,512]{2,1,0:T(8,128)(2,1)S(1)}, u32[]{:S(2)}, u32[]{:S(2)}) collective-permute-start(bf16[3,40,512]{2,1,0:T(8,128)(2,1)S(1)} %get-tuple-element.14), channel_id=1, source_target_pairs={{2,4},{4,2},{6,8},{8,6},{10,12},{12,10},{3,5},{5,3},{7,9},{9,7},{1... | collective-permute-start | bytes 368648 | tf_op jit(solution)/shard_map/ppermute | solution.py:852
  20.7 1.3 %collective-permute-start.3 = (bf16[160,256]{1,0:T(8,128)(2,1)S(1)}, bf16[160,256]{1,0:T(8,128)(2,1)S(1)}, u32[]{:S(2)}, u32[]{:S(2)}) collective-permute-start(bf16[160,256]{1,0:T(8,128)(2,1)S(1)} %border.1), channel_id=1, source_target_pairs={{0,1},{1,0},{2,3},{3,2},{4,5},{5,4},{6,7},{7,6},{8,9},{9,8},{10,11... | collective-permute-start | bytes 245768 | tf_op jit(solution)/shard_map/ppermute | solution.py:715
  22.0 7.1 %collective-permute-start.4 = (bf16[160,256]{1,0:T(8,128)(2,1)S(1)}, bf16[160,256]{1,0:T(8,128)(2,1)S(1)}, u32[]{:S(2)}, u32[]{:S(2)}) collective-permute-start(bf16[160,256]{1,0:T(8,128)(2,1)S(1)} %add_convert_fusion.3), channel_id=1, source_target_pairs={{0,2},{2,0},{4,6},{6,4},{8,10},{10,8},{12,14},{14,12},{1,3},{3,1},... | collective-permute-start | bytes 245768 | tf_op jit(solution)/shard_map/ppermute | solution.py:715
  29.2 5.4 %collective-permute-start.5 = (bf16[160,256]{1,0:T(8,128)(2,1)S(1)}, bf16[160,256]{1,0:T(8,128)(2,1)S(1)}, u32[]{:S(2)}, u32[]{:S(2)}) collective-permute-start(bf16[160,256]{1,0:T(8,128)(2,1)S(1)} %add_convert_fusion.2), channel_id=1, source_target_pairs={{0,4},{2,6},{4,0},{6,2},{8,12},{10,14},{12,8},{14,10},{1,5},{3,7},... | collective-permute-start | bytes 245768 | tf_op jit(solution)/shard_map/ppermute | solution.py:715
  31.8 8.6 %copy-start.4 = (bf16[1024,512]{1,0:T(8,128)(2,1)S(1)}, bf16[1024,512]{1,0:T(8,128)(2,1)}, u32[]{:S(2)}) copy-start(bf16[1024,512]{1,0:T(8,128)(2,1)} %refs_7_.7) | copy-start | bytes 3145732
  34.6 5.8 %copy-start.3 = (bf16[2048,512]{1,0:T(8,128)(2,1)S(1)}, bf16[2048,512]{1,0:T(8,128)(2,1)}, u32[]{:S(2)}) copy-start(bf16[2048,512]{1,0:T(8,128)(2,1)} %refs_11_.2) | copy-start | bytes 6291460
  34.6 5.8 %copy-start.2 = (bf16[512,4096]{1,0:T(8,128)(2,1)S(1)}, bf16[512,4096]{1,0:T(8,128)(2,1)}, u32[]{:S(2)}) copy-start(bf16[512,4096]{1,0:T(8,128)(2,1)} %refs_9_.5) | copy-start | bytes 12582916
  34.6 5.8 %copy-start.6 = (bf16[3,3,4096]{2,1,0:T(4,128)(2,1)S(1)}, bf16[3,3,4096]{2,1,0:T(4,128)(2,1)}, u32[]{:S(2)}) copy-start(bf16[3,3,4096]{2,1,0:T(4,128)(2,1)} %refs_10_.2) | copy-start | bytes 221188
  34.6 5.8 %copy-start.7 = (f32[512]{0:T(512)S(1)}, f32[512]{0:T(512)}, u32[]{:S(2)}) copy-start(f32[512]{0:T(512)} %param.17) | copy-start | bytes 6148
  34.6 5.8 %copy-start.8 = (f32[512]{0:T(512)S(1)}, f32[512]{0:T(512)}, u32[]{:S(2)}) copy-start(f32[512]{0:T(512)} %param.21) | copy-start | bytes 6148
  34.7 5.7 %collective-permute-start.6 = (bf16[160,256]{1,0:T(8,128)(2,1)S(1)}, bf16[160,256]{1,0:T(8,128)(2,1)S(1)}, u32[]{:S(2)}, u32[]{:S(2)}) collective-permute-start(bf16[160,256]{1,0:T(8,128)(2,1)S(1)} %add_convert_fusion.1), channel_id=1, source_target_pairs={{0,8},{2,10},{4,12},{6,14},{8,0},{10,2},{12,4},{14,6},{1,9},{3,11}... | collective-permute-start | bytes 245768 | tf_op jit(solution)/shard_map/ppermute | solution.py:715
